TPU v7x, 32 devices: a whole 2x2x4 slice. The times are simulated.
32 devices in a mesh: dp: 4 (over y, core), expert: 8 (over z, x).
Axes of the slice: x: 2, y: 2, z: 4, core: 2. Of those that a mesh axis runs over, the one named last changes fastest.
Arguments:
- tokens: bfloat16 [4096, 3584], P(('dp', 'expert')), may hold values from -6 to 6
- cotangent: bfloat16 [4096, 3584], P(('dp', 'expert')), may hold values from -0.29882812 to 0.29882812
- routes: int32 [4096, 4], P(('dp', 'expert')), may hold values from 0 to 7, all different within a row; in each aligned block of 128 rows (0 to 127, 128 to 255, ...) at most 80 rows name the same one
- route_gain: float32 [4096, 4], P(('dp', 'expert')), may hold values from 0.2 to 1
- expert_alive: int32 [8], replicated, may hold values 0 or 1
- w_gate: bfloat16 [8, 3584, 1024], P('expert'), may hold values from -0.09375 to 0.09375
- w_up: bfloat16 [8, 3584, 1024], P('expert'), may hold values from -0.09375 to 0.09375
- w_down: bfloat16 [8, 1024, 3584], P('expert'), may hold values from -0.1875 to 0.1875
Outputs:
- grad_gate: bfloat16 [8, 3584, 1024], P('expert', 'dp')
- grad_up: bfloat16 [8, 3584, 1024], P('expert', 'dp')
- grad_down: bfloat16 [8, 1024, 3584], P('expert', 'dp')
Inputs may be any that keep to these rules, and one draw needn't show every extreme that they name: `routes`: in each block of 128 tokens no expert is named by more than 80 pairs.
All inputs are finite; a program needn't handle non-finite values.
Results may differ from a plain program's by a relative error of at most 0.009.
Values may be sent and summed in bfloat16 or wider, within the bound.
No kernel may reach another device: no remote copies, remote signals or barrier semaphores. Data moves between devices by JAX's collectives and lax.ppermute only.
A program may use at most 128 MiB of HBM per device.

v0:
```python
import jax
import jax.numpy as jnp
from jax import lax
from jax.sharding import PartitionSpec as P


def contract_rows(left, right):
    return lax.dot_general(
        left, right, (((0,), (0,)), ((), ())), preferred_element_type=jnp.float32
    )


def expert_terms(x_rows, cot_rows, gate_w, up_w, down_w):
    gate_proj = jnp.dot(x_rows, gate_w, preferred_element_type=jnp.float32)
    up_proj = jnp.dot(x_rows, up_w, preferred_element_type=jnp.float32)
    sigmoid_gate = jax.nn.sigmoid(gate_proj)
    activated = gate_proj * sigmoid_gate
    hidden = (activated * up_proj).astype(jnp.bfloat16)
    d_hidden = lax.dot_general(
        cot_rows, down_w, (((1,), (1,)), ((), ())), preferred_element_type=jnp.float32
    )
    d_gate = (d_hidden * up_proj * sigmoid_gate * (1.0 + gate_proj * (1.0 - sigmoid_gate))).astype(
        jnp.bfloat16
    )
    d_up = (d_hidden * activated).astype(jnp.bfloat16)
    return (hidden, d_gate, d_up)


def per_device(tokens, cotangent, routes, route_gain, expert_alive, w_gate, w_up, w_down):
    tok_count = tokens.shape[0]
    top_count = routes.shape[1]
    width = tokens.shape[1]
    experts_all = expert_alive.shape[0]
    slots_per = tok_count * top_count * 5 // (4 * experts_all)
    expert_ids = jnp.arange(experts_all, dtype=jnp.int32)
    pair_routes = routes.reshape(-1)
    one_hot = (pair_routes[:, None] == expert_ids[None, :]).astype(jnp.int32) * expert_alive[
        None, :
    ]
    is_live = jnp.sum(one_hot, axis=1)
    slot_index = jnp.sum((jnp.cumsum(one_hot, axis=0) - one_hot) * one_hot, axis=1)
    dest_row = jnp.where(is_live > 0, pair_routes * slots_per + slot_index, experts_all * slots_per)
    pair_index = jnp.arange(tok_count * top_count, dtype=jnp.int32)
    source_pair = (
        jnp.zeros((experts_all * slots_per,), jnp.int32).at[dest_row].set(pair_index, mode="drop")
    )
    filled = jnp.zeros((experts_all * slots_per,), jnp.int32).at[dest_row].set(1, mode="drop")
    token_row = source_pair // top_count
    x_slots = jnp.where(filled[:, None] > 0, tokens[token_row], jnp.zeros((), jnp.bfloat16))
    pair_gain = jnp.where(filled > 0, route_gain.reshape(-1)[source_pair], 0.0)
    cot_slots = (pair_gain[:, None] * cotangent[token_row].astype(jnp.float32)).astype(jnp.bfloat16)
    x_recv, cot_recv = (
        lax.all_to_all(
            x_slots.reshape(experts_all, slots_per, width),
            "expert",
            split_axis=0,
            concat_axis=1,
            tiled=True,
        ),
        lax.all_to_all(
            cot_slots.reshape(experts_all, slots_per, width),
            "expert",
            split_axis=0,
            concat_axis=1,
            tiled=True,
        ),
    )
    x_rows = x_recv[0]
    cot_rows = cot_recv[0]
    hidden, d_gate, d_up = expert_terms(x_rows, cot_rows, w_gate[0], w_up[0], w_down[0])
    gate_list = [contract_rows(x_rows, d_gate)]
    up_list = [contract_rows(x_rows, d_up)]
    down_list = [contract_rows(hidden, cot_rows)]
    summed_gate, summed_up, summed_down = (
        lax.psum_scatter(
            jnp.stack(gate_list).astype(jnp.bfloat16), "dp", scatter_dimension=1, tiled=True
        ).astype(jnp.float32),
        lax.psum_scatter(
            jnp.stack(up_list).astype(jnp.bfloat16), "dp", scatter_dimension=1, tiled=True
        ).astype(jnp.float32),
        lax.psum_scatter(
            jnp.stack(down_list).astype(jnp.bfloat16), "dp", scatter_dimension=1, tiled=True
        ).astype(jnp.float32),
    )
    return (
        summed_gate.astype(jnp.bfloat16),
        summed_up.astype(jnp.bfloat16),
        summed_down.astype(jnp.bfloat16),
    )


def solution(mesh):
    in_specs = (
        P(("dp", "expert"), None),
        P(("dp", "expert"), None),
        P(("dp", "expert"), None),
        P(("dp", "expert"), None),
        P(),
        P("expert", None, None),
        P("expert", None, None),
        P("expert", None, None),
    )
    out_specs = (P("expert", "dp", None), P("expert", "dp", None), P("expert", "dp", None))
    return jax.shard_map(
        per_device, mesh=mesh, in_specs=in_specs, out_specs=out_specs, check_vma=False
    )
```

profile of v0, /device:TPU:0, one launch (start us, length us, event | category | flops | bytes accessed | tf_op | source)
XLA Modules:
  0.0 466.3 jit_solution(11148459767277712539)
XLA Ops:
  7.2 0.9 copy.11
  8.2 0.1 eq.25
  8.3 0.7 broadcast_multiply_fusion
  8.9 0.7 fusion.15
  9.7 1.1 reduce-window.6
  10.8 0.2 slice_reduce_fusion
  11.1 0.8 fusion.14
  11.8 0.1 copy.12
  12.1 2.4 scatter_custom_fusion.1
  14.5 0.8 copy.14
  15.4 2.4 scatter_custom_fusion
  17.9 4.3 gather_fusion.1
  22.3 5.2 %gather_fusion = bf16[640,3584]{1,0:T(8,128)(2,1)} fusion(bf16[128,3584]{1,0:T(8,128)(2,1)S(1)} %copy-done, s32[1024]{0:T(1024)S(1)} %get-tuple-element.10), kind=kCustom, calls=%fused_computation | custom fusion | bytes 9177600 | tf_op jit(solution)/shard_map/gather | solution.py:49
  27.5 4.7 %broadcast_select_fusion = bf16[8,80,3584]{2,1,0:T(8,128)(2,1)} fusion(bf16[8,80,3584]{2,1,0:T(8,128)(2,1)} %bitcast.33, pred[8,80]{1,0:T(8,128)(4,1)S(1)} %broadcast_in_dim.40), kind=kLoop, calls=%fused_computation.19 | loop fusion | flops 2293760 | bytes 9175680 | tf_op jit(solution)/shard_map/jit(_where)/select_n | solution.py:49
  32.2 7.4 %all-to-all-start = ((bf16[8,80,3584]{2,1,0:T(8,128)(2,1)}), bf16[8,80,3584]{2,1,0:T(8,128)(2,1)}, u32[]{:S(2)}, u32[]{:S(2)}) async-start(bf16[8,80,3584]{2,1,0:T(8,128)(2,1)} %broadcast_select_fusion), calls=%async_computation | async-start | bytes 9175040 | tf_op jit(solution)/shard_map/all_to_all | solution.py:53
  39.7 5.2 %gather_fusion.2 = bf16[640,3584]{1,0:T(8,128)(2,1)} fusion(bf16[128,3584]{1,0:T(8,128)(2,1)S(1)} %copy-done.2, s32[1024]{0:T(1024)S(1)} %get-tuple-element.10), kind=kCustom, calls=%fused_computation.2 | custom fusion | bytes 9177600 | tf_op jit(solution)/shard_map/gather | solution.py:51
  44.9 5.9 %fusion = bf16[8,80,3584]{2,1,0:T(8,128)(2,1)} fusion(bf16[8,80,3584]{2,1,0:T(8,128)(2,1)} %bitcast.32, f32[8,80]{1,0:T(8,128)S(1)} %mul.71), kind=kLoop, calls=%fused_computation.6 | loop fusion | flops 6881280 | bytes 9177600 | tf_op jit(solution)/shard_map/convert_element_type | solution.py:51
  50.7 90.6 %all-to-all-done = bf16[8,80,3584]{2,1,0:T(8,128)(2,1)} async-done(((bf16[8,80,3584]{2,1,0:T(8,128)(2,1)}), bf16[8,80,3584]{2,1,0:T(8,128)(2,1)}, u32[]{:S(2)}, u32[]{:S(2)}) %all-to-all-start) | async-done | bytes 4587552 | tf_op jit(solution)/shard_map/all_to_all | solution.py:53
  141.3 4.6 all-to-all-start.1
  145.9 0.2 reduce-scatter.8.cloned.1.call-start
  146.2 8.5 %fusion.1 = f32[640,1024]{1,0:T(8,128)S(1)} fusion(bf16[640,3584]{1,0:T(8,128)(2,1)} %bitcast.5, bf16[1,3584,1024]{2,1,0:T(8,128)(2,1)} %param.13), kind=kOutput, calls=%fused_computation.10 | convolution fusion | flops 4697620480 | bytes 14548992 | tf_op jit(solution)/shard_map/dot_general | solution.py:14
  154.7 10.8 %fusion.3 = f32[640,1024]{1,0:T(8,128)} fusion(bf16[640,3584]{1,0:T(8,128)(2,1)} %bitcast.5, bf16[1,3584,1024]{2,1,0:T(8,128)(2,1)} %param.14), kind=kOutput, calls=%fused_computation.12 | convolution fusion | flops 4697620480 | bytes 14548992 | tf_op jit(solution)/shard_map/dot_general | solution.py:15
  165.5 81.3 %all-to-all-done.1 = bf16[8,80,3584]{2,1,0:T(8,128)(2,1)} async-done(((bf16[8,80,3584]{2,1,0:T(8,128)(2,1)}), bf16[8,80,3584]{2,1,0:T(8,128)(2,1)}, u32[]{:S(2)}, u32[]{:S(2)}) %all-to-all-start.1) | async-done | bytes 4587552 | tf_op jit(solution)/shard_map/all_to_all | solution.py:60
  246.9 10.8 %fusion.7 = bf16[1,1024,3584]{2,1,0:T(8,128)(2,1)} fusion(bf16[640,3584]{1,0:T(8,128)(2,1)} %bitcast.7, f32[640,1024]{1,0:T(8,128)} %fusion.3, f32[640,1024]{1,0:T(8,128)S(1)} %fusion.1), kind=kOutput, calls=%fused_computation.16 | convolution fusion | flops 4705222656 | bytes 17170432 | tf_op jit(solution)/shard_map/dot_general | solution.py:8
  257.7 8.6 %fusion.5 = f32[640,1024]{1,0:T(8,128)S(1)} fusion(bf16[640,3584]{1,0:T(8,128)(2,1)} %bitcast.7, bf16[1,1024,3584]{2,1,0:T(8,128)(2,1)} %param.15), kind=kOutput, calls=%fused_computation.14 | convolution fusion | flops 4697620480 | bytes 14548992 | tf_op jit(solution)/shard_map/dot_general | solution.py:19
  266.3 1.6 copy-done.3
  267.8 11.0 %fusion.9 = bf16[1,3584,1024]{2,1,0:T(8,128)(2,1)} fusion(bf16[640,3584]{1,0:T(8,128)(2,1)} %bitcast.5, f32[640,1024]{1,0:T(8,128)S(1)} %fusion.5, f32[640,1024]{1,0:T(8,128)S(1)} %fusion.1), kind=kOutput, calls=%fused_computation.18 | convolution fusion | flops 4705222656 | bytes 17170432 | tf_op jit(solution)/shard_map/dot_general | solution.py:8
  278.8 0.3 reduce-scatter.4.cloned.1.call-start
  279.1 12.1 %fusion.8 = bf16[1,3584,1024]{2,1,0:T(8,128)(2,1)} fusion(bf16[640,3584]{1,0:T(8,128)(2,1)} %bitcast.5, f32[640,1024]{1,0:T(8,128)S(1)} %fusion.1, f32[640,1024]{1,0:T(8,128)} %copy-done.3, f32[640,1024]{1,0:T(8,128)} %fusion.3), kind=kOutput, calls=%fused_computation.17 | convolution fusion | flops 4707844096 | bytes 19791872 | tf_op jit(solution)/shard_map/dot_general | solution.py:8
  291.3 31.1 %reduce-scatter.8.cloned.1.call-done = bf16[1,256,3584]{2,1,0:T(8,128)(2,1)} async-done(((bf16[1,1024,3584]{2,1,0:T(8,128)(2,1)}), bf16[1,256,3584]{2,1,0:T(8,128)(2,1)}) %reduce-scatter.8.cloned.1.call-update) | async-done | bytes 1835024 | tf_op jit(solution)/shard_map/reduce_scatter | solution.py:81
  322.4 68.8 %reduce-scatter.6.cloned.1.call-done = bf16[1,896,1024]{2,1,0:T(8,128)(2,1)} async-done(((bf16[1,3584,1024]{2,1,0:T(8,128)(2,1)}), bf16[1,896,1024]{2,1,0:T(8,128)(2,1)}) %reduce-scatter.6.cloned.1.call-update) | async-done | bytes 1835024 | tf_op jit(solution)/shard_map/reduce_scatter | solution.py:78
  391.1 68.6 %reduce-scatter.4.cloned.1.call-done = bf16[1,896,1024]{2,1,0:T(8,128)(2,1)} async-done(((bf16[1,3584,1024]{2,1,0:T(8,128)(2,1)}), bf16[1,896,1024]{2,1,0:T(8,128)(2,1)}) %reduce-scatter.4.cloned.1.call-update) | async-done | bytes 1835024 | tf_op jit(solution)/shard_map/reduce_scatter | solution.py:75
  (25 shorter events, 0.7 us)
Async XLA Ops:
  7.2 15.2 %copy-start = (bf16[128,3584]{1,0:T(8,128)(2,1)S(1)}, bf16[128,3584]{1,0:T(8,128)(2,1)}, u32[]{:S(2)}) copy-start(bf16[128,3584]{1,0:T(8,128)(2,1)} %param.8) | copy-start | bytes 2752516
  32.2 7.5 %copy-start.2 = (bf16[128,3584]{1,0:T(8,128)(2,1)S(1)}, bf16[128,3584]{1,0:T(8,128)(2,1)}, u32[]{:S(2)}) copy-start(bf16[128,3584]{1,0:T(8,128)(2,1)} %param.9) | copy-start | bytes 2752516
  32.2 109.1 %all-to-all-start = ((bf16[8,80,3584]{2,1,0:T(8,128)(2,1)}), bf16[8,80,3584]{2,1,0:T(8,128)(2,1)}, u32[]{:S(2)}, u32[]{:S(2)}) async-start(bf16[8,80,3584]{2,1,0:T(8,128)(2,1)} %broadcast_select_fusion), calls=%async_computation | async-start | bytes 9175040 | tf_op jit(solution)/shard_map/all_to_all | solution.py:53
  141.3 105.5 %all-to-all-start.1 = ((bf16[8,80,3584]{2,1,0:T(8,128)(2,1)}), bf16[8,80,3584]{2,1,0:T(8,128)(2,1)}, u32[]{:S(2)}, u32[]{:S(2)}) async-start(bf16[8,80,3584]{2,1,0:T(8,128)(2,1)} %fusion), calls=%async_computation.1 | async-start | bytes 9175040 | tf_op jit(solution)/shard_map/all_to_all | solution.py:60
  145.9 176.4 %reduce-scatter.8.cloned.1.call-start = ((), (), s32[]{:S(2)}) async-start(), calls=%async_computation.7 | async-start | bytes 9175040 | tf_op jit(solution)/shard_map/reduce_scatter | solution.py:81
  257.6 133.5 %reduce-scatter.6.cloned.1.call-start = ((), (), s32[]{:S(2)}) async-start(), calls=%async_computation.6 | async-start | bytes 9175040 | tf_op jit(solution)/shard_map/reduce_scatter | solution.py:78
  266.3 1.6 copy-start.3
  278.8 180.9 %reduce-scatter.4.cloned.1.call-start = ((), (), s32[]{:S(2)}) async-start(), calls=%async_computation.5 | async-start | bytes 9175040 | tf_op jit(solution)/shard_map/reduce_scatter | solution.py:75
  279.1 180.7 %copy-start.1 = (bf16[128,3584]{1,0:T(8,128)(2,1)S(1)}, bf16[128,3584]{1,0:T(8,128)(2,1)}, u32[]{:S(2)}) copy-start(bf16[128,3584]{1,0:T(8,128)(2,1)} %param.8) | copy-start | bytes 2752516
Sparse Core Ops, SparseCore 0:
  257.8 64.5 reduce-scatter.7
  325.6 65.4 reduce-scatter.5
  394.3 65.4 reduce-scatter.3
where the time goes:
time: 467 us; the launch traced here: 466 us
  waiting for transfers between devices  340 us (73%)
  matrix products  61.8 us (13%)
  local copies, waits for them, and re-layouts  23.7 us (5%)
  other arithmetic  14 us (3%)
  between operations  13.9 us (3%)
  starting transfers between devices  12.5 us (3%)
    all_to_all x1, waiting for transfers between devices, per_device(): lax.all_to_all(x_slots.reshape(experts_all, slots_per, width), 'expert',...  90.6 us
    all_to_all x1, waiting for transfers between devices, per_device(): lax.all_to_all(cot_slots.reshape(experts_all, slots_per, width), 'expert'...  81.3 us
    reduce_scatter x1, waiting for transfers between devices, per_device(): lax.psum_scatter(jnp.stack(up_list).astype(jnp.bfloat16), 'dp', scatter_d...  68.8 us
    reduce_scatter x1, waiting for transfers between devices, per_device(): lax.psum_scatter(jnp.stack(gate_list).astype(jnp.bfloat16), 'dp', scatter...  68.6 us
    dot_general x3, matrix products, contract_rows(): lax.dot_general(left, right, (((0,), (0,)), ((), ())), preferred_element_...  33.8 us
    reduce_scatter x1, waiting for transfers between devices, per_device(): lax.psum_scatter(jnp.stack(down_list).astype(jnp.bfloat16), 'dp', scatter...  31.1 us
    dot_general x1, matrix products, expert_terms(): up_proj = jnp.dot(x_rows, up_w, preferred_element_type=jnp.float32)  10.8 us
  transfers between devices with their start and end apart: 5, of which 5 were waited for; matrix products, arithmetic and copies ran while one was open for 13% of the time, Pallas kernels for 0%

commit v1 on v0

v1 whole, which is shorter than its diff:
```python
import jax
import jax.numpy as jnp
from jax import lax
from jax.sharding import PartitionSpec as P

NZ = 4
NC = 2


def contract_rows(left, right):
    return lax.dot_general(
        left, right, (((0,), (0,)), ((), ())), preferred_element_type=jnp.float32
    )


def make_per_device(n_dp, n_expert):
    nx = n_expert // NZ
    ny = n_dp // NC

    def ex(z, x):
        return z * nx + x

    def zpairs(moves):
        return [(ex(a, x), ex(b, x)) for a, b in moves for x in range(nx)]

    ends_first = zpairs([(0, 1), (1, 0), (2, 3), (3, 2)])
    middle = zpairs([(1, 2), (2, 1)])
    outward = zpairs([(1, 0), (2, 3)])

    def z_chain(block):
        a = lax.ppermute(block, "expert", ends_first)
        c_mid = lax.ppermute(block, "expert", middle)
        b_end = lax.ppermute(c_mid, "expert", outward)
        b_mid = lax.ppermute(a, "expert", middle)
        c_end = lax.ppermute(b_mid, "expert", outward)
        return [(block,), (a,), (b_end, b_mid), (c_mid, c_end)]

    def x_pairs(k):
        return [(ex(z, x), ex(z, x ^ k)) for z in range(NZ) for x in range(nx)]

    core_pairs = [(y * NC + c, y * NC + 1 - c) for y in range(ny) for c in range(NC)]

    def y_pairs(k):
        return [(y * NC + c, (y ^ k) * NC + c) for y in range(ny) for c in range(NC)]

    def join(parts):
        return parts[0] if len(parts) == 1 else parts[0] + parts[1]

    def per_device(tokens, cotangent, routes, route_gain, expert_alive, w_gate, w_up, w_down):
        tok_count, width = tokens.shape
        top_count = routes.shape[1]
        experts_all = expert_alive.shape[0]
        cap = tok_count * top_count * 5 // (4 * experts_all)
        me = lax.axis_index("expert")
        z, x = me // nx, me % nx
        d = lax.axis_index("dp")
        y, c = d // NC, d % NC

        meta = jnp.concatenate([routes.T.astype(jnp.float32), route_gain.T], axis=0)
        metas = z_chain(meta)
        toks = z_chain(tokens)
        cots = z_chain(cotangent)

        ids = jnp.stack([z * nx + (x ^ k) for k in range(nx)])
        alive = jnp.sum(
            jnp.where(ids[:, None] == jnp.arange(experts_all)[None, :], expert_alive[None, :], 0),
            axis=1,
        )
        t_iota = jnp.arange(tok_count)
        before = (t_iota[:, None] < t_iota[None, :]).astype(jnp.bfloat16)
        slots = jnp.arange(cap, dtype=jnp.float32)

        x_parts, c_parts = [], []
        for meta_s, tok_s, cot_s in zip(metas, toks, cots):
            m = join(meta_s)
            r, g = m[:top_count], m[top_count:]
            named = r[None] == ids[:, None, None].astype(jnp.float32)
            match = jnp.any(named, axis=1) & (alive[:, None] > 0)
            gain_t = jnp.sum(jnp.where(named, g[None], 0.0), axis=1)
            pos = jnp.dot(match.astype(jnp.bfloat16), before, preferred_element_type=jnp.float32)
            pick = (pos[:, None, :] == slots[None, :, None]) & match[:, None, :]
            gain_s = jnp.sum(jnp.where(pick, gain_t[:, None, :], 0.0), axis=2).reshape(nx * cap, 1)
            pick = pick.astype(jnp.bfloat16).reshape(nx * cap, tok_count)
            x_sel = jnp.dot(pick, join(tok_s), preferred_element_type=jnp.float32).astype(
                jnp.bfloat16
            )
            c_sel = (
                gain_s * jnp.dot(pick, join(cot_s), preferred_element_type=jnp.float32)
            ).astype(jnp.bfloat16)
            for sel, parts in ((x_sel, x_parts), (c_sel, c_parts)):
                sel = sel.reshape(nx, cap, width)
                parts.append(sel[0])
                for k in range(1, nx):
                    parts.append(lax.ppermute(sel[k], "expert", x_pairs(k)))
        x_rows = jnp.concatenate(x_parts, axis=0)
        cot_rows = jnp.concatenate(c_parts, axis=0)

        gate_proj = jnp.dot(x_rows, w_gate[0], preferred_element_type=jnp.float32)
        up_proj = jnp.dot(x_rows, w_up[0], preferred_element_type=jnp.float32)
        sigmoid_gate = jax.nn.sigmoid(gate_proj)
        activated = gate_proj * sigmoid_gate
        hidden = (activated * up_proj).astype(jnp.bfloat16)
        d_hidden = lax.dot_general(
            cot_rows, w_down[0], (((1,), (1,)), ((), ())), preferred_element_type=jnp.float32
        )
        d_gate = (
            d_hidden * up_proj * sigmoid_gate * (1.0 + gate_proj * (1.0 - sigmoid_gate))
        ).astype(jnp.bfloat16)
        d_up = (d_hidden * activated).astype(jnp.bfloat16)

        def reduce_over_dp(left, right):
            n = left.shape[1] // n_dp

            def part(yy, cc):
                cols = lax.dynamic_slice_in_dim(left, (yy * NC + cc) * n, n, 1)
                return contract_rows(cols, right)

            def over_cores(yy):
                send = part(yy, 1 - c).astype(jnp.bfloat16)
                recv = lax.ppermute(send, "dp", core_pairs)
                return part(yy, c) + recv.astype(jnp.float32)

            arrived = []
            for k in range(1, ny):
                total = over_cores(y ^ k).astype(jnp.bfloat16)
                arrived.append(lax.ppermute(total, "dp", y_pairs(k)))
            total = over_cores(y)
            for a in arrived:
                total = total + a.astype(jnp.float32)
            return total.astype(jnp.bfloat16)[None]

        grad_down = reduce_over_dp(hidden, cot_rows)
        grad_gate = reduce_over_dp(x_rows, d_gate)
        grad_up = reduce_over_dp(x_rows, d_up)
        return grad_gate, grad_up, grad_down

    return per_device


def solution(mesh):
    in_specs = (
        P(("dp", "expert"), None),
        P(("dp", "expert"), None),
        P(("dp", "expert"), None),
        P(("dp", "expert"), None),
        P(),
        P("expert", None, None),
        P("expert", None, None),
        P("expert", None, None),
    )
    out_specs = (P("expert", "dp", None), P("expert", "dp", None), P("expert", "dp", None))
    per_device = make_per_device(mesh.shape["dp"], mesh.shape["expert"])
    return jax.shard_map(
        per_device, mesh=mesh, in_specs=in_specs, out_specs=out_specs, check_vma=False
    )
```

time: 467 us -> 352 us (0.75)
  waiting for transfers between devices: 340 us -> 210 us
  starting transfers between devices: 12.5 us -> 34.4 us
  between operations: 13.9 us -> 1.09 us
  matrix products: 61.8 us -> 74.5 us
    ppermute x0 -> x32, waiting for transfers between devices: none -> 210 us  [the longest x3 92.9 us: reduce_over_dp(): arrived.append(lax.ppermute(total, 'dp', y_pairs(k)))]
    all_to_all x2 -> x0, waiting for transfers between devices: 172 us -> none  [the longest x1 90.6 us: per_device(): lax.all_to_all(x_slots.reshape(experts_all, slots_per, width), 'expert',...]
    reduce_scatter x3 -> x0, waiting for transfers between devices: 169 us -> none  [the longest x1 68.8 us: per_device(): lax.psum_scatter(jnp.stack(up_list).astype(jnp.bfloat16), 'dp', scatter_d...]
    ppermute x0 -> x32, starting transfers between devices: none -> 34.4 us  [the longest x3 8.79 us: z_chain(): a = lax.ppermute(block, 'expert', ends_first)]
    gather x3 -> x0, local copies, waits for them, and re-layouts: 14.6 us -> none  [the longest x1 5.16 us: per_device(): cotangent[token_row].astype(jnp.float32)]
    all_to_all x2 -> x0, starting transfers between devices: 12 us -> none  [the longest x1 7.39 us: per_device(): lax.all_to_all(x_slots.reshape(experts_all, slots_per, width), 'expert',...]
    dot_general x3 -> x12, matrix products: 33.8 us -> 42.7 us  [contract_rows(): lax.dot_general(left, right, (((0,), (0,)), ((), ())), preferred_element_...]
    unnamed x10 -> x48, local copies, waits for them, and re-layouts: 3.24 us -> 11.6 us
  transfers between devices with their start and end apart: 5 -> 32, of which waited for: 5 -> 14; matrix products, arithmetic and copies ran while one was open for 13% -> 23% of each run, Pallas kernels for 0% -> 0%
where the time goes in v1:
time: 352 us; the launch traced here: 351 us
  waiting for transfers between devices  210 us (60%)
  matrix products  74.5 us (21%)
  starting transfers between devices  34.4 us (10%)
  local copies, waits for them, and re-layouts  19.1 us (5%)
  other arithmetic  12.2 us (3%)
    ppermute x3, waiting for transfers between devices, reduce_over_dp(): arrived.append(lax.ppermute(total, 'dp', y_pairs(k)))  92.9 us
    ppermute x3, waiting for transfers between devices, z_chain(): b_end = lax.ppermute(c_mid, 'expert', outward)  50.9 us
    dot_general x12, matrix products, contract_rows(): lax.dot_general(left, right, (((0,), (0,)), ((), ())), preferred_element_...  42.7 us
    ppermute x8, waiting for transfers between devices, per_device(): parts.append(lax.ppermute(sel[k], 'expert', x_pairs(k)))  39.6 us
    ppermute x3, waiting for transfers between devices, z_chain(): c_end = lax.ppermute(b_mid, 'expert', outward)  26.3 us
    unnamed x48, local copies, waits for them, and re-layouts  11.6 us
    dot_general x1, matrix products, per_device(): up_proj = jnp.dot(x_rows, w_up[0], preferred_element_type=jnp.float32)  10.1 us
    dot_general x1, matrix products, per_device(): lax.dot_general(cot_rows, w_down[0], (((1,), (1,)), ((), ())), preferred_...  9.06 us
  transfers between devices with their start and end apart: 32, of which 14 were waited for; matrix products, arithmetic and copies ran while one was open for 23% of the time, Pallas kernels for 0%

profile of v1, /device:TPU:0, one launch (start us, length us, event | category | flops | bytes accessed | tf_op | source)
XLA Modules:
  0.0 351.1 jit_solution(17042004906225367341)
XLA Ops:
  2.1 3.0 collective-permute-start.1
  5.8 4.5 %collective-permute-start.15 = (bf16[128,3584]{1,0:T(8,128)(2,1)}, bf16[128,3584]{1,0:T(8,128)(2,1)}, u32[]{:S(2)}, u32[]{:S(2)}) collective-permute-start(bf16[128,3584]{1,0:T(8,128)(2,1)} %param.9), channel_id=1, source_target_pairs={{0,2},{1,3},{2,0},{3,1},{4,6},{5,7},{6,4},{7,5},{8,10},{9,11},{10,... | collective-permute-start | bytes 2752520 | tf_op jit(solution)/shard_map/ppermute | solution.py:31
  16.6 33.5 %collective-permute-done.5 = f32[8,128]{1,0:T(8,128)S(1)} collective-permute-done((f32[8,128]{1,0:T(8,128)S(1)}, f32[8,128]{1,0:T(8,128)S(1)}, u32[]{:S(2)}, u32[]{:S(2)}) %collective-permute-start.5) | collective-permute-done | bytes 4128 | tf_op jit(solution)/shard_map/ppermute | solution.py:33
  58.2 13.1 %collective-permute-done.14 = bf16[80,3584]{1,0:T(8,128)(2,1)} collective-permute-done((bf16[80,3584]{1,0:T(8,128)(2,1)}, bf16[80,3584]{1,0:T(8,128)(2,1)}, u32[]{:S(2)}, u32[]{:S(2)}) %collective-permute-start.14) | collective-permute-done | bytes 573472 | tf_op jit(solution)/shard_map/ppermute | solution.py:94
  74.9 6.4 %collective-permute-done = bf16[80,3584]{1,0:T(8,128)(2,1)} collective-permute-done((bf16[80,3584]{1,0:T(8,128)(2,1)S(1)}, bf16[80,3584]{1,0:T(8,128)(2,1)}, u32[]{:S(2)}, u32[]{:S(2)}) %collective-permute-start) | collective-permute-done | bytes 573472 | tf_op jit(solution)/shard_map/ppermute | solution.py:94
  92.3 9.5 %collective-permute-done.16 = bf16[80,3584]{1,0:T(8,128)(2,1)} collective-permute-done((bf16[80,3584]{1,0:T(8,128)(2,1)S(1)}, bf16[80,3584]{1,0:T(8,128)(2,1)}, u32[]{:S(2)}, u32[]{:S(2)}) %collective-permute-start.16) | collective-permute-done | bytes 573472 | tf_op jit(solution)/shard_map/ppermute | solution.py:94
  105.0 5.8 %collective-permute-done.3 = bf16[80,3584]{1,0:T(8,128)(2,1)} collective-permute-done((bf16[80,3584]{1,0:T(8,128)(2,1)}, bf16[80,3584]{1,0:T(8,128)(2,1)}, u32[]{:S(2)}, u32[]{:S(2)}) %collective-permute-start.3) | collective-permute-done | bytes 573472 | tf_op jit(solution)/shard_map/ppermute | solution.py:94
  112.7 4.8 %collective-permute-done.18 = bf16[128,3584]{1,0:T(8,128)(2,1)S(1)} collective-permute-done((bf16[128,3584]{1,0:T(8,128)(2,1)S(1)}, bf16[128,3584]{1,0:T(8,128)(2,1)S(1)}, u32[]{:S(2)}, u32[]{:S(2)}) %collective-permute-start.18) | collective-permute-done | bytes 917536 | tf_op jit(solution)/shard_map/ppermute | solution.py:33
  120.4 12.6 %collective-permute-done.8 = bf16[128,3584]{1,0:T(8,128)(2,1)S(1)} collective-permute-done((bf16[128,3584]{1,0:T(8,128)(2,1)}, bf16[128,3584]{1,0:T(8,128)(2,1)S(1)}, u32[]{:S(2)}, u32[]{:S(2)}) %collective-permute-start.8) | collective-permute-done | bytes 917536 | tf_op jit(solution)/shard_map/ppermute | solution.py:33
  140.8 4.8 %collective-permute-done.10 = bf16[80,3584]{1,0:T(8,128)(2,1)} collective-permute-done((bf16[80,3584]{1,0:T(8,128)(2,1)}, bf16[80,3584]{1,0:T(8,128)(2,1)}, u32[]{:S(2)}, u32[]{:S(2)}) %collective-permute-start.10) | collective-permute-done | bytes 573472 | tf_op jit(solution)/shard_map/ppermute | solution.py:94
  147.5 13.9 %collective-permute-done.21 = bf16[128,3584]{1,0:T(8,128)(2,1)S(1)} collective-permute-done((bf16[128,3584]{1,0:T(8,128)(2,1)S(1)}, bf16[128,3584]{1,0:T(8,128)(2,1)S(1)}, u32[]{:S(2)}, u32[]{:S(2)}) %collective-permute-start.21) | collective-permute-done | bytes 917536 | tf_op jit(solution)/shard_map/ppermute | solution.py:35
  163.3 12.3 %collective-permute-done.12 = bf16[128,3584]{1,0:T(8,128)(2,1)S(1)} collective-permute-done((bf16[128,3584]{1,0:T(8,128)(2,1)}, bf16[128,3584]{1,0:T(8,128)(2,1)S(1)}, u32[]{:S(2)}, u32[]{:S(2)}) %collective-permute-start.12) | collective-permute-done | bytes 917536 | tf_op jit(solution)/shard_map/ppermute | solution.py:35
  178.0 9.1 %fusion.4 = f32[640,1024]{1,0:T(8,128)S(1)} fusion(bf16[640,3584]{1,0:T(8,128)(2,1)S(1)} %constant_dynamic-update-slice_fusion.4, bf16[1,1024,3584]{2,1,0:T(8,128)(2,1)} %param.15), kind=kOutput, calls=%fused_computation.4 | convolution fusion | flops 4697620480 | bytes 14548992 | tf_op jit(solution)/shard_map/dot_general | solution.py:103
  187.2 4.9 %fusion = f32[640,1024]{1,0:T(8,128)S(1)} fusion(bf16[640,3584]{1,0:T(8,128)(2,1)S(1)} %constant_dynamic-update-slice_fusion, bf16[1,3584,1024]{2,1,0:T(8,128)(2,1)S(1)} %bitcast.86), kind=kOutput, calls=%fused_computation | convolution fusion | flops 4697620480 | bytes 14548992 | tf_op jit(solution)/shard_map/dot_general | solution.py:98
  192.1 10.1 %multiply_convert_fusion = (bf16[640,1024]{1,0:T(8,128)(2,1)S(1)}, bf16[640,1024]{1,0:T(8,128)(2,1)}, bf16[640,1024]{1,0:T(8,128)(2,1)S(1)}) fusion(f32[640,1024]{1,0:T(8,128)S(1)} %fusion, f32[640,1024]{1,0:T(8,128)S(1)} %fusion.4, bf16[640,3584]{1,0:T(8,128)(2,1)S(1)} %constant_dynamic-update-slice_fusion, bf16[1,3584,1024]{2,1,0:T(8,128)(2,1)} %param.14), kind=kOutput, calls=%fused_computation.30 | convolution fusion | flops 4707450880 | bytes 21102592 | tf_op jit(solution)/shard_map/dot_general | solution.py:99
  202.2 2.9 convolution_convert_fusion.6
  205.1 5.2 %convolution_convert_fusion = bf16[256,3584]{1,0:T(8,128)(2,1)} fusion(bf16[640,3584]{1,0:T(8,128)(2,1)} %copy-done.1, bf16[640,1024]{1,0:T(8,128)(2,1)S(1)} %get-tuple-element.13, s32[]{:T(128)S(6)} %select_n.96), kind=kOutput, calls=%fused_computation.9 | convolution fusion | flops 1175322624 | bytes 6750212 | tf_op jit(solution)/shard_map/dot_general | solution.py:11
  210.8 3.4 convolution_convert_fusion.8
  214.3 3.6 %convolution_convert_fusion.7 = bf16[896,1024]{1,0:T(8,128)(2,1)S(1)} fusion(bf16[640,1024]{1,0:T(8,128)(2,1)} %copy-done.11, bf16[640,3584]{1,0:T(8,128)(2,1)} %copy-done.8, s32[]{:T(128)S(6)} %select_n.90), kind=kOutput, calls=%fused_computation.38 | convolution fusion | flops 1175322624 | bytes 4292612 | tf_op jit(solution)/shard_map/dot_general | solution.py:11
  218.4 3.0 convolution_convert_fusion.1
  221.5 4.4 %add_convert_fusion.1 = bf16[896,1024]{1,0:T(8,128)(2,1)} fusion(bf16[896,1024]{1,0:T(8,128)(2,1)} %collective-permute-done.27, bf16[640,1024]{1,0:T(8,128)(2,1)S(1)} %copy-done.12, bf16[640,3584]{1,0:T(8,128)(2,1)S(1)} %bitcast.82, s32[]{:T(128)S(6)} %select_n.91), kind=kOutput, calls=%fused_computation.27 | convolution fusion | flops 1177157632 | bytes 6127620 | tf_op jit(solution)/shard_map/dot_general | solution.py:11
  227.5 2.9 fusion.7
  230.9 2.9 convolution_convert_fusion.9
  233.8 2.9 add_convert_fusion.3
  238.3 3.4 fusion.23
  241.7 3.0 fusion.25
  244.7 24.3 %collective-permute-done.28 = bf16[896,1024]{1,0:T(8,128)(2,1)} collective-permute-done((bf16[896,1024]{1,0:T(8,128)(2,1)}, bf16[896,1024]{1,0:T(8,128)(2,1)}, u32[]{:S(2)}, u32[]{:S(2)}) %collective-permute-start.28) | collective-permute-done | bytes 1835040 | tf_op jit(solution)/shard_map/ppermute | solution.py:126
  269.0 4.4 %fusion.16 = bf16[1,896,1024]{2,1,0:T(8,128)(2,1)} fusion(bf16[896,1024]{1,0:T(8,128)(2,1)} %collective-permute-done.28, f32[896,1024]{1,0:T(8,128)S(1)} %fusion.23, bf16[896,1024]{1,0:T(8,128)(2,1)} %collective-permute-done.26), kind=kLoop, calls=%fused_computation.36 | loop fusion | flops 4587520 | bytes 9175040 | tf_op jit(solution)/shard_map/broadcast_in_dim | solution.py:130
  273.4 34.9 %collective-permute-done.31 = bf16[256,3584]{1,0:T(8,128)(2,1)} collective-permute-done((bf16[256,3584]{1,0:T(8,128)(2,1)}, bf16[256,3584]{1,0:T(8,128)(2,1)}, u32[]{:S(2)}, u32[]{:S(2)}) %collective-permute-start.31) | collective-permute-done | bytes 1835040 | tf_op jit(solution)/shard_map/ppermute | solution.py:126
  308.4 5.1 %fusion.9 = bf16[1,256,3584]{2,1,0:T(8,128)(2,1)} fusion(bf16[640,3584]{1,0:T(8,128)(2,1)S(1)} %bitcast.80, bf16[256,3584]{1,0:T(8,128)(2,1)} %collective-permute-done.31, bf16[256,3584]{1,0:T(8,128)(2,1)} %collective-permute-done.29, bf16[640,1024]{1,0:T(8,128)(2,1)S(1)} %get-tuple-element.13, s32[]{:T(128)S(6)} %select_n.93), kind=kOutput, calls=%fused_computation.17 | convolution fusion | flops 1178992640 | bytes 10420228 | tf_op jit(solution)/shard_map/dot_general | solution.py:11
  313.5 33.7 %collective-permute-done.25 = bf16[896,1024]{1,0:T(8,128)(2,1)} collective-permute-done((bf16[896,1024]{1,0:T(8,128)(2,1)}, bf16[896,1024]{1,0:T(8,128)(2,1)}, u32[]{:S(2)}, u32[]{:S(2)}) %collective-permute-start.25) | collective-permute-done | bytes 1835040 | tf_op jit(solution)/shard_map/ppermute | solution.py:126
  347.2 3.8 %fusion.15 = bf16[1,896,1024]{2,1,0:T(8,128)(2,1)} fusion(bf16[896,1024]{1,0:T(8,128)(2,1)} %collective-permute-done.25, f32[896,1024]{1,0:T(8,128)S(1)} %fusion.25, bf16[896,1024]{1,0:T(8,128)(2,1)S(1)} %collective-permute-done.23), kind=kLoop, calls=%fused_computation.35 | loop fusion | flops 4587520 | bytes 9175040 | tf_op jit(solution)/shard_map/broadcast_in_dim | solution.py:130
  (147 shorter events, 57.9 us)
Async XLA Ops:
  2.1 11.2 %collective-permute-start.1 = (f32[8,128]{1,0:T(8,128)S(1)}, f32[8,128]{1,0:T(8,128)S(1)}, u32[]{:S(2)}, u32[]{:S(2)}) collective-permute-start(f32[8,128]{1,0:T(8,128)S(1)} %pad_maximum_fusion), channel_id=1, source_target_pairs={{0,2},{1,3},{2,0},{3,1},{4,6},{5,7},{6,4},{7,5},{8,10},{9,11},{10,... | collective-permute-start | bytes 12296 | tf_op jit(solution)/shard_map/ppermute | solution.py:31
  5.1 8.8 %collective-permute-start.4 = (f32[8,128]{1,0:T(8,128)S(1)}, f32[8,128]{1,0:T(8,128)S(1)}, u32[]{:S(2)}, u32[]{:S(2)}) collective-permute-start(f32[8,128]{1,0:T(8,128)S(1)} %pad_maximum_fusion), channel_id=1, source_target_pairs={{2,4},{3,5},{4,2},{5,3},{10,12},{11,13},{12,10},{13,11},{18,20},{1... | collective-permute-start | bytes 12296 | tf_op jit(solution)/shard_map/ppermute | solution.py:32
  5.8 77.4 %collective-permute-start.15 = (bf16[128,3584]{1,0:T(8,128)(2,1)}, bf16[128,3584]{1,0:T(8,128)(2,1)}, u32[]{:S(2)}, u32[]{:S(2)}) collective-permute-start(bf16[128,3584]{1,0:T(8,128)(2,1)} %param.9), channel_id=1, source_target_pairs={{0,2},{1,3},{2,0},{3,1},{4,6},{5,7},{6,4},{7,5},{8,10},{9,11},{10,... | collective-permute-start | bytes 2752520 | tf_op jit(solution)/shard_map/ppermute | solution.py:31
  10.2 80.0 %collective-permute-start.17 = (bf16[128,3584]{1,0:T(8,128)(2,1)}, bf16[128,3584]{1,0:T(8,128)(2,1)S(1)}, u32[]{:S(2)}, u32[]{:S(2)}) collective-permute-start(bf16[128,3584]{1,0:T(8,128)(2,1)} %param.9), channel_id=1, source_target_pairs={{2,4},{3,5},{4,2},{5,3},{10,12},{11,13},{12,10},{13,11},{18,20},{1... | collective-permute-start | bytes 2752520 | tf_op jit(solution)/shard_map/ppermute | solution.py:32
  11.0 76.3 %collective-permute-start.2 = (bf16[128,3584]{1,0:T(8,128)(2,1)}, bf16[128,3584]{1,0:T(8,128)(2,1)S(1)}, u32[]{:S(2)}, u32[]{:S(2)}) collective-permute-start(bf16[128,3584]{1,0:T(8,128)(2,1)} %param.8), channel_id=1, source_target_pairs={{0,2},{1,3},{2,0},{3,1},{4,6},{5,7},{6,4},{7,5},{8,10},{9,11},{10,... | collective-permute-start | bytes 2752520 | tf_op jit(solution)/shard_map/ppermute | solution.py:31
  13.3 2.0 collective-permute-start.6
  14.0 36.1 %collective-permute-start.5 = (f32[8,128]{1,0:T(8,128)S(1)}, f32[8,128]{1,0:T(8,128)S(1)}, u32[]{:S(2)}, u32[]{:S(2)}) collective-permute-start(f32[8,128]{1,0:T(8,128)S(1)} %collective-permute-done.4), channel_id=1, source_target_pairs={{2,0},{3,1},{4,6},{5,7},{10,8},{11,9},{12,14},{13,15},{18,16},{19,... | collective-permute-start | bytes 12296 | tf_op jit(solution)/shard_map/ppermute | solution.py:33
  15.3 34.8 %collective-permute-start.11 = (f32[8,128]{1,0:T(8,128)S(1)}, f32[8,128]{1,0:T(8,128)S(1)}, u32[]{:S(2)}, u32[]{:S(2)}) collective-permute-start(f32[8,128]{1,0:T(8,128)S(1)} %collective-permute-done.6), channel_id=1, source_target_pairs={{2,0},{3,1},{4,6},{5,7},{10,8},{11,9},{12,14},{13,15},{18,16},{19,... | collective-permute-start | bytes 12296 | tf_op jit(solution)/shard_map/ppermute | solution.py:35
  55.1 16.2 %collective-permute-start.14 = (bf16[80,3584]{1,0:T(8,128)(2,1)}, bf16[80,3584]{1,0:T(8,128)(2,1)}, u32[]{:S(2)}, u32[]{:S(2)}) collective-permute-start(bf16[80,3584]{1,0:T(8,128)(2,1)} %get-tuple-element.22), channel_id=1, source_target_pairs={{0,1},{1,0},{2,3},{3,2},{4,5},{5,4},{6,7},{7,6},{8,9},{9,8},{10,11... | collective-permute-start | bytes 1720328 | tf_op jit(solution)/shard_map/ppermute | solution.py:94
  57.5 23.8 %collective-permute-start = (bf16[80,3584]{1,0:T(8,128)(2,1)S(1)}, bf16[80,3584]{1,0:T(8,128)(2,1)}, u32[]{:S(2)}, u32[]{:S(2)}) collective-permute-start(bf16[80,3584]{1,0:T(8,128)(2,1)S(1)} %get-tuple-element.30), channel_id=1, source_target_pairs={{0,1},{1,0},{2,3},{3,2},{4,5},{5,4},{6,7},{7,6},{8,9},{9,8},{10,11... | collective-permute-start | bytes 1720328 | tf_op jit(solution)/shard_map/ppermute | solution.py:94
  71.4 19.6 %collective-permute-start.7 = (bf16[128,3584]{1,0:T(8,128)(2,1)S(1)}, bf16[128,3584]{1,0:T(8,128)(2,1)}, u32[]{:S(2)}, u32[]{:S(2)}) collective-permute-start(bf16[128,3584]{1,0:T(8,128)(2,1)S(1)} %copy-done.3), channel_id=1, source_target_pairs={{2,4},{3,5},{4,2},{5,3},{10,12},{11,13},{12,10},{13,11},{18,20},{1... | collective-permute-start | bytes 2752520 | tf_op jit(solution)/shard_map/ppermute | solution.py:32
  85.7 16.0 %collective-permute-start.16 = (bf16[80,3584]{1,0:T(8,128)(2,1)S(1)}, bf16[80,3584]{1,0:T(8,128)(2,1)}, u32[]{:S(2)}, u32[]{:S(2)}) collective-permute-start(bf16[80,3584]{1,0:T(8,128)(2,1)S(1)} %get-tuple-element.20), channel_id=1, source_target_pairs={{0,1},{1,0},{2,3},{3,2},{4,5},{5,4},{6,7},{7,6},{8,9},{9,8},{10,11... | collective-permute-start | bytes 1720328 | tf_op jit(solution)/shard_map/ppermute | solution.py:94
  88.8 21.9 %collective-permute-start.3 = (bf16[80,3584]{1,0:T(8,128)(2,1)}, bf16[80,3584]{1,0:T(8,128)(2,1)}, u32[]{:S(2)}, u32[]{:S(2)}) collective-permute-start(bf16[80,3584]{1,0:T(8,128)(2,1)} %get-tuple-element.28), channel_id=1, source_target_pairs={{0,1},{1,0},{2,3},{3,2},{4,5},{5,4},{6,7},{7,6},{8,9},{9,8},{10,11... | collective-permute-start | bytes 1720328 | tf_op jit(solution)/shard_map/ppermute | solution.py:94
  89.5 23.1 %collective-permute-start.19 = (bf16[128,3584]{1,0:T(8,128)(2,1)}, bf16[128,3584]{1,0:T(8,128)(2,1)S(1)}, u32[]{:S(2)}, u32[]{:S(2)}) collective-permute-start(bf16[128,3584]{1,0:T(8,128)(2,1)} %collective-permute-done.15), channel_id=1, source_target_pairs={{2,4},{3,5},{4,2},{5,3},{10,12},{11,13},{12,10},{13,11},{18,20},{1... | collective-permute-start | bytes 2752520 | tf_op jit(solution)/shard_map/ppermute | solution.py:34
  90.3 30.1 %collective-permute-start.9 = (bf16[128,3584]{1,0:T(8,128)(2,1)S(1)}, bf16[128,3584]{1,0:T(8,128)(2,1)S(1)}, u32[]{:S(2)}, u32[]{:S(2)}) collective-permute-start(bf16[128,3584]{1,0:T(8,128)(2,1)S(1)} %collective-permute-done.2), channel_id=1, source_target_pairs={{2,4},{3,5},{4,2},{5,3},{10,12},{11,13},{12,10},{13,11},{18,20},{1... | collective-permute-start | bytes 2752520 | tf_op jit(solution)/shard_map/ppermute | solution.py:34
  91.0 26.5 %collective-permute-start.18 = (bf16[128,3584]{1,0:T(8,128)(2,1)S(1)}, bf16[128,3584]{1,0:T(8,128)(2,1)S(1)}, u32[]{:S(2)}, u32[]{:S(2)}) collective-permute-start(bf16[128,3584]{1,0:T(8,128)(2,1)S(1)} %collective-permute-done.17), channel_id=1, source_target_pairs={{2,0},{3,1},{4,6},{5,7},{10,8},{11,9},{12,14},{13,15},{18,16},{19,... | collective-permute-start | bytes 2752520 | tf_op jit(solution)/shard_map/ppermute | solution.py:33
  101.8 31.2 %collective-permute-start.8 = (bf16[128,3584]{1,0:T(8,128)(2,1)}, bf16[128,3584]{1,0:T(8,128)(2,1)S(1)}, u32[]{:S(2)}, u32[]{:S(2)}) collective-permute-start(bf16[128,3584]{1,0:T(8,128)(2,1)} %collective-permute-done.7), channel_id=1, source_target_pairs={{2,0},{3,1},{4,6},{5,7},{10,8},{11,9},{12,14},{13,15},{18,16},{19,... | collective-permute-start | bytes 2752520 | tf_op jit(solution)/shard_map/ppermute | solution.py:33
  118.9 19.9 %collective-permute-start.20 = (bf16[80,3584]{1,0:T(8,128)(2,1)S(1)}, bf16[80,3584]{1,0:T(8,128)(2,1)}, u32[]{:S(2)}, u32[]{:S(2)}) collective-permute-start(bf16[80,3584]{1,0:T(8,128)(2,1)S(1)} %get-tuple-element.18), channel_id=1, source_target_pairs={{0,1},{1,0},{2,3},{3,2},{4,5},{5,4},{6,7},{7,6},{8,9},{9,8},{10,11... | collective-permute-start | bytes 1720328 | tf_op jit(solution)/shard_map/ppermute | solution.py:94
  134.5 11.1 %collective-permute-start.10 = (bf16[80,3584]{1,0:T(8,128)(2,1)}, bf16[80,3584]{1,0:T(8,128)(2,1)}, u32[]{:S(2)}, u32[]{:S(2)}) collective-permute-start(bf16[80,3584]{1,0:T(8,128)(2,1)} %get-tuple-element.26), channel_id=1, source_target_pairs={{0,1},{1,0},{2,3},{3,2},{4,5},{5,4},{6,7},{7,6},{8,9},{9,8},{10,11... | collective-permute-start | bytes 1720328 | tf_op jit(solution)/shard_map/ppermute | solution.py:94
  136.2 25.2 %collective-permute-start.21 = (bf16[128,3584]{1,0:T(8,128)(2,1)S(1)}, bf16[128,3584]{1,0:T(8,128)(2,1)S(1)}, u32[]{:S(2)}, u32[]{:S(2)}) collective-permute-start(bf16[128,3584]{1,0:T(8,128)(2,1)S(1)} %copy-done.6), channel_id=1, source_target_pairs={{2,0},{3,1},{4,6},{5,7},{10,8},{11,9},{12,14},{13,15},{18,16},{19,... | collective-permute-start | bytes 2752520 | tf_op jit(solution)/shard_map/ppermute | solution.py:35
  137.5 38.1 %collective-permute-start.12 = (bf16[128,3584]{1,0:T(8,128)(2,1)}, bf16[128,3584]{1,0:T(8,128)(2,1)S(1)}, u32[]{:S(2)}, u32[]{:S(2)}) collective-permute-start(bf16[128,3584]{1,0:T(8,128)(2,1)} %copy-done.4), channel_id=1, source_target_pairs={{2,0},{3,1},{4,6},{5,7},{10,8},{11,9},{12,14},{13,15},{18,16},{19,... | collective-permute-start | bytes 2752520 | tf_op jit(solution)/shard_map/ppermute | solution.py:35
  162.8 15.1 %collective-permute-start.22 = (bf16[80,3584]{1,0:T(8,128)(2,1)S(1)}, bf16[80,3584]{1,0:T(8,128)(2,1)S(1)}, u32[]{:S(2)}, u32[]{:S(2)}) collective-permute-start(bf16[80,3584]{1,0:T(8,128)(2,1)S(1)} %get-tuple-element.16), channel_id=1, source_target_pairs={{0,1},{1,0},{2,3},{3,2},{4,5},{5,4},{6,7},{7,6},{8,9},{9,8},{10,11... | collective-permute-start | bytes 1720328 | tf_op jit(solution)/shard_map/ppermute | solution.py:94
  177.4 9.8 %collective-permute-start.13 = (bf16[80,3584]{1,0:T(8,128)(2,1)S(1)}, bf16[80,3584]{1,0:T(8,128)(2,1)S(1)}, u32[]{:S(2)}, u32[]{:S(2)}) collective-permute-start(bf16[80,3584]{1,0:T(8,128)(2,1)S(1)} %get-tuple-element.24), channel_id=1, source_target_pairs={{0,1},{1,0},{2,3},{3,2},{4,5},{5,4},{6,7},{7,6},{8,9},{9,8},{10,11... | collective-permute-start | bytes 1720328 | tf_op jit(solution)/shard_map/ppermute | solution.py:94
  205.1 16.4 %collective-permute-start.27 = (bf16[896,1024]{1,0:T(8,128)(2,1)}, bf16[896,1024]{1,0:T(8,128)(2,1)}, u32[]{:S(2)}, u32[]{:S(2)}) collective-permute-start(bf16[896,1024]{1,0:T(8,128)(2,1)} %convolution_convert_fusion.6), channel_id=1, source_target_pairs={{0,8},{8,0},{16,24},{24,16},{1,9},{9,1},{17,25},{25,17},{2,10},{10... | collective-permute-start | bytes 5505032 | tf_op jit(solution)/shard_map/ppermute | solution.py:120
  210.3 17.2 %collective-permute-start.30 = (bf16[256,3584]{1,0:T(8,128)(2,1)}, bf16[256,3584]{1,0:T(8,128)(2,1)S(1)}, u32[]{:S(2)}, u32[]{:S(2)}) collective-permute-start(bf16[256,3584]{1,0:T(8,128)(2,1)} %convolution_convert_fusion), channel_id=1, source_target_pairs={{0,8},{8,0},{16,24},{24,16},{1,9},{9,1},{17,25},{25,17},{2,10},{10... | collective-permute-start | bytes 5505032 | tf_op jit(solution)/shard_map/ppermute | solution.py:120
  214.2 19.5 %collective-permute-start.24 = (bf16[896,1024]{1,0:T(8,128)(2,1)S(1)}, bf16[896,1024]{1,0:T(8,128)(2,1)S(1)}, u32[]{:S(2)}, u32[]{:S(2)}) collective-permute-start(bf16[896,1024]{1,0:T(8,128)(2,1)S(1)} %convolution_convert_fusion.8), channel_id=1, source_target_pairs={{0,8},{8,0},{16,24},{24,16},{1,9},{9,1},{17,25},{25,17},{2,10},{10... | collective-permute-start | bytes 5505032 | tf_op jit(solution)/shard_map/ppermute | solution.py:120
  217.9 18.7 %collective-permute-start.26 = (bf16[896,1024]{1,0:T(8,128)(2,1)S(1)}, bf16[896,1024]{1,0:T(8,128)(2,1)}, u32[]{:S(2)}, u32[]{:S(2)}) collective-permute-start(bf16[896,1024]{1,0:T(8,128)(2,1)S(1)} %convolution_convert_fusion.7), channel_id=1, source_target_pairs={{0,8},{8,0},{16,24},{24,16},{1,9},{9,1},{17,25},{25,17},{2,10},{10... | collective-permute-start | bytes 5505032 | tf_op jit(solution)/shard_map/ppermute | solution.py:120
  221.4 52.0 %collective-permute-start.29 = (bf16[256,3584]{1,0:T(8,128)(2,1)}, bf16[256,3584]{1,0:T(8,128)(2,1)}, u32[]{:S(2)}, u32[]{:S(2)}) collective-permute-start(bf16[256,3584]{1,0:T(8,128)(2,1)} %convolution_convert_fusion.1), channel_id=1, source_target_pairs={{0,8},{8,0},{16,24},{24,16},{1,9},{9,1},{17,25},{25,17},{2,10},{10... | collective-permute-start | bytes 5505032 | tf_op jit(solution)/shard_map/ppermute | solution.py:120
  225.9 43.1 %collective-permute-start.28 = (bf16[896,1024]{1,0:T(8,128)(2,1)}, bf16[896,1024]{1,0:T(8,128)(2,1)}, u32[]{:S(2)}, u32[]{:S(2)}) collective-permute-start(bf16[896,1024]{1,0:T(8,128)(2,1)} %add_convert_fusion.1), channel_id=1, source_target_pairs={{0,16},{8,24},{16,0},{24,8},{1,17},{9,25},{17,1},{25,9},{2,18},{10... | collective-permute-start | bytes 5505032 | tf_op jit(solution)/shard_map/ppermute | solution.py:126
  230.4 77.9 %collective-permute-start.31 = (bf16[256,3584]{1,0:T(8,128)(2,1)}, bf16[256,3584]{1,0:T(8,128)(2,1)}, u32[]{:S(2)}, u32[]{:S(2)}) collective-permute-start(bf16[256,3584]{1,0:T(8,128)(2,1)} %fusion.7), channel_id=1, source_target_pairs={{0,16},{8,24},{16,0},{24,8},{1,17},{9,25},{17,1},{25,9},{2,18},{10... | collective-permute-start | bytes 5505032 | tf_op jit(solution)/shard_map/ppermute | solution.py:126
  233.8 79.8 %collective-permute-start.23 = (bf16[896,1024]{1,0:T(8,128)(2,1)}, bf16[896,1024]{1,0:T(8,128)(2,1)S(1)}, u32[]{:S(2)}, u32[]{:S(2)}) collective-permute-start(bf16[896,1024]{1,0:T(8,128)(2,1)} %convolution_convert_fusion.9), channel_id=1, source_target_pairs={{0,8},{8,0},{16,24},{24,16},{1,9},{9,1},{17,25},{25,17},{2,10},{10... | collective-permute-start | bytes 5505032 | tf_op jit(solution)/shard_map/ppermute | solution.py:120
  236.7 110.6 %collective-permute-start.25 = (bf16[896,1024]{1,0:T(8,128)(2,1)}, bf16[896,1024]{1,0:T(8,128)(2,1)}, u32[]{:S(2)}, u32[]{:S(2)}) collective-permute-start(bf16[896,1024]{1,0:T(8,128)(2,1)} %add_convert_fusion.3), channel_id=1, source_target_pairs={{0,16},{8,24},{16,0},{24,8},{1,17},{9,25},{17,1},{25,9},{2,18},{10... | collective-permute-start | bytes 5505032 | tf_op jit(solution)/shard_map/ppermute | solution.py:126
  (21 other events, 356.7 us)

commit v2 on v1

v2 whole, which is shorter than its diff:
```python
import functools

import jax
import jax.numpy as jnp
from jax import lax
from jax.experimental import pallas as pl
from jax.experimental.pallas import tpu as pltpu
from jax.sharding import PartitionSpec as P

NZ = 4
NC = 2
F32, BF16 = jnp.float32, jnp.bfloat16
COST = pl.CostEstimate(flops=1000, bytes_accessed=1000, transcendentals=0)


LANES = 128


def params(mib):
    return pltpu.CompilerParams(vmem_limit_bytes=mib << 20)


def contract_rows(left, right):
    return lax.dot_general(left, right, (((0,), (0,)), ((), ())), preferred_element_type=F32)


def after(values, *deps):
    return lax.optimization_barrier((values, deps))[0]


def pack_kernel(routes_ref, gain_ref, tok_ref, cot_ref, out_ref):
    top = routes_ref.shape[0]
    toks, width = tok_ref.shape
    g = gain_ref[...]
    high = g.astype(BF16)
    g = g - high.astype(F32)
    mid = g.astype(BF16)
    low = (g - mid.astype(F32)).astype(BF16)
    rows = [routes_ref[...].astype(F32), high.astype(F32), mid.astype(F32), low.astype(F32)]
    total = jnp.zeros((toks, LANES), F32)
    for i, r in enumerate(rows):
        row = lax.broadcasted_iota(jnp.int32, (top, LANES), 0)
        col = lax.broadcasted_iota(jnp.int32, (top, LANES), 1)
        place = jnp.where(col == row + i * top, 1.0, 0.0).astype(BF16)
        total = total + contract_rows(r.astype(BF16), place)
    out_ref[:toks, :width] = tok_ref[...]
    out_ref[:toks, width:] = total.astype(BF16)
    out_ref[toks:, :width] = cot_ref[...]
    out_ref[toks:, width:] = jnp.zeros((toks, LANES), BF16)


def pack(tokens, cotangent, routes, gain):
    toks, width = tokens.shape
    return pl.pallas_call(
        pack_kernel,
        in_specs=[pl.BlockSpec(memory_space=pltpu.VMEM)] * 4,
        out_specs=pl.BlockSpec(memory_space=pltpu.VMEM),
        out_shape=jax.ShapeDtypeStruct((2 * toks, width + LANES), BF16),
        compiler_params=params(8),
        cost_estimate=COST,
        name="pack",
    )(routes.T, gain.T, tokens, cotangent)


def added(refs):
    value = refs[0][...]
    for r in refs[1:]:
        value = value + r[...]
    return value


def pick_kernel(ids_ref, *refs, nx, top, n_meta, n_x, n_c):
    meta_refs, refs = refs[:n_meta], refs[n_meta:]
    x_refs, c_refs, refs = refs[:n_x], refs[n_x : n_x + n_c], refs[n_x + n_c :]
    kinds = (1 if n_x else 0) + (1 if n_c else 0)
    own_refs, send_refs = refs[:kinds], refs[kinds : kinds + nx - 1]
    pick_ref, gain_ref = refs[-2:]
    cap, toks = pick_ref.shape[1:]

    @pl.when(pl.program_id(0) == 0)
    def _():
        row = lax.broadcasted_iota(jnp.int32, (4 * top, LANES), 0)
        col = lax.broadcasted_iota(jnp.int32, (4 * top, LANES), 1)
        place = jnp.where(col == row, 1.0, 0.0).astype(BF16)
        meta = lax.dot_general(
            place, added(meta_refs), (((1,), (1,)), ((), ())), preferred_element_type=F32
        )
        r = meta[0:top]
        g = (meta[top : 2 * top] + meta[2 * top : 3 * top]) + meta[3 * top :]
        row = lax.broadcasted_iota(jnp.int32, (toks, toks), 0)
        col = lax.broadcasted_iota(jnp.int32, (toks, toks), 1)
        before = jnp.where(row < col, 1.0, 0.0).astype(BF16)
        place = lax.broadcasted_iota(jnp.int32, (cap, toks), 0).astype(F32)
        for k in range(nx):
            named = r == ids_ref[0, k].astype(F32)
            alive = ids_ref[1, k].astype(F32)
            match = jnp.sum(jnp.where(named, 1.0, 0.0), axis=0, keepdims=True) * alive
            gain_t = jnp.sum(jnp.where(named, g, 0.0), axis=0, keepdims=True)
            wide = jnp.broadcast_to(match, (8, toks)).astype(BF16)
            pos = jnp.dot(wide, before, preferred_element_type=F32)[0:1]
            pick = jnp.where(place == pos, jnp.broadcast_to(match, (cap, toks)), 0.0)
            pick_ref[k] = pick.astype(BF16)
            if n_c:
                gain_ref[k] = jnp.sum(pick * gain_t, axis=1, keepdims=True)

    for i, (block_refs, weighted) in enumerate(
        ([(x_refs, False)] if n_x else []) + ([(c_refs, True)] if n_c else [])
    ):
        block = added(block_refs)
        for k in range(nx):
            sel = jnp.dot(pick_ref[k], block, preferred_element_type=F32)
            if weighted:
                sel = gain_ref[k] * sel
            if k == 0:
                own_refs[i][...] = sel.astype(BF16)
            else:
                send_refs[k - 1][i * cap : (i + 1) * cap, :] = sel.astype(BF16)


def pick_rows(ids, metas, xs, cs, nx, cap, top, width, toks):
    tile = width // 4
    kinds = (1 if xs else 0) + (1 if cs else 0)
    out = pl.pallas_call(
        functools.partial(
            pick_kernel, nx=nx, top=top, n_meta=len(metas), n_x=len(xs), n_c=len(cs)
        ),
        grid=(width // tile,),
        in_specs=[pl.BlockSpec(memory_space=pltpu.SMEM)]
        + [pl.BlockSpec((toks, LANES), lambda j: (0, width // LANES))] * len(metas)
        + [pl.BlockSpec((toks, tile), lambda j: (0, j))] * len(xs)
        + [
            pl.BlockSpec((toks, tile), lambda j, at=v.shape[0] // toks - 1: (at, j)) for v in cs
        ],
        out_specs=[pl.BlockSpec((cap, tile), lambda j: (0, j))] * kinds
        + [pl.BlockSpec((kinds * cap, tile), lambda j: (0, j))] * (nx - 1),
        out_shape=[jax.ShapeDtypeStruct((cap, width), BF16)] * kinds
        + [jax.ShapeDtypeStruct((kinds * cap, width), BF16)] * (nx - 1),
        scratch_shapes=[pltpu.VMEM((nx, cap, toks), BF16), pltpu.VMEM((nx, cap, 1), F32)],
        compiler_params=params(6),
        cost_estimate=COST,
        name="pick",
    )(ids, *metas, *xs, *cs)
    return out[:kinds], out[kinds:]


def gate_up_kernel(y_ref, *refs, parts, ny, tpy, shift):
    rows_in, (wg_ref, wu_ref) = refs[:parts], refs[parts : parts + 2]
    gate_ref, up_ref, *splits = refs[parts + 2 : parts + 4 + ny]
    joined = refs[parts + 4 + ny]
    cap, tile = rows_in[0].shape
    j = pl.program_id(0)
    for k in range(parts):
        joined[k * cap : (k + 1) * cap, :] = rows_in[k][...]
    x = joined[...]
    gate = jnp.dot(x, wg_ref[0], preferred_element_type=F32)
    up = jnp.dot(x, wu_ref[0], preferred_element_type=F32)

    @pl.when(j == 0)
    def _():
        gate_ref[...] = gate
        up_ref[...] = up

    @pl.when(j > 0)
    def _():
        gate_ref[...] += gate
        up_ref[...] += up

    for w in range(ny):
        begin = shift if w < ny - 1 else 0
        for t in range(tpy):

            @pl.when(j == w * tpy + t)
            def _(w=w, at=begin + t * tile):
                splits[w][:, at : at + tile] = x


def gate_up(y, parts, w_gate, w_up, cap, ny, shift):
    width = parts[0].shape[1]
    ff = w_gate.shape[2]
    rows = cap * len(parts)
    tile = width // 4
    tpy = 4 // ny

    def col(j, y_ref):
        return (y_ref[0] ^ ((j // tpy + 1) % ny)) * tpy + j % tpy

    sizes = [shift + width // ny] * (ny - 1) + [width // ny]
    return pl.pallas_call(
        functools.partial(gate_up_kernel, parts=len(parts), ny=ny, tpy=tpy, shift=shift),
        grid_spec=pltpu.PrefetchScalarGridSpec(
            num_scalar_prefetch=1,
            grid=(4,),
            in_specs=[pl.BlockSpec((cap, tile), lambda j, y_ref: (0, col(j, y_ref)))] * len(parts)
            + [pl.BlockSpec((1, tile, ff), lambda j, y_ref: (0, col(j, y_ref), 0))] * 2,
            out_specs=[pl.BlockSpec((rows, ff), lambda j, y_ref: (0, 0))] * 2
            + [pl.BlockSpec((rows, s), lambda j, y_ref: (0, 0)) for s in sizes],
            scratch_shapes=[pltpu.VMEM((rows, tile), BF16)],
        ),
        out_shape=[jax.ShapeDtypeStruct((rows, ff), F32)] * 2
        + [jax.ShapeDtypeStruct((rows, s), BF16) for s in sizes],
        compiler_params=params(12),
        cost_estimate=COST,
        name="gate_up",
    )(y, *parts, w_gate, w_up)


def back_kernel(*refs, parts, aliased, n_d):
    rows_in, (wd_ref, gate_ref, up_ref) = refs[:parts], refs[parts : parts + 3]
    outs = refs[parts + 3 + aliased :]
    d_refs, (hid_ref, cot_ref, acc) = outs[:n_d], outs[n_d:]
    cap = rows_in[0].shape[0]
    ff = gate_ref.shape[1]
    j = pl.program_id(0)
    for k in range(parts):
        cot_ref[k * cap : (k + 1) * cap, :] = rows_in[k][...]
    dh = lax.dot_general(
        cot_ref[...], wd_ref[0], (((1,), (1,)), ((), ())), preferred_element_type=F32
    )

    @pl.when(j == 0)
    def _():
        acc[...] = dh

    @pl.when(j > 0)
    def _():
        acc[...] += dh

    @pl.when(j == pl.num_programs(0) - 1)
    def _():
        gate, up, total = gate_ref[...], up_ref[...], acc[...]
        sig = jax.nn.sigmoid(gate)
        act = gate * sig
        hid_ref[...] = (act * up).astype(BF16)
        d_gate = (total * up * sig * (1.0 + gate * (1.0 - sig))).astype(BF16)
        d_up = (total * act).astype(BF16)
        for d_ref in d_refs:
            d_ref[:, :ff] = d_gate
            d_ref[:, ff:] = d_up


def back(parts, at, w_down, gate, up, behind, joined, slot, cap):
    width = parts[0].shape[1]
    rows, ff = gate.shape
    tile = width // 4
    n = len(parts)
    n_d = max(len(behind), 1)
    d_shapes = [b.shape for b in behind] or [(rows, 2 * ff)]
    first = 0 if behind else 1
    aliased = [*behind, *joined]
    return pl.pallas_call(
        functools.partial(back_kernel, parts=n, aliased=len(aliased), n_d=n_d),
        grid=(4,),
        in_specs=[pl.BlockSpec((cap, tile), lambda j: (0, j))]
        + [pl.BlockSpec((cap, tile), lambda j: (at, j))] * (n - 1)
        + [pl.BlockSpec((1, ff, tile), lambda j: (0, 0, j))]
        + [pl.BlockSpec((rows, ff), lambda j: (0, 0))] * 2
        + [pl.BlockSpec(memory_space=pl.ANY)] * len(aliased),
        out_specs=[pl.BlockSpec((rows, 2 * ff), lambda j: (0, 0))] * n_d
        + [
            pl.BlockSpec((rows, ff), lambda j: (slot, 0)),
            pl.BlockSpec((rows, tile), lambda j: (slot, j)),
        ],
        out_shape=[jax.ShapeDtypeStruct(s, BF16) for s in d_shapes]
        + [
            jax.ShapeDtypeStruct((NZ * rows, ff), BF16),
            jax.ShapeDtypeStruct((NZ * rows, width), BF16),
        ],
        scratch_shapes=[pltpu.VMEM((rows, ff), F32)],
        input_output_aliases={n + 3 + i: first + i for i in range(len(aliased))},
        compiler_params=params(11),
        cost_estimate=COST,
        name="back",
    )(*parts, w_down, gate, up, *aliased)


def down_kernel(s_ref, hid_ref, cot_ref, *refs, chunks, outs):
    ins, out_refs, acc = refs[: sum(chunks)], refs[-1 - outs : -1], refs[-1]
    j, steps = pl.program_id(0), pl.num_programs(0)
    acc[...] = contract_rows(hid_ref[...], cot_ref[...])
    i = 0
    for count in chunks:
        for w in range(count):

            @pl.when(j * count // steps == w)
            def _(ref=ins[i]):
                acc[...] += ref[...].astype(F32)

            i += 1
    for w in range(outs):

        @pl.when(j * outs // steps == w)
        def _(w=w):
            out_refs[w][...] = acc[...].astype(BF16)


def down_part(index, hidden, cot, n, arrived=(), outs=1):
    k, width = cot.shape
    steps = 4
    tile = width // steps

    def chunk(w, count):
        per = steps // count
        return pl.BlockSpec(
            (n, tile), lambda j, s_ref: (0, jnp.minimum(jnp.maximum(j - w * per, 0), per - 1))
        )

    return pl.pallas_call(
        functools.partial(down_kernel, chunks=tuple(len(a) for a in arrived), outs=outs),
        grid_spec=pltpu.PrefetchScalarGridSpec(
            num_scalar_prefetch=1,
            grid=(steps,),
            in_specs=[
                pl.BlockSpec((k, n), lambda j, s_ref: (0, s_ref[0])),
                pl.BlockSpec((k, tile), lambda j, s_ref: (0, j)),
            ]
            + [chunk(w, len(a)) for a in arrived for w in range(len(a))],
            out_specs=[chunk(w, outs) for w in range(outs)],
            scratch_shapes=[pltpu.VMEM((n, tile), F32)],
        ),
        out_shape=[jax.ShapeDtypeStruct((n, width // outs), BF16)] * outs,
        compiler_params=params(9),
        cost_estimate=COST,
        name="down_part",
    )(index, hidden, cot, *[piece for a in arrived for piece in a])


def both_kernel(c_ref, *refs, pieces, add):
    xs, ds = refs[:pieces], refs[pieces : 2 * pieces]
    rest = refs[2 * pieces :]
    got, outs, (left, right, acc) = rest[:add], rest[add:-3], rest[-3:]
    rows = xs[0].shape[0]
    j = pl.program_id(0)

    @pl.when(j == 0)
    def _():
        for i in range(pieces):
            left[i * rows : (i + 1) * rows, :] = xs[i][...]

    for i in range(pieces):
        right[i * rows : (i + 1) * rows, :] = ds[i][...]
    acc[...] = contract_rows(left[...], right[...])
    for w, out in enumerate(outs):

        @pl.when(j * len(outs) // pl.num_programs(0) == w)
        def _(w=w, out=out):
            total = acc[...]
            if add:
                total = total + got[w][...].astype(F32)
            out[...] = total.astype(BF16)


def both_part(index, xs, ds, n, ff2, half, arrived=()):
    rows = ds[0].shape[0]
    steps, tile = 4, ff2 // 4
    m = len(xs)
    add = len(arrived)
    outs = 2
    per = steps // outs
    pair = [
        pl.BlockSpec(
            (n, tile),
            lambda j, c_ref, w=w: (0, jnp.minimum(jnp.maximum(j - w * per, 0), per - 1)),
        )
        for w in range(outs)
    ]

    def x_spec(value):
        begin = value.shape[1] - half
        if begin == 0:
            return pl.BlockSpec((rows, n), lambda j, c_ref: (0, c_ref[0]))
        return pl.BlockSpec(
            (pl.Element(rows), pl.Element(n)),
            lambda j, c_ref: (0, pl.multiple_of(begin + c_ref[0] * n, LANES)),
        )

    return pl.pallas_call(
        functools.partial(both_kernel, pieces=m, add=add),
        grid_spec=pltpu.PrefetchScalarGridSpec(
            num_scalar_prefetch=1,
            grid=(steps,),
            in_specs=[x_spec(v) for v in xs]
            + [pl.BlockSpec((rows, tile), lambda j, c_ref: (0, j))] * m
            + pair[:add],
            out_specs=pair,
            scratch_shapes=[
                pltpu.VMEM((m * rows, n), BF16),
                pltpu.VMEM((m * rows, tile), BF16),
                pltpu.VMEM((n, tile), F32),
            ],
        ),
        out_shape=[jax.ShapeDtypeStruct((n, ff2 // outs), BF16)] * outs,
        compiler_params=params(22),
        cost_estimate=COST,
        name="both_part",
    )(index, *xs, *ds, *arrived)


def make_per_device(n_dp, n_expert):
    nx = n_expert // NZ
    ny = n_dp // NC

    def ex(z, x):
        return z * nx + x

    def zpairs(moves):
        return [(ex(a, x), ex(b, x)) for a, b in moves for x in range(nx)]

    ends_first = zpairs([(0, 1), (1, 0), (2, 3), (3, 2)])
    middle = zpairs([(1, 2), (2, 1)])
    outward = zpairs([(1, 0), (2, 3)])

    def hop1(block):
        return lax.ppermute(block, "expert", ends_first), lax.ppermute(block, "expert", middle)

    def hop2(a, c_mid):
        return lax.ppermute(c_mid, "expert", outward), lax.ppermute(a, "expert", middle)

    def hop3(b_mid):
        return lax.ppermute(b_mid, "expert", outward)

    def over_x(sends):
        out = []
        for k in range(1, nx):
            pairs = [(ex(z, x), ex(z, x ^ k)) for z in range(NZ) for x in range(nx)]
            out.append(lax.ppermute(sends[k - 1], "expert", pairs))
        return out

    core_pairs = [(y * NC + c, y * NC + 1 - c) for y in range(ny) for c in range(NC)]

    def over_core(value):
        return lax.ppermute(value, "dp", core_pairs)

    def over_y(value, k):
        return lax.ppermute(
            value, "dp", [(y * NC + c, (y ^ k) * NC + c) for y in range(ny) for c in range(NC)]
        )

    def per_device(tokens, cotangent, routes, route_gain, expert_alive, w_gate, w_up, w_down):
        tok_count, width = tokens.shape
        top = routes.shape[1]
        experts_all = expert_alive.shape[0]
        cap = tok_count * top * 5 // (4 * experts_all)
        ff = w_gate.shape[2]
        half = width // ny
        me = lax.axis_index("expert")
        z, x = me // nx, me % nx
        d = lax.axis_index("dp")
        y_arr = (d // NC).astype(jnp.int32)[None]
        c_arr = (d % NC).astype(jnp.int32)[None]

        own = pack(tokens, cotangent, routes, route_gain)
        a, c_mid = hop1(own)

        own_ids = z * nx + (x ^ jnp.arange(nx, dtype=jnp.int32))
        alive = jnp.sum(
            jnp.where(
                own_ids[:, None] == jnp.arange(experts_all)[None, :], expert_alive[None, :], 0
            ),
            axis=1,
        )
        ids = jnp.stack([own_ids, alive.astype(jnp.int32)])

        def pick(metas, xs=(), cs=()):
            own, sends = pick_rows(ids, metas, xs, cs, nx, cap, top, width, tok_count)
            return own, over_x(sends)

        x_own, x_got, d_own, d_got, joined = [], [], [], [], []

        def forward(parts, shift):
            gate, up, *splits = gate_up(y_arr, parts, w_gate, w_up, cap, ny, shift)
            x_own.append(splits[-1])
            return gate, up, splits[:-1]

        def backward(parts, at, gate, up, behind, slot):
            out = back(parts, at, w_down, gate, up, behind, joined, slot, cap)
            joined[:] = out[-2:]
            return out[:-2]

        def exchange(filled):
            d_own.append(filled[0])
            got = [over_y(f, k) for k, f in zip(range(1, ny), filled)]
            x_got.append(got)
            d_got.append(got)
            return got

        (x0,), s0 = pick([own], [own])
        (c0,), t0 = pick([own], (), [after(own, x0)])
        s0 = after(s0, c0)
        g0, u0, b0 = forward([x0, *s0], 2 * ff)
        f0 = backward([c0, *t0], 0, g0, u0, b0, 0)
        y0 = exchange(f0)
        a, c_mid = after((a, c_mid), f0)
        b_end, b_mid = hop2(a, c_mid)
        (x1, c1), s1 = pick([a], [a], [a])
        s1 = after(s1, y0)
        g1, u1, b1 = forward([x1, *s1], 2 * ff)
        f1 = backward([c1, *s1], 1, g1, u1, b1, 1)
        y1 = exchange(f1)
        xc_end = hop3(b_mid[:tok_count])
        cc_end = hop3(b_mid[tok_count:, :width])
        b_end, b_mid = after((b_end, b_mid), f1)
        (x2,), s2 = pick([b_end, b_mid], [b_end, b_mid])
        (c2,), t2 = pick([b_end, b_mid], (), after([b_end, b_mid], x2))
        s2 = after(s2, c2)
        g2, u2, b2 = forward([x2, *s2], 2 * ff)
        c_mid, xc_end = after((c_mid, xc_end), g2, y1)
        (x3,), s3 = pick([c_mid, xc_end], [c_mid, xc_end])
        t2 = after(t2, x3)
        f2 = backward([c2, *t2], 0, g2, u2, b2, 2)
        y2 = exchange(f2)
        s3 = after(s3, f2)
        g3, u3, b3 = forward([x3, *s3], 0)
        x_got.append([over_y(b, k) for k, b in zip(range(1, ny), b3)])
        cc_end = after(cc_end, g3)
        (c3,), t3 = pick([c_mid, xc_end], (), [c_mid, cc_end])
        t3 = after(t3, c3, y2, x_got[-1])
        (f3,) = backward([c3, *t3], 0, g3, u3, [], 3)
        d_own.append(f3)
        d_got.append([over_y(f3, k) for k in range(1, ny)])

        hidden, cot_rows = joined
        n = ff // n_dp

        def to_core(yy):
            return over_core(down_part(yy * NC + (1 - c_arr), hidden, cot_rows, n)[0])

        landed, totals = [], []
        for k in range(1, ny):
            recv = to_core(y_arr ^ k)
            first, second = down_part(
                (y_arr ^ k) * NC + c_arr, hidden, cot_rows, n, [[recv]], outs=2
            )
            first = over_y(first, k)
            landed.append([first, over_y(after(second, first), k)])
            totals.append(second)

        m = half // NC
        xs, ds = [], []
        for s in range(NZ):
            xs += [x_own[s], *x_got[s]]
            ds += [d_own[s], *d_got[s]]
        if m % LANES == 0:
            ds[0] = after(ds[0], totals)
            recv = [over_core(v) for v in both_part(1 - c_arr, xs, ds, m, 2 * ff, half)]
            own_recv = to_core(y_arr)
            grad_gate, grad_up = both_part(c_arr, xs, ds, m, 2 * ff, half, recv)
        else:
            x_all = jnp.concatenate([v[:, v.shape[1] - half :] for v in xs], axis=0)
            d_all = jnp.concatenate([v[:, : 2 * ff] for v in ds], axis=0)

            def part(c):
                return contract_rows(lax.dynamic_slice_in_dim(x_all, c * m, m, 1), d_all)

            recv = over_core(part(1 - c_arr[0]).astype(BF16))
            own_recv = to_core(y_arr)
            total = (part(c_arr[0]) + recv.astype(F32)).astype(BF16)
            grad_gate, grad_up = total[:, :ff], total[:, ff:]

        (grad_down,) = down_part(
            y_arr * NC + c_arr, hidden, cot_rows, n, [[own_recv], *landed]
        )
        return grad_gate[None], grad_up[None], grad_down[None]

    return per_device


def solution(mesh):
    in_specs = (
        P(("dp", "expert"), None),
        P(("dp", "expert"), None),
        P(("dp", "expert"), None),
        P(("dp", "expert"), None),
        P(),
        P("expert", None, None),
        P("expert", None, None),
        P("expert", None, None),
    )
    out_specs = (P("expert", "dp", None), P("expert", "dp", None), P("expert", "dp", None))
    per_device = make_per_device(mesh.shape["dp"], mesh.shape["expert"])
    return jax.shard_map(
        per_device, mesh=mesh, in_specs=in_specs, out_specs=out_specs, check_vma=False
    )
```

time: 352 us -> 252 us (0.72)
  waiting for transfers between devices: 210 us -> 93.6 us
  Pallas kernels: 0 us -> 102 us
  matrix products: 74.5 us -> 0 us
  other arithmetic: 12.2 us -> 0.21 us
  local copies, waits for them, and re-layouts: 19.1 us -> 24.1 us
  starting transfers between devices: 34.4 us -> 29.8 us
    ppermute x32 -> x24, waiting for transfers between devices: 210 us -> 93.6 us  [the longest x7 49.5 us: over_y(): lax.ppermute(value, 'dp', [(y * NC + c, (y ^ k) * NC + c) for y in range(...]
    pallas_call x0 -> x22, Pallas kernels: none -> 102 us  [the longest x7 24.7 us: pick_rows(): pl.pallas_call(functools.partial(pick_kernel, nx=nx, top=top, n_meta=len(...]
    dot_general x27 -> x0, matrix products: 74.5 us -> none  [the longest x12 42.7 us: contract_rows(): lax.dot_general(left, right, (((0,), (0,)), ((), ())), preferred_element_...]
    unnamed x48 -> x90, local copies, waits for them, and re-layouts: 11.6 us -> 24 us
    broadcast_in_dim x2 -> x0, other arithmetic: 8.24 us -> none  [reduce_over_dp(): return total.astype(jnp.bfloat16)[None]]
    slice x11 -> x2, local copies, waits for them, and re-layouts: 6.99 us -> 0.13 us  [the longest x1 0.07 us: per_device(): xc_end = hop3(b_mid[:tok_count])]
    ppermute x32 -> x24, starting transfers between devices: 34.4 us -> 29.8 us  [the longest x7 8.89 us: over_y(): lax.ppermute(value, 'dp', [(y * NC + c, (y ^ k) * NC + c) for y in range(...]
  transfers between devices with their start and end apart: 32 -> 24, of which waited for: 14 -> 14; matrix products, arithmetic and copies ran while one was open for 23% -> 0% of each run, Pallas kernels for 0% -> 35%
where the time goes in v2:
time: 252 us; the launch traced here: 251 us
  Pallas kernels  102 us (40%)
  waiting for transfers between devices  93.6 us (37%)
  starting transfers between devices  29.8 us (12%)
  local copies, waits for them, and re-layouts  24.1 us (10%)
    ppermute x7, waiting for transfers between devices, over_y(): lax.ppermute(value, 'dp', [(y * NC + c, (y ^ k) * NC + c) for y in range(...  49.5 us
    ppermute x7, waiting for transfers between devices, over_x(): out.append(lax.ppermute(sends[k - 1], 'expert', pairs))  40.5 us
    pallas_call x7, Pallas kernels, pick_rows(): pl.pallas_call(functools.partial(pick_kernel, nx=nx, top=top, n_meta=len(...  24.7 us
    unnamed x90, local copies, waits for them, and re-layouts  24 us
    pallas_call x4, Pallas kernels, gate_up(): pl.pallas_call(functools.partial(gate_up_kernel, parts=len(parts), ny=ny,...  21 us
    pallas_call x4, Pallas kernels, back(): pl.pallas_call(functools.partial(back_kernel, parts=n, aliased=len(aliase...  20.5 us
    pallas_call x2, Pallas kernels, both_part(): pl.pallas_call(functools.partial(both_kernel, pieces=m, add=add), grid_sp...  19.4 us
    pallas_call x4, Pallas kernels, down_part(): pl.pallas_call(functools.partial(down_kernel, chunks=tuple((len(a) for a...  15.1 us
  transfers between devices with their start and end apart: 24, of which 14 were waited for; matrix products, arithmetic and copies ran while one was open for 0% of the time, Pallas kernels for 35%

profile of v2, /device:TPU:0, one launch (start us, length us, event | category | flops | bytes accessed | tf_op | source)
XLA Modules:
  0.0 251.1 jit_solution(3754393600242488090)
XLA Ops:
  7.8 4.7 %collective-permute-start.3 = (bf16[256,3712]{1,0:T(8,128)(2,1)}, bf16[256,3712]{1,0:T(8,128)(2,1)}, u32[]{:S(2)}, u32[]{:S(2)}) collective-permute-start(bf16[256,3712]{1,0:T(8,128)(2,1)} %pack.1.refs_0_.refs_1_), channel_id=1, source_target_pairs={{0,2},{1,3},{2,0},{3,1},{4,6},{5,7},{6,4},{7,5},{8,10},{9,11},{10,... | collective-permute-start | bytes 5701640 | tf_op jit(solution)/shard_map/ppermute | solution.py:413
  12.7 4.2 %pick.7 = (bf16[80,3584]{1,0:T(8,128)(2,1)S(1)}, bf16[80,3584]{1,0:T(8,128)(2,1)}) custom-call(s32[2,2]{1,0:T(2,128)S(1)} %pad_add_fusion.ids_ref, bf16[256,3712]{1,0:T(8,128)(2,1)} %pack.1.refs_0_.refs_1_, bf16[256,3712]{1,0:T(8,128)(2,1)} %pack.1.refs_0_.refs_1_), custom_call_target="tpu_custom_call" | custom-call | flops 1000 | bytes 1000 | tf_op jit(solution)/shard_map/pick/pallas_call | solution.py:123
  19.2 4.1 %pick.8 = (bf16[80,3584]{1,0:T(8,128)(2,1)S(1)}, bf16[80,3584]{1,0:T(8,128)(2,1)}) custom-call(s32[2,2]{1,0:T(2,128)S(1)} %pad_add_fusion.ids_ref, bf16[256,3712]{1,0:T(8,128)(2,1)} %pack.1.refs_0_.refs_1_, bf16[256,3712]{1,0:T(8,128)(2,1)} %pack.1.refs_0_.refs_1_), custom_call_target="tpu_custom_call" | custom-call | flops 1000 | bytes 1000 | tf_op jit(solution)/shard_map/pick/pallas_call | solution.py:123
  24.6 9.3 %collective-permute-done.refs_1_ = bf16[80,3584]{1,0:T(8,128)(2,1)} collective-permute-done((bf16[80,3584]{1,0:T(8,128)(2,1)}, bf16[80,3584]{1,0:T(8,128)(2,1)}, u32[]{:S(2)}, u32[]{:S(2)}) %collective-permute-start) | collective-permute-done | bytes 573472 | tf_op jit(solution)/shard_map/ppermute | solution.py:425
  33.9 3.1 %copy-done.3 = bf16[1,3584,1024]{2,1,0:T(8,128)(2,1)S(1)} copy-done((bf16[1,3584,1024]{2,1,0:T(8,128)(2,1)S(1)}, bf16[1,3584,1024]{2,1,0:T(8,128)(2,1)}, u32[]{:S(2)}) %copy-start.3) | copy-done | bytes 7340056
  37.0 3.1 %copy-done.4 = bf16[1,3584,1024]{2,1,0:T(8,128)(2,1)S(1)} copy-done((bf16[1,3584,1024]{2,1,0:T(8,128)(2,1)S(1)}, bf16[1,3584,1024]{2,1,0:T(8,128)(2,1)}, u32[]{:S(2)}) %copy-start.4) | copy-done | bytes 7340056
  41.1 5.9 %gate_up.4 = (f32[160,1024]{1,0:T(8,128)S(1)}, f32[160,1024]{1,0:T(8,128)S(1)}, bf16[160,3840]{1,0:T(8,128)(2,1)S(1)}, bf16[160,1792]{1,0:T(8,128)(2,1)S(1)}) custom-call(s32[1]{0:T(128)} %bitcast.1.y_ref, bf16[80,3584]{1,0:T(8,128)(2,1)S(1)} %copy-done.29, bf16[80,3584]{1,0:T(8,128)(2,1)} %collective-permute-done.refs_1_, ...), custom_call_target="tpu_custom_call" | custom-call | flops 1000 | bytes 1000 | tf_op jit(solution)/shard_map/gate_up/pallas_call | solution.py:188
  48.0 5.7 %back.4 = (bf16[160,3840]{1,0:T(8,128)(2,1)S(1)}, bf16[640,1024]{1,0:T(8,128)(2,1)S(1)}, bf16[640,3584]{1,0:T(8,128)(2,1)S(1)}) custom-call(bf16[80,3584]{1,0:T(8,128)(2,1)S(1)} %copy-done.31, bf16[80,3584]{1,0:T(8,128)(2,1)} %collective-permute-done.1.refs_1_, bf16[1,1024,3584]{2,1,0:T(8,128)(2,1)S(1)} %bitcast.15, ...), custom_call_target="tpu_custom_call", output_to_operand_aliasing={{0}: (5, {})} | custom-call | flops 1000 | bytes 1000 | tf_op jit(solution)/shard_map/back/pallas_call | solution.py:250
  57.6 3.7 %pick.9 = (bf16[80,3584]{1,0:T(8,128)(2,1)S(1)}, bf16[80,3584]{1,0:T(8,128)(2,1)S(1)}, bf16[160,3584]{1,0:T(8,128)(2,1)S(1)}) custom-call(s32[2,2]{1,0:T(2,128)S(1)} %pad_add_fusion.ids_ref, bf16[256,3712]{1,0:T(8,128)(2,1)} %collective-permute-done.3.refs_0_.refs_1_.refs_2_, bf16[256,3712]{1,0:T(8,128)(2,1)} %collective-permute-done.3.refs_0_.refs_1_.refs_2_, ...), custom_call_target="tpu_custom_call" | custom-call | flops 1000 | bytes 1000 | tf_op jit(solution)/shard_map/pick/pallas_call | solution.py:123
  62.9 21.1 %collective-permute-done.2.refs_1_.refs_9_ = bf16[160,3840]{1,0:T(8,128)(2,1)S(1)} collective-permute-done((bf16[160,3840]{1,0:T(8,128)(2,1)S(1)}, bf16[160,3840]{1,0:T(8,128)(2,1)S(1)}, u32[]{:S(2)}, u32[]{:S(2)}) %collective-permute-start.2) | collective-permute-done | bytes 1228832 | tf_op jit(solution)/shard_map/ppermute | solution.py:434
  87.3 4.5 %gate_up.5 = (f32[160,1024]{1,0:T(8,128)S(1)}, f32[160,1024]{1,0:T(8,128)S(1)}, bf16[160,3840]{1,0:T(8,128)(2,1)S(1)}, bf16[160,1792]{1,0:T(8,128)(2,1)S(1)}) custom-call(s32[1]{0:T(128)} %bitcast.1.y_ref, bf16[80,3584]{1,0:T(8,128)(2,1)S(1)} %get-tuple-element.82.refs_0_, bf16[160,3584]{1,0:T(8,128)(2,1)S(1)} %collective-permute-done.5.refs_1_, ...), custom_call_target="tpu_custom_call" | custom-call | flops 1000 | bytes 1000 | tf_op jit(solution)/shard_map/gate_up/pallas_call | solution.py:188
  91.8 4.5 %back.5 = (bf16[160,3840]{1,0:T(8,128)(2,1)S(1)}, bf16[640,1024]{1,0:T(8,128)(2,1)S(1)}, bf16[640,3584]{1,0:T(8,128)(2,1)S(1)}) custom-call(bf16[80,3584]{1,0:T(8,128)(2,1)S(1)} %get-tuple-element.86.refs_0_, bf16[160,3584]{1,0:T(8,128)(2,1)S(1)} %collective-permute-done.5.refs_1_, ...), custom_call_target="tpu_custom_call", output_to_operand_aliasing={{0}: (5, {}), {1}: (6, {}), {2}: (7, {})} | custom-call | flops 1000 | bytes 1000 | tf_op jit(solution)/shard_map/back/pallas_call | solution.py:250
  107.9 9.9 %collective-permute-done.9.refs_1_ = bf16[80,3584]{1,0:T(8,128)(2,1)S(1)} collective-permute-done((bf16[80,3584]{1,0:T(8,128)(2,1)S(1)}, bf16[80,3584]{1,0:T(8,128)(2,1)S(1)}, u32[]{:S(2)}, u32[]{:S(2)}) %collective-permute-start.9) | collective-permute-done | bytes 573472 | tf_op jit(solution)/shard_map/ppermute | solution.py:425
  117.8 5.4 %gate_up.6 = (f32[160,1024]{1,0:T(8,128)S(1)}, f32[160,1024]{1,0:T(8,128)S(1)}, bf16[160,3840]{1,0:T(8,128)(2,1)}, bf16[160,1792]{1,0:T(8,128)(2,1)S(1)}) custom-call(s32[1]{0:T(128)} %bitcast.1.y_ref, bf16[80,3584]{1,0:T(8,128)(2,1)S(1)} %get-tuple-element.96.refs_0_, bf16[80,3584]{1,0:T(8,128)(2,1)S(1)} %collective-permute-done.9.refs_1_, ...), custom_call_target="tpu_custom_call" | custom-call | flops 1000 | bytes 1000 | tf_op jit(solution)/shard_map/gate_up/pallas_call | solution.py:188
  123.2 3.4 %pick.12 = (bf16[80,3584]{1,0:T(8,128)(2,1)S(1)}, bf16[80,3584]{1,0:T(8,128)(2,1)S(1)}) custom-call(s32[2,2]{1,0:T(2,128)S(1)} %pad_add_fusion.ids_ref, bf16[256,3712]{1,0:T(8,128)(2,1)} %collective-permute-done.4.refs_0_.refs_2_, bf16[128,3712]{1,0:T(8,128)(2,1)S(1)} %collective-permute-done.11.refs_1_.refs_3_, ...), custom_call_target="tpu_custom_call" | custom-call | flops 1000 | bytes 1000 | tf_op jit(solution)/shard_map/pick/pallas_call | solution.py:123
  126.8 5.3 %back.6 = (bf16[160,3840]{1,0:T(8,128)(2,1)}, bf16[640,1024]{1,0:T(8,128)(2,1)S(1)}, bf16[640,3584]{1,0:T(8,128)(2,1)S(1)}) custom-call(bf16[80,3584]{1,0:T(8,128)(2,1)S(1)} %get-tuple-element.100.refs_0_, bf16[80,3584]{1,0:T(8,128)(2,1)S(1)} %collective-permute-done.10.refs_1_, ...), custom_call_target="tpu_custom_call", output_to_operand_aliasing={{0}: (5, {}), {1}: (6, {}), {2}: (7, {})} | custom-call | flops 1000 | bytes 1000 | tf_op jit(solution)/shard_map/back/pallas_call | solution.py:250
  135.1 10.0 %collective-permute-done.13.refs_1_ = bf16[80,3584]{1,0:T(8,128)(2,1)S(1)} collective-permute-done((bf16[80,3584]{1,0:T(8,128)(2,1)S(1)}, bf16[80,3584]{1,0:T(8,128)(2,1)S(1)}, u32[]{:S(2)}, u32[]{:S(2)}) %collective-permute-start.13) | collective-permute-done | bytes 573472 | tf_op jit(solution)/shard_map/ppermute | solution.py:425
  145.1 5.3 %gate_up.7 = (f32[160,1024]{1,0:T(8,128)S(1)}, f32[160,1024]{1,0:T(8,128)S(1)}, bf16[160,1792]{1,0:T(8,128)(2,1)}, bf16[160,1792]{1,0:T(8,128)(2,1)S(1)}) custom-call(s32[1]{0:T(128)} %bitcast.1.y_ref, bf16[80,3584]{1,0:T(8,128)(2,1)S(1)} %get-tuple-element.107.refs_0_, bf16[80,3584]{1,0:T(8,128)(2,1)S(1)} %collective-permute-done.13.refs_1_, ...), custom_call_target="tpu_custom_call" | custom-call | flops 1000 | bytes 1000 | tf_op jit(solution)/shard_map/gate_up/pallas_call | solution.py:188
  150.4 4.6 %pick.13 = (bf16[80,3584]{1,0:T(8,128)(2,1)S(1)}, bf16[80,3584]{1,0:T(8,128)(2,1)}) custom-call(s32[2,2]{1,0:T(2,128)S(1)} %pad_add_fusion.ids_ref, bf16[256,3712]{1,0:T(8,128)(2,1)} %collective-permute-done.4.refs_0_.refs_2_, bf16[128,3712]{1,0:T(8,128)(2,1)S(1)} %collective-permute-done.11.refs_1_.refs_3_, ...), custom_call_target="tpu_custom_call" | custom-call | flops 1000 | bytes 1000 | tf_op jit(solution)/shard_map/pick/pallas_call | solution.py:123
  157.9 8.9 %collective-permute-done.16.refs_1_ = bf16[80,3584]{1,0:T(8,128)(2,1)} collective-permute-done((bf16[80,3584]{1,0:T(8,128)(2,1)}, bf16[80,3584]{1,0:T(8,128)(2,1)}, u32[]{:S(2)}, u32[]{:S(2)}) %collective-permute-start.16) | collective-permute-done | bytes 573472 | tf_op jit(solution)/shard_map/ppermute | solution.py:425
  166.7 3.8 %collective-permute-done.14.refs_7_ = bf16[160,1792]{1,0:T(8,128)(2,1)} collective-permute-done((bf16[160,1792]{1,0:T(8,128)(2,1)}, bf16[160,1792]{1,0:T(8,128)(2,1)}, u32[]{:S(2)}, u32[]{:S(2)}) %collective-permute-start.14) | collective-permute-done | bytes 573472 | tf_op jit(solution)/shard_map/ppermute | solution.py:434
  172.8 3.1 %copy-done.5 = bf16[1,1024,3584]{2,1,0:T(8,128)(2,1)S(1)} copy-done((bf16[1,1024,3584]{2,1,0:T(8,128)(2,1)S(1)}, bf16[1,1024,3584]{2,1,0:T(8,128)(2,1)}, u32[]{:S(2)}) %copy-start.5) | copy-done | bytes 7340056
  179.2 5.0 %back.7 = (bf16[160,2048]{1,0:T(8,128)(2,1)S(1)}, bf16[640,1024]{1,0:T(8,128)(2,1)S(1)}, bf16[640,3584]{1,0:T(8,128)(2,1)S(1)}) custom-call(bf16[80,3584]{1,0:T(8,128)(2,1)S(1)} %copy-done.33, bf16[80,3584]{1,0:T(8,128)(2,1)} %collective-permute-done.16.refs_1_, bf16[1,1024,3584]{2,1,0:T(8,128)(2,1)S(1)} %copy-done.5, ...), custom_call_target="tpu_custom_call", output_to_operand_aliasing={{1}: (5, {}), {2}: (6, {})} | custom-call | flops 1000 | bytes 1000 | tf_op jit(solution)/shard_map/back/pallas_call | solution.py:250
  184.1 3.2 %down_part.4 = bf16[256,3584]{1,0:T(8,128)(2,1)S(1)} custom-call(s32[1]{0:T(128)S(6)} %add.49.s_ref, bf16[640,1024]{1,0:T(8,128)(2,1)S(1)} %get-tuple-element.126.hid_ref, bf16[640,3584]{1,0:T(8,128)(2,1)S(1)} %get-tuple-element.127.cot_ref), custom_call_target="tpu_custom_call" | custom-call | flops 1000 | bytes 1000 | tf_op jit(solution)/shard_map/down_part/pallas_call | solution.py:307
  191.2 3.8 %down_part.5 = (bf16[256,1792]{1,0:T(8,128)(2,1)S(1)}, bf16[256,1792]{1,0:T(8,128)(2,1)S(1)}) custom-call(s32[1]{0:T(128)S(6)} %add.48.s_ref, bf16[640,1024]{1,0:T(8,128)(2,1)S(1)} %get-tuple-element.126.hid_ref, bf16[640,3584]{1,0:T(8,128)(2,1)S(1)} %get-tuple-element.127.cot_ref, bf16[256,3584]{1,0:T(8,128)(2,1)S(1)} %collective-permute-done.17.refs_0_), custom_call_target="tpu_custom_call" | custom-call | flops 1000 | bytes 1000 | tf_op jit(solution)/shard_map/down_part/pallas_call | solution.py:307
  196.6 8.4 %collective-permute-done.18.refs_15_ = bf16[160,2048]{1,0:T(8,128)(2,1)S(1)} collective-permute-done((bf16[160,2048]{1,0:T(8,128)(2,1)S(1)}, bf16[160,2048]{1,0:T(8,128)(2,1)S(1)}, u32[]{:S(2)}, u32[]{:S(2)}) %collective-permute-start.18) | collective-permute-done | bytes 655392 | tf_op jit(solution)/shard_map/ppermute | solution.py:434
  205.1 9.1 %both_part.2 = (bf16[896,1024]{1,0:T(8,128)(2,1)S(1)}, bf16[896,1024]{1,0:T(8,128)(2,1)S(1)}) custom-call(s32[1]{0:T(128)S(6)} %sub.14.c_ref, bf16[160,1792]{1,0:T(8,128)(2,1)S(1)} %copy-done.17, bf16[160,3840]{1,0:T(8,128)(2,1)S(1)} %copy-done.9, bf16[160,1792]{1,0:T(8,128)(2,1)S(1)} %copy-done.19, bf16[160,3840]{1,0:T(8,128)(2,1)S(1)} %copy-done.11, ...), custom_call_target="tpu_custom_call" | custom-call | flops 1000 | bytes 1000 | tf_op jit(solution)/shard_map/both_part/pallas_call | solution.py:376
  214.8 3.2 %down_part.6 = bf16[256,3584]{1,0:T(8,128)(2,1)S(1)} custom-call(s32[1]{0:T(128)S(6)} %add.51.s_ref, bf16[640,1024]{1,0:T(8,128)(2,1)S(1)} %get-tuple-element.126.hid_ref, bf16[640,3584]{1,0:T(8,128)(2,1)S(1)} %bitcast.9), custom_call_target="tpu_custom_call" | custom-call | flops 1000 | bytes 1000 | tf_op jit(solution)/shard_map/down_part/pallas_call | solution.py:307
  218.1 6.1 %collective-permute-done.22.refs_1_ = bf16[256,1792]{1,0:T(8,128)(2,1)S(1)} collective-permute-done((bf16[256,1792]{1,0:T(8,128)(2,1)S(1)}, bf16[256,1792]{1,0:T(8,128)(2,1)S(1)}, u32[]{:S(2)}, u32[]{:S(2)}) %collective-permute-start.22) | collective-permute-done | bytes 917536 | tf_op jit(solution)/shard_map/ppermute | solution.py:434
  225.8 10.3 %both_part.3 = (bf16[896,1024]{1,0:T(8,128)(2,1)}, bf16[896,1024]{1,0:T(8,128)(2,1)}) custom-call(s32[1]{0:T(128)} %bitcast.c_ref, bf16[160,1792]{1,0:T(8,128)(2,1)S(1)} %copy-done.17, bf16[160,3840]{1,0:T(8,128)(2,1)S(1)} %copy-done.9, bf16[160,1792]{1,0:T(8,128)(2,1)S(1)} %copy-done.19, bf16[160,3840]{1,0:T(8,128)(2,1)S(1)} %copy-done.11, ...), custom_call_target="tpu_custom_call" | custom-call | flops 1000 | bytes 1000 | tf_op jit(solution)/shard_map/both_part/pallas_call | solution.py:376
  236.1 10.0 %collective-permute-done.23.refs_2_ = bf16[256,1792]{1,0:T(8,128)(2,1)S(1)} collective-permute-done((bf16[256,1792]{1,0:T(8,128)(2,1)S(1)}, bf16[256,1792]{1,0:T(8,128)(2,1)S(1)}, u32[]{:S(2)}, u32[]{:S(2)}) %collective-permute-start.23) | collective-permute-done | bytes 917536 | tf_op jit(solution)/shard_map/ppermute | solution.py:434
  246.2 4.9 %down_part.7 = bf16[256,3584]{1,0:T(8,128)(2,1)} custom-call(s32[1]{0:T(128)S(6)} %add.50.s_ref, bf16[640,1024]{1,0:T(8,128)(2,1)S(1)} %get-tuple-element.126.hid_ref, bf16[640,3584]{1,0:T(8,128)(2,1)S(1)} %bitcast.9, bf16[256,3584]{1,0:T(8,128)(2,1)S(1)} %collective-permute-done.21.refs_0_, bf16[256,1792]{1,0:T(8,128)(2,1)S(1)} %collective-permute-done.22.refs_1_, ...), custom_call_target="tpu_custom_call" | custom-call | flops 1000 | bytes 1000 | tf_op jit(solution)/shard_map/down_part/pallas_call | solution.py:307
  (138 shorter events, 52.5 us)
Async XLA Ops:
  5.9 47.8 %collective-permute-start.4 = (bf16[256,3712]{1,0:T(8,128)(2,1)}, bf16[256,3712]{1,0:T(8,128)(2,1)}, u32[]{:S(2)}, u32[]{:S(2)}) collective-permute-start(bf16[256,3712]{1,0:T(8,128)(2,1)} %pack.1.refs_0_.refs_1_), channel_id=1, source_target_pairs={{2,4},{3,5},{4,2},{5,3},{10,12},{11,13},{12,10},{13,11},{18,20},{1... | collective-permute-start | bytes 5701640 | tf_op jit(solution)/shard_map/ppermute | solution.py:413
  7.8 46.1 %collective-permute-start.3 = (bf16[256,3712]{1,0:T(8,128)(2,1)}, bf16[256,3712]{1,0:T(8,128)(2,1)}, u32[]{:S(2)}, u32[]{:S(2)}) collective-permute-start(bf16[256,3712]{1,0:T(8,128)(2,1)} %pack.1.refs_0_.refs_1_), channel_id=1, source_target_pairs={{0,2},{1,3},{2,0},{3,1},{4,6},{5,7},{6,4},{7,5},{8,10},{9,11},{10,... | collective-permute-start | bytes 5701640 | tf_op jit(solution)/shard_map/ppermute | solution.py:413
  12.7 35.2 %slice-start.6 = ((s8[7340032]{0:T(1024)(128)(4,1)}), s8[3145728]{0:T(1024)(128)(4,1)S(1)}, s32[]{:S(2)}) async-start(s8[7340032]{0:T(1024)(128)(4,1)} %bitcast.14), calls=%async_computation.6 | async-start | bytes 6291456
  17.7 16.2 %collective-permute-start = (bf16[80,3584]{1,0:T(8,128)(2,1)}, bf16[80,3584]{1,0:T(8,128)(2,1)}, u32[]{:S(2)}, u32[]{:S(2)}) collective-permute-start(bf16[80,3584]{1,0:T(8,128)(2,1)} %get-tuple-element.71), channel_id=1, source_target_pairs={{0,1},{1,0},{2,3},{3,2},{4,5},{5,4},{6,7},{7,6},{8,9},{9,8},{10,11... | collective-permute-start | bytes 1720328 | tf_op jit(solution)/shard_map/ppermute | solution.py:425
  24.1 23.8 %collective-permute-start.1 = (bf16[80,3584]{1,0:T(8,128)(2,1)}, bf16[80,3584]{1,0:T(8,128)(2,1)}, u32[]{:S(2)}, u32[]{:S(2)}) collective-permute-start(bf16[80,3584]{1,0:T(8,128)(2,1)} %get-tuple-element.76), channel_id=1, source_target_pairs={{0,1},{1,0},{2,3},{3,2},{4,5},{5,4},{6,7},{7,6},{8,9},{9,8},{10,11... | collective-permute-start | bytes 1720328 | tf_op jit(solution)/shard_map/ppermute | solution.py:425
  41.1 46.1 %slice-start.4 = ((s8[7340032]{0:T(1024)(128)(4,1)}), s8[4194304]{0:T(1024)(128)(4,1)S(1)}, s32[]{:S(2)}) async-start(s8[7340032]{0:T(1024)(128)(4,1)} %bitcast.12), calls=%async_computation.4 | async-start | bytes 8388608
  47.9 39.3 %slice-start.2 = ((s8[7340032]{0:T(1024)(128)(4,1)}), s8[4194304]{0:T(1024)(128)(4,1)S(1)}, s32[]{:S(2)}) async-start(s8[7340032]{0:T(1024)(128)(4,1)} %bitcast.10), calls=%async_computation.2 | async-start | bytes 8388608
  47.9 39.3 %slice-start.3 = ((s8[7340032]{0:T(1024)(128)(4,1)}), s8[3145728]{0:T(1024)(128)(4,1)S(1)}, s32[]{:S(2)}) async-start(s8[7340032]{0:T(1024)(128)(4,1)} %bitcast.10), calls=%async_computation.3 | async-start | bytes 6291456
  47.9 39.3 %slice-start.5 = ((s8[7340032]{0:T(1024)(128)(4,1)}), s8[3145728]{0:T(1024)(128)(4,1)S(1)}, s32[]{:S(2)}) async-start(s8[7340032]{0:T(1024)(128)(4,1)} %bitcast.12), calls=%async_computation.5 | async-start | bytes 6291456
  53.9 43.0 %collective-permute-start.8 = (bf16[256,3712]{1,0:T(8,128)(2,1)}, bf16[256,3712]{1,0:T(8,128)(2,1)S(1)}, u32[]{:S(2)}, u32[]{:S(2)}) collective-permute-start(bf16[256,3712]{1,0:T(8,128)(2,1)} %collective-permute-done.3.refs_0_.refs_1_.refs_2_), channel_id=1, source_target_pairs={{2,4},{3,5},{4,2},{5,3},{10,12},{11,13},{12,10},{13,11},{18,20},{1... | collective-permute-start | bytes 5701640 | tf_op jit(solution)/shard_map/ppermute | solution.py:416
  54.7 44.8 %collective-permute-start.7 = (bf16[256,3712]{1,0:T(8,128)(2,1)}, bf16[256,3712]{1,0:T(8,128)(2,1)S(1)}, u32[]{:S(2)}, u32[]{:S(2)}) collective-permute-start(bf16[256,3712]{1,0:T(8,128)(2,1)} %collective-permute-done.4.refs_0_.refs_2_), channel_id=1, source_target_pairs={{2,0},{3,1},{4,6},{5,7},{10,8},{11,9},{12,14},{13,15},{18,16},{19,... | collective-permute-start | bytes 5701640 | tf_op jit(solution)/shard_map/ppermute | solution.py:416
  56.0 28.0 %collective-permute-start.2 = (bf16[160,3840]{1,0:T(8,128)(2,1)S(1)}, bf16[160,3840]{1,0:T(8,128)(2,1)S(1)}, u32[]{:S(2)}, u32[]{:S(2)}) collective-permute-start(bf16[160,3840]{1,0:T(8,128)(2,1)S(1)} %get-tuple-element.129.refs_8_), channel_id=1, source_target_pairs={{0,16},{8,24},{16,0},{24,8},{1,17},{9,25},{17,1},{25,9},{2,18},{10... | collective-permute-start | bytes 3686408 | tf_op jit(solution)/shard_map/ppermute | solution.py:434
  61.3 25.9 %collective-permute-start.5 = (bf16[160,3584]{1,0:T(8,128)(2,1)S(1)}, bf16[160,3584]{1,0:T(8,128)(2,1)S(1)}, u32[]{:S(2)}, u32[]{:S(2)}) collective-permute-start(bf16[160,3584]{1,0:T(8,128)(2,1)S(1)} %get-tuple-element.83), channel_id=1, source_target_pairs={{0,1},{1,0},{2,3},{3,2},{4,5},{5,4},{6,7},{7,6},{8,9},{9,8},{10,11... | collective-permute-start | bytes 3440648 | tf_op jit(solution)/shard_map/ppermute | solution.py:425
  96.3 26.9 %collective-permute-start.6 = (bf16[160,3840]{1,0:T(8,128)(2,1)S(1)}, bf16[160,3840]{1,0:T(8,128)(2,1)S(1)}, u32[]{:S(2)}, u32[]{:S(2)}) collective-permute-start(bf16[160,3840]{1,0:T(8,128)(2,1)S(1)} %get-tuple-element.92.refs_10_), channel_id=1, source_target_pairs={{0,16},{8,24},{16,0},{24,8},{1,17},{9,25},{17,1},{25,9},{2,18},{10... | collective-permute-start | bytes 3686408 | tf_op jit(solution)/shard_map/ppermute | solution.py:434
  97.0 26.2 %collective-permute-start.11 = (bf16[128,3712]{1,0:T(8,128)(2,1)S(1)}, bf16[128,3712]{1,0:T(8,128)(2,1)S(1)}, u32[]{:S(2)}, u32[]{:S(2)}) collective-permute-start(bf16[128,3712]{1,0:T(8,128)(2,1)S(1)} %slice.8), channel_id=1, source_target_pairs={{2,0},{3,1},{4,6},{5,7},{10,8},{11,9},{12,14},{13,15},{18,16},{19,... | collective-permute-start | bytes 2850824 | tf_op jit(solution)/shard_map/ppermute | solution.py:419
  101.8 16.0 %collective-permute-start.9 = (bf16[80,3584]{1,0:T(8,128)(2,1)S(1)}, bf16[80,3584]{1,0:T(8,128)(2,1)S(1)}, u32[]{:S(2)}, u32[]{:S(2)}) collective-permute-start(bf16[80,3584]{1,0:T(8,128)(2,1)S(1)} %get-tuple-element.97), channel_id=1, source_target_pairs={{0,1},{1,0},{2,3},{3,2},{4,5},{5,4},{6,7},{7,6},{8,9},{9,8},{10,11... | collective-permute-start | bytes 1720328 | tf_op jit(solution)/shard_map/ppermute | solution.py:425
  105.8 21.1 %collective-permute-start.10 = (bf16[80,3584]{1,0:T(8,128)(2,1)S(1)}, bf16[80,3584]{1,0:T(8,128)(2,1)S(1)}, u32[]{:S(2)}, u32[]{:S(2)}) collective-permute-start(bf16[80,3584]{1,0:T(8,128)(2,1)S(1)} %get-tuple-element.103), channel_id=1, source_target_pairs={{0,1},{1,0},{2,3},{3,2},{4,5},{5,4},{6,7},{7,6},{8,9},{9,8},{10,11... | collective-permute-start | bytes 1720328 | tf_op jit(solution)/shard_map/ppermute | solution.py:425
  106.4 44.0 %collective-permute-start.15 = (bf16[128,3584]{1,0:T(8,128)(2,1)S(1)}, bf16[128,3584]{1,0:T(8,128)(2,1)S(1)}, u32[]{:S(2)}, u32[]{:S(2)}) collective-permute-start(bf16[128,3584]{1,0:T(8,128)(2,1)S(1)} %slice.9), channel_id=1, source_target_pairs={{2,0},{3,1},{4,6},{5,7},{10,8},{11,9},{12,14},{13,15},{18,16},{19,... | collective-permute-start | bytes 2752520 | tf_op jit(solution)/shard_map/ppermute | solution.py:419
  132.1 18.3 %copy-start = (bf16[640,3584]{1,0:T(8,128)(2,1)}, bf16[640,3584]{1,0:T(8,128)(2,1)S(1)}, u32[]{:S(2)}) copy-start(bf16[640,3584]{1,0:T(8,128)(2,1)S(1)} %get-tuple-element.125.refs_6_) | copy-start | bytes 13762564
  132.1 18.3 %copy-start.6 = (bf16[640,1024]{1,0:T(8,128)(2,1)}, bf16[640,1024]{1,0:T(8,128)(2,1)S(1)}, u32[]{:S(2)}) copy-start(bf16[640,1024]{1,0:T(8,128)(2,1)S(1)} %get-tuple-element.124.refs_5_) | copy-start | bytes 3932164
  132.1 38.4 %collective-permute-start.12 = (bf16[160,3840]{1,0:T(8,128)(2,1)}, bf16[160,3840]{1,0:T(8,128)(2,1)S(1)}, u32[]{:S(2)}, u32[]{:S(2)}) collective-permute-start(bf16[160,3840]{1,0:T(8,128)(2,1)} %get-tuple-element.113.refs_12_), channel_id=1, source_target_pairs={{0,16},{8,24},{16,0},{24,8},{1,17},{9,25},{17,1},{25,9},{2,18},{10... | collective-permute-start | bytes 3686408 | tf_op jit(solution)/shard_map/ppermute | solution.py:434
  133.6 11.5 %collective-permute-start.13 = (bf16[80,3584]{1,0:T(8,128)(2,1)S(1)}, bf16[80,3584]{1,0:T(8,128)(2,1)S(1)}, u32[]{:S(2)}, u32[]{:S(2)}) collective-permute-start(bf16[80,3584]{1,0:T(8,128)(2,1)S(1)} %get-tuple-element.114), channel_id=1, source_target_pairs={{0,1},{1,0},{2,3},{3,2},{4,5},{5,4},{6,7},{7,6},{8,9},{9,8},{10,11... | collective-permute-start | bytes 1720328 | tf_op jit(solution)/shard_map/ppermute | solution.py:425
  150.4 20.1 %copy-start.7 = (bf16[640,1024]{1,0:T(8,128)(2,1)S(1)}, bf16[640,1024]{1,0:T(8,128)(2,1)}, u32[]{:S(2)}) copy-start(bf16[640,1024]{1,0:T(8,128)(2,1)} %copy-done.6) | copy-start | bytes 3932164
  155.9 10.9 %collective-permute-start.16 = (bf16[80,3584]{1,0:T(8,128)(2,1)}, bf16[80,3584]{1,0:T(8,128)(2,1)}, u32[]{:S(2)}, u32[]{:S(2)}) collective-permute-start(bf16[80,3584]{1,0:T(8,128)(2,1)} %get-tuple-element.121), channel_id=1, source_target_pairs={{0,1},{1,0},{2,3},{3,2},{4,5},{5,4},{6,7},{7,6},{8,9},{9,8},{10,11... | collective-permute-start | bytes 1720328 | tf_op jit(solution)/shard_map/ppermute | solution.py:425
  157.3 13.2 %collective-permute-start.14 = (bf16[160,1792]{1,0:T(8,128)(2,1)}, bf16[160,1792]{1,0:T(8,128)(2,1)}, u32[]{:S(2)}, u32[]{:S(2)}) collective-permute-start(bf16[160,1792]{1,0:T(8,128)(2,1)} %get-tuple-element.117), channel_id=1, source_target_pairs={{0,16},{8,24},{16,0},{24,8},{1,17},{9,25},{17,1},{25,9},{2,18},{10... | collective-permute-start | bytes 1720328 | tf_op jit(solution)/shard_map/ppermute | solution.py:434
  187.4 3.9 %collective-permute-start.17 = (bf16[256,3584]{1,0:T(8,128)(2,1)S(1)}, bf16[256,3584]{1,0:T(8,128)(2,1)S(1)}, u32[]{:S(2)}, u32[]{:S(2)}) collective-permute-start(bf16[256,3584]{1,0:T(8,128)(2,1)S(1)} %down_part.4), channel_id=1, source_target_pairs={{0,8},{8,0},{16,24},{24,16},{1,9},{9,1},{17,25},{25,17},{2,10},{10... | collective-permute-start | bytes 5505032 | tf_op jit(solution)/shard_map/ppermute | solution.py:431
  187.5 17.6 %collective-permute-start.18 = (bf16[160,2048]{1,0:T(8,128)(2,1)S(1)}, bf16[160,2048]{1,0:T(8,128)(2,1)S(1)}, u32[]{:S(2)}, u32[]{:S(2)}) collective-permute-start(bf16[160,2048]{1,0:T(8,128)(2,1)S(1)} %get-tuple-element.130.refs_14_), channel_id=1, source_target_pairs={{0,16},{8,24},{16,0},{24,8},{1,17},{9,25},{17,1},{25,9},{2,18},{10... | collective-permute-start | bytes 1966088 | tf_op jit(solution)/shard_map/ppermute | solution.py:434
  195.0 29.2 %collective-permute-start.22 = (bf16[256,1792]{1,0:T(8,128)(2,1)S(1)}, bf16[256,1792]{1,0:T(8,128)(2,1)S(1)}, u32[]{:S(2)}, u32[]{:S(2)}) collective-permute-start(bf16[256,1792]{1,0:T(8,128)(2,1)S(1)} %get-tuple-element.135), channel_id=1, source_target_pairs={{0,16},{8,24},{16,0},{24,8},{1,17},{9,25},{17,1},{25,9},{2,18},{10... | collective-permute-start | bytes 2752520 | tf_op jit(solution)/shard_map/ppermute | solution.py:434
  214.2 11.6 %collective-permute-start.19 = (bf16[896,1024]{1,0:T(8,128)(2,1)S(1)}, bf16[896,1024]{1,0:T(8,128)(2,1)S(1)}, u32[]{:S(2)}, u32[]{:S(2)}) collective-permute-start(bf16[896,1024]{1,0:T(8,128)(2,1)S(1)} %get-tuple-element.131), channel_id=1, source_target_pairs={{0,8},{8,0},{16,24},{24,16},{1,9},{9,1},{17,25},{25,17},{2,10},{10... | collective-permute-start | bytes 5505032 | tf_op jit(solution)/shard_map/ppermute | solution.py:431
  214.3 11.5 %collective-permute-start.20 = (bf16[896,1024]{1,0:T(8,128)(2,1)S(1)}, bf16[896,1024]{1,0:T(8,128)(2,1)S(1)}, u32[]{:S(2)}, u32[]{:S(2)}) collective-permute-start(bf16[896,1024]{1,0:T(8,128)(2,1)S(1)} %get-tuple-element.132), channel_id=1, source_target_pairs={{0,8},{8,0},{16,24},{24,16},{1,9},{9,1},{17,25},{25,17},{2,10},{10... | collective-permute-start | bytes 5505032 | tf_op jit(solution)/shard_map/ppermute | solution.py:431
  218.0 18.1 %collective-permute-start.21 = (bf16[256,3584]{1,0:T(8,128)(2,1)S(1)}, bf16[256,3584]{1,0:T(8,128)(2,1)S(1)}, u32[]{:S(2)}, u32[]{:S(2)}) collective-permute-start(bf16[256,3584]{1,0:T(8,128)(2,1)S(1)} %down_part.6), channel_id=1, source_target_pairs={{0,8},{8,0},{16,24},{24,16},{1,9},{9,1},{17,25},{25,17},{2,10},{10... | collective-permute-start | bytes 5505032 | tf_op jit(solution)/shard_map/ppermute | solution.py:431
  224.3 21.9 %collective-permute-start.23 = (bf16[256,1792]{1,0:T(8,128)(2,1)S(1)}, bf16[256,1792]{1,0:T(8,128)(2,1)S(1)}, u32[]{:S(2)}, u32[]{:S(2)}) collective-permute-start(bf16[256,1792]{1,0:T(8,128)(2,1)S(1)} %get-tuple-element.136), channel_id=1, source_target_pairs={{0,16},{8,24},{16,0},{24,8},{1,17},{9,25},{17,1},{25,9},{2,18},{10... | collective-permute-start | bytes 2752520 | tf_op jit(solution)/shard_map/ppermute | solution.py:434
  (37 other events, 218.0 us)

commit v3 on v2

v3 whole, which is shorter than its diff:
```python
import functools

import jax
import jax.numpy as jnp
from jax import lax
from jax.experimental import pallas as pl
from jax.experimental.pallas import tpu as pltpu
from jax.sharding import PartitionSpec as P

NZ = 4
NC = 2
F32, BF16 = jnp.float32, jnp.bfloat16
COST = pl.CostEstimate(flops=3000000000, bytes_accessed=1000, transcendentals=0)


LANES = 128


def params(mib):
    return pltpu.CompilerParams(vmem_limit_bytes=mib << 20)


def contract_rows(left, right):
    return lax.dot_general(left, right, (((0,), (0,)), ((), ())), preferred_element_type=F32)


def after(values, *deps):
    return lax.optimization_barrier((values, deps))[0]


def pack_kernel(routes_ref, gain_ref, tok_ref, cot_ref, out_ref):
    top = routes_ref.shape[0]
    toks, width = tok_ref.shape
    g = gain_ref[...]
    high = g.astype(BF16)
    g = g - high.astype(F32)
    mid = g.astype(BF16)
    low = (g - mid.astype(F32)).astype(BF16)
    rows = [routes_ref[...].astype(F32), high.astype(F32), mid.astype(F32), low.astype(F32)]
    total = jnp.zeros((toks, LANES), F32)
    for i, r in enumerate(rows):
        row = lax.broadcasted_iota(jnp.int32, (top, LANES), 0)
        col = lax.broadcasted_iota(jnp.int32, (top, LANES), 1)
        place = jnp.where(col == row + i * top, 1.0, 0.0).astype(BF16)
        total = total + contract_rows(r.astype(BF16), place)
    out_ref[:toks, :width] = tok_ref[...]
    out_ref[:toks, width:] = total.astype(BF16)
    out_ref[toks:, :width] = cot_ref[...]
    out_ref[toks:, width:] = jnp.zeros((toks, LANES), BF16)


def pack(tokens, cotangent, routes, gain):
    toks, width = tokens.shape
    return pl.pallas_call(
        pack_kernel,
        in_specs=[pl.BlockSpec(memory_space=pltpu.VMEM)] * 4,
        out_specs=pl.BlockSpec(memory_space=pltpu.VMEM),
        out_shape=jax.ShapeDtypeStruct((2 * toks, width + LANES), BF16),
        compiler_params=params(8),
        cost_estimate=COST,
        name="pack",
    )(routes.T, gain.T, tokens, cotangent)


def added(refs):
    value = refs[0][...]
    for r in refs[1:]:
        value = value + r[...]
    return value


def pick_kernel(ids_ref, *refs, nx, top, n_meta, n_x, n_c):
    meta_refs, refs = refs[:n_meta], refs[n_meta:]
    x_refs, c_refs, refs = refs[:n_x], refs[n_x : n_x + n_c], refs[n_x + n_c :]
    kinds = (1 if n_x else 0) + (1 if n_c else 0)
    own_refs, send_refs = refs[:kinds], refs[kinds : kinds + nx - 1]
    pick_ref, gain_ref = refs[-2:]
    cap, toks = pick_ref.shape[1:]

    @pl.when(pl.program_id(0) == 0)
    def _():
        row = lax.broadcasted_iota(jnp.int32, (4 * top, LANES), 0)
        col = lax.broadcasted_iota(jnp.int32, (4 * top, LANES), 1)
        place = jnp.where(col == row, 1.0, 0.0).astype(BF16)
        meta = lax.dot_general(
            place, added(meta_refs), (((1,), (1,)), ((), ())), preferred_element_type=F32
        )
        r = meta[0:top]
        g = (meta[top : 2 * top] + meta[2 * top : 3 * top]) + meta[3 * top :]
        row = lax.broadcasted_iota(jnp.int32, (toks, toks), 0)
        col = lax.broadcasted_iota(jnp.int32, (toks, toks), 1)
        before = jnp.where(row < col, 1.0, 0.0).astype(BF16)
        place = lax.broadcasted_iota(jnp.int32, (cap, toks), 0).astype(F32)
        for k in range(nx):
            named = r == ids_ref[0, k].astype(F32)
            alive = ids_ref[1, k].astype(F32)
            match = jnp.sum(jnp.where(named, 1.0, 0.0), axis=0, keepdims=True) * alive
            gain_t = jnp.sum(jnp.where(named, g, 0.0), axis=0, keepdims=True)
            wide = jnp.broadcast_to(match, (8, toks)).astype(BF16)
            pos = jnp.dot(wide, before, preferred_element_type=F32)[0:1]
            pick = jnp.where(place == pos, jnp.broadcast_to(match, (cap, toks)), 0.0)
            pick_ref[k] = pick.astype(BF16)
            if n_c:
                gain_ref[k] = jnp.sum(pick * gain_t, axis=1, keepdims=True)

    for i, (block_refs, weighted) in enumerate(
        ([(x_refs, False)] if n_x else []) + ([(c_refs, True)] if n_c else [])
    ):
        block = added(block_refs)
        for k in range(nx):
            sel = jnp.dot(pick_ref[k], block, preferred_element_type=F32)
            if weighted:
                sel = gain_ref[k] * sel
            if k == 0:
                own_refs[i][...] = sel.astype(BF16)
            else:
                send_refs[k - 1][i * cap : (i + 1) * cap, :] = sel.astype(BF16)


def pick_rows(ids, metas, xs, cs, nx, cap, top, width, toks):
    tile = width // 4
    kinds = (1 if xs else 0) + (1 if cs else 0)
    own, *sends = pl.pallas_call(
        functools.partial(
            pick_kernel, nx=nx, top=top, n_meta=len(metas), n_x=len(xs), n_c=len(cs)
        ),
        grid=(width // tile,),
        in_specs=[pl.BlockSpec(memory_space=pltpu.SMEM)]
        + [pl.BlockSpec((toks, LANES), lambda j: (0, width // LANES))] * len(metas)
        + [pl.BlockSpec((toks, tile), lambda j: (0, j))] * len(xs)
        + [
            pl.BlockSpec((toks, tile), lambda j, at=v.shape[0] // toks - 1: (at, j)) for v in cs
        ],
        out_specs=[pl.BlockSpec((cap, tile), lambda j: (0, j))] * kinds
        + [pl.BlockSpec((kinds * cap, tile), lambda j: (0, j))] * (nx - 1),
        out_shape=[jax.ShapeDtypeStruct((cap, width), BF16)] * kinds
        + [jax.ShapeDtypeStruct((kinds * cap, width), BF16)] * (nx - 1),
        scratch_shapes=[pltpu.VMEM((nx, cap, toks), BF16), pltpu.VMEM((nx, cap, 1), F32)],
        compiler_params=params(6),
        cost_estimate=COST,
        name="pick",
    )(ids, *metas, *xs, *cs)
    return own, sends


def whole(count):
    return [pl.BlockSpec(memory_space=pltpu.VMEM)] * count


def gate_up_kernel(y_ref, *refs, parts, ny):
    rows_in, (wg_ref, wu_ref) = refs[:parts], refs[parts : parts + 2]
    gate_ref, up_ref, *splits = refs[parts + 2 : parts + 4 + ny]
    joined = refs[parts + 4 + ny]
    cap = rows_in[0].shape[0]
    for k in range(parts):
        joined[k * cap : (k + 1) * cap, :] = rows_in[k][...]
    half = joined.shape[1] // ny
    for k in range(ny):
        begin = pl.multiple_of((y_ref[0] ^ k) * half, LANES)
        splits[k][...] = joined[:, pl.ds(begin, half)]
    x = joined[...]
    gate_ref[...] = jnp.dot(x, wg_ref[0], preferred_element_type=F32)
    up_ref[...] = jnp.dot(x, wu_ref[0], preferred_element_type=F32)


def gate_up(y, parts, w_gate, w_up, ny):
    cap, width = parts[0].shape
    ff = w_gate.shape[2]
    rows = cap * len(parts)
    return pl.pallas_call(
        functools.partial(gate_up_kernel, parts=len(parts), ny=ny),
        in_specs=[pl.BlockSpec(memory_space=pltpu.SMEM)] + whole(len(parts) + 2),
        out_specs=whole(2 + ny),
        out_shape=[jax.ShapeDtypeStruct((rows, ff), F32)] * 2
        + [jax.ShapeDtypeStruct((rows, width // ny), BF16)] * ny,
        scratch_shapes=[pltpu.VMEM((rows, width), BF16)],
        compiler_params=params(10),
        cost_estimate=COST,
        name="gate_up",
    )(y, *parts, w_gate, w_up)


def back_kernel(*refs, parts):
    rows_in, (wd_ref, gate_ref, up_ref) = refs[:parts], refs[parts : parts + 3]
    d_ref, hid_ref, cot_ref = refs[parts + 3 :]
    cap = rows_in[0].shape[0]
    ff = gate_ref.shape[1]
    for k in range(parts):
        cot_ref[k * cap : (k + 1) * cap, :] = rows_in[k][...]
    total = lax.dot_general(
        cot_ref[...], wd_ref[0], (((1,), (1,)), ((), ())), preferred_element_type=F32
    )
    gate, up = gate_ref[...], up_ref[...]
    sig = jax.nn.sigmoid(gate)
    act = gate * sig
    hid_ref[...] = (act * up).astype(BF16)
    d_ref[:, :ff] = (total * up * sig * (1.0 + gate * (1.0 - sig))).astype(BF16)
    d_ref[:, ff:] = (total * act).astype(BF16)


def back(parts, w_down, gate, up):
    width = parts[0].shape[1]
    rows, ff = gate.shape
    n = len(parts)
    return pl.pallas_call(
        functools.partial(back_kernel, parts=n),
        in_specs=whole(n + 3),
        out_specs=whole(3),
        out_shape=[
            jax.ShapeDtypeStruct((rows, 2 * ff), BF16),
            jax.ShapeDtypeStruct((rows, ff), BF16),
            jax.ShapeDtypeStruct((rows, width), BF16),
        ],
        compiler_params=params(10),
        cost_estimate=COST,
        name="back",
    )(*parts, w_down, gate, up)


def down_kernel(s_ref, *refs, pieces, ins, outs):
    hids, cots, refs = refs[:pieces], refs[pieces : 2 * pieces], refs[2 * pieces :]
    in_refs, out_refs, (left, right, acc) = refs[: len(ins)], refs[len(ins) : -3], refs[-3:]
    j = pl.program_id(0)
    rows = hids[0].shape[0]
    for k in range(pieces):
        left[k * rows : (k + 1) * rows, :] = hids[k][...]
        right[k * rows : (k + 1) * rows, :] = cots[k][...]
    acc[...] = contract_rows(left[...], right[...])
    for (begin, size), ref in zip(ins, in_refs):

        @pl.when((j >= begin) & (j < begin + size))
        def _(ref=ref):
            acc[...] += ref[...].astype(F32)

    for (begin, size), ref in zip(outs, out_refs):

        @pl.when((j >= begin) & (j < begin + size))
        def _(ref=ref):
            ref[...] = acc[...].astype(ref.dtype)


def down_part(index, hidden, cot, n, arrived=(), outs=(4,), dtype=BF16):
    rows, width = cot[0].shape
    m = len(cot)
    steps = 4
    tile = width // steps

    def ranges(sizes):
        return [(sum(sizes[:i]), size) for i, size in enumerate(sizes)]

    def chunk(begin, size):
        return pl.BlockSpec(
            (n, tile), lambda j, s_ref: (0, jnp.minimum(jnp.maximum(j - begin, 0), size - 1))
        )

    ins = [r for a in arrived for r in ranges([v.shape[1] // tile for v in a])]
    outs = ranges(outs)
    return pl.pallas_call(
        functools.partial(down_kernel, pieces=m, ins=ins, outs=outs),
        grid_spec=pltpu.PrefetchScalarGridSpec(
            num_scalar_prefetch=1,
            grid=(steps,),
            in_specs=[pl.BlockSpec((rows, n), lambda j, s_ref: (0, s_ref[0]))] * m
            + [pl.BlockSpec((rows, tile), lambda j, s_ref: (0, j))] * m
            + [chunk(*r) for r in ins],
            out_specs=[chunk(*r) for r in outs],
            scratch_shapes=[
                pltpu.VMEM((m * rows, n), BF16),
                pltpu.VMEM((m * rows, tile), BF16),
                pltpu.VMEM((n, tile), F32),
            ],
        ),
        out_shape=[jax.ShapeDtypeStruct((n, tile * size), dtype) for _, size in outs],
        compiler_params=params(9),
        cost_estimate=COST,
        name="down_part",
    )(index, *hidden, *cot, *[piece for a in arrived for piece in a])


def both_kernel(c_ref, *refs, pieces, add):
    xs, ds = refs[:pieces], refs[pieces : 2 * pieces]
    rest = refs[2 * pieces :]
    got, outs, (left, right, acc) = rest[:add], rest[add:-3], rest[-3:]
    rows = xs[0].shape[0]
    j = pl.program_id(0)

    @pl.when(j == 0)
    def _():
        for i in range(pieces):
            left[i * rows : (i + 1) * rows, :] = xs[i][...]

    for i in range(pieces):
        right[i * rows : (i + 1) * rows, :] = ds[i][...]
    acc[...] = contract_rows(left[...], right[...])
    for w, ref in enumerate(got):

        @pl.when(j == w)
        def _(ref=ref):
            acc[...] += ref[...].astype(F32)

    for w, out in enumerate(outs):

        @pl.when(j * len(outs) // pl.num_programs(0) == w)
        def _(w=w, out=out):
            total = acc[...]
            out[...] = total.astype(BF16)


def both_part(index, xs, ds, n, arrived=()):
    rows, ff2 = ds[0].shape
    steps, tile = 4, ff2 // 4
    m = len(xs)
    add = len(arrived)
    outs = 2 if add else steps
    per = steps // outs

    return pl.pallas_call(
        functools.partial(both_kernel, pieces=m, add=add),
        grid_spec=pltpu.PrefetchScalarGridSpec(
            num_scalar_prefetch=1,
            grid=(steps,),
            in_specs=[pl.BlockSpec((rows, n), lambda j, c_ref: (0, c_ref[0]))] * m
            + [pl.BlockSpec((rows, tile), lambda j, c_ref: (0, j))] * m
            + [pl.BlockSpec((n, tile), lambda j, c_ref: (0, 0))] * add,
            out_specs=[
                pl.BlockSpec(
                    (n, tile),
                    lambda j, c_ref, w=w: (0, jnp.minimum(jnp.maximum(j - w * per, 0), per - 1)),
                )
                for w in range(outs)
            ],
            scratch_shapes=[
                pltpu.VMEM((m * rows, n), BF16),
                pltpu.VMEM((m * rows, tile), BF16),
                pltpu.VMEM((n, tile), F32),
            ],
        ),
        out_shape=[jax.ShapeDtypeStruct((n, ff2 // outs), BF16)] * outs,
        compiler_params=params(22),
        cost_estimate=COST,
        name="both_part",
    )(index, *xs, *ds, *arrived)


def make_per_device(n_dp, n_expert):
    nx = n_expert // NZ
    ny = n_dp // NC

    def ex(z, x):
        return z * nx + x

    def zpairs(moves):
        return [(ex(a, x), ex(b, x)) for a, b in moves for x in range(nx)]

    ends_first = zpairs([(0, 1), (1, 0), (2, 3), (3, 2)])
    middle = zpairs([(1, 2), (2, 1)])
    outward = zpairs([(1, 0), (2, 3)])

    def hop1(block):
        return lax.ppermute(block, "expert", ends_first), lax.ppermute(block, "expert", middle)

    def hop2(a, c_mid):
        return lax.ppermute(c_mid, "expert", outward), lax.ppermute(a, "expert", middle)

    def hop3(b_mid):
        return lax.ppermute(b_mid, "expert", outward)

    def over_x(sends):
        out = []
        for k in range(1, nx):
            pairs = [(ex(z, x), ex(z, x ^ k)) for z in range(NZ) for x in range(nx)]
            out.append(lax.ppermute(sends[k - 1], "expert", pairs))
        return out

    core_pairs = [(y * NC + c, y * NC + 1 - c) for y in range(ny) for c in range(NC)]

    def over_core(value):
        return lax.ppermute(value, "dp", core_pairs)

    def over_y(value, k):
        return lax.ppermute(
            value, "dp", [(y * NC + c, (y ^ k) * NC + c) for y in range(ny) for c in range(NC)]
        )

    def per_device(tokens, cotangent, routes, route_gain, expert_alive, w_gate, w_up, w_down):
        tok_count, width = tokens.shape
        top = routes.shape[1]
        experts_all = expert_alive.shape[0]
        cap = tok_count * top * 5 // (4 * experts_all)
        ff = w_gate.shape[2]
        half = width // ny
        me = lax.axis_index("expert")
        z, x = me // nx, me % nx
        d = lax.axis_index("dp")
        y_arr = (d // NC).astype(jnp.int32)[None]
        c_arr = (d % NC).astype(jnp.int32)[None]

        own = pack(tokens, cotangent, routes, route_gain)
        a, c_mid = hop1(own)

        own_ids = z * nx + (x ^ jnp.arange(nx, dtype=jnp.int32))
        alive = jnp.sum(
            jnp.where(
                own_ids[:, None] == jnp.arange(experts_all)[None, :], expert_alive[None, :], 0
            ),
            axis=1,
        )
        ids = jnp.stack([own_ids, alive.astype(jnp.int32)])

        def pick(metas, xs=(), cs=()):
            own, sends = pick_rows(ids, metas, xs, cs, nx, cap, top, width, tok_count)
            return own, over_x(sends)

        xs, ds, hidden, cot_rows = [], [], [], []

        def spread(pieces, values):
            got = [over_y(values[k], k) for k in range(1, ny)]
            pieces += [values[0], *got]
            return got

        def forward(parts):
            gate, up, *splits = gate_up(y_arr, parts, w_gate, w_up, ny)
            return gate, up, spread(xs, splits)

        def backward(parts, gate, up):
            both, hid, cot = back(parts, w_down, gate, up)
            hidden.append(hid)
            cot_rows.append(cot)
            return both, spread(ds, [both] * ny)

        x0, s0 = pick([own], [own])
        c0, t0 = pick([own], (), [after(own, x0)])
        g0, u0, xs0 = forward([x0, *s0])
        f0, d0 = backward([c0, *t0], g0, u0)
        a, c_mid = after((a, c_mid), f0)
        b_end, b_mid = hop2(a, c_mid)
        x1, s1 = pick([a], [a])
        c1, t1 = pick([a], (), [after(a, x1)])
        s1 = after(s1, c1, xs0)
        g1, u1, xs1 = forward([x1, *s1])
        t1 = after(t1, d0)
        f1, d1 = backward([c1, *t1], g1, u1)
        xc_end = hop3(b_mid[:tok_count])
        cc_end = hop3(b_mid[tok_count:, :width])
        b_end, b_mid = after((b_end, b_mid), f1)
        x2, s2 = pick([b_end, b_mid], [b_end, b_mid])
        c2, t2 = pick([b_end, b_mid], (), after([b_end, b_mid], x2))
        s2 = after(s2, c2, xs1)
        g2, u2, xs2 = forward([x2, *s2])
        c_mid, xc_end = after((c_mid, xc_end), g2)
        x3, s3 = pick([c_mid, xc_end], [c_mid, xc_end])
        t2 = after(t2, x3, d1)
        f2, d2 = backward([c2, *t2], g2, u2)
        cc_end = after(cc_end, f2)
        c3, t3 = pick([c_mid, xc_end], (), [c_mid, cc_end])
        s3 = after(s3, c3)
        g3, u3, xs3 = forward([x3, *s3])
        t3 = after(t3, xs2, d2, xs3)
        f3, d3 = backward([c3, *t3], g3, u3)

        n = ff // n_dp

        def to_core(yy):
            return over_core(down_part(yy * NC + (1 - c_arr), hidden, cot_rows, n)[0])

        sent = [to_core(y_arr ^ k) for k in range(1, ny)]
        own_recv = to_core(y_arr)
        landed, totals = [], []
        for k in range(1, ny):
            recv = sent[k - 1]
            (total,) = down_part((y_arr ^ k) * NC + c_arr, hidden, cot_rows, n, [[after(recv, own_recv)]])
            landed.append([over_y(total, k)])
            totals.append(total)

        m = half // NC
        if m % LANES == 0:
            ds[0] = after(ds[0], totals)
            recv = [over_core(v) for v in both_part(1 - c_arr, xs, ds, m)]
            grad_gate, grad_up = both_part(c_arr, xs, ds, m, recv)
        else:
            x_all = jnp.concatenate(xs, axis=0)
            d_all = jnp.concatenate(ds, axis=0)

            def part(c):
                return contract_rows(lax.dynamic_slice_in_dim(x_all, c * m, m, 1), d_all)

            recv = over_core(part(1 - c_arr[0]).astype(BF16))
            total = (part(c_arr[0]) + recv.astype(F32)).astype(BF16)
            grad_gate, grad_up = total[:, :ff], total[:, ff:]

        (kept,) = down_part(
            y_arr * NC + c_arr, hidden, cot_rows, n, [[own_recv]], dtype=F32
        )
        landed = after(landed, kept, grad_up)
        for (part,) in landed:
            kept = kept + part.astype(F32)
        grad_down = kept.astype(BF16)
        return grad_gate[None], grad_up[None], grad_down[None]

    return per_device


def solution(mesh):
    in_specs = (
        P(("dp", "expert"), None),
        P(("dp", "expert"), None),
        P(("dp", "expert"), None),
        P(("dp", "expert"), None),
        P(),
        P("expert", None, None),
        P("expert", None, None),
        P("expert", None, None),
    )
    out_specs = (P("expert", "dp", None), P("expert", "dp", None), P("expert", "dp", None))
    per_device = make_per_device(mesh.shape["dp"], mesh.shape["expert"])
    return jax.shard_map(
        per_device, mesh=mesh, in_specs=in_specs, out_specs=out_specs, check_vma=False
    )
```

time: 252 us -> 240 us (0.952)
  Pallas kernels: 102 us -> 84.3 us
  starting transfers between devices: 29.8 us -> 35.1 us
    pallas_call x12, Pallas kernels: 56.7 us -> 40.5 us  [the longest x4 14.8 us: down_part(): pl.pallas_call(functools.partial(down_kernel, pieces=m, ins=ins, outs=out...]
    ppermute x7 -> x9, waiting for transfers between devices: 49.5 us -> 37.9 us  [over_y(): lax.ppermute(value, 'dp', [(y * NC + c, (y ^ k) * NC + c) for y in range(...]
    ppermute x2, waiting for transfers between devices: 0.01 us -> 10.5 us  [hop3(): return lax.ppermute(b_mid, 'expert', outward)]
    ppermute x7 -> x8, waiting for transfers between devices: 40.5 us -> 30.5 us  [over_x(): out.append(lax.ppermute(sends[k - 1], 'expert', pairs))]
    ppermute x1, waiting for transfers between devices: 0.19 us -> 3.69 us  [hop1(): lax.ppermute(block, 'expert', ends_first)]
    ppermute x4 -> x6, waiting for transfers between devices: 2.15 us -> 5.64 us  [over_core(): return lax.ppermute(value, 'dp', core_pairs)]
    ppermute x7 -> x9, starting transfers between devices: 8.89 us -> 11.8 us  [over_y(): lax.ppermute(value, 'dp', [(y * NC + c, (y ^ k) * NC + c) for y in range(...]
    ppermute x7 -> x8, starting transfers between devices: 8.68 us -> 10.2 us  [over_x(): out.append(lax.ppermute(sends[k - 1], 'expert', pairs))]
  transfers between devices with their start and end apart: 24 -> 29, of which waited for: 14 -> 18; matrix products, arithmetic and copies ran while one was open for 0% -> 0% of each run, Pallas kernels for 35% -> 31%
where the time goes in v3:
time: 240 us; the launch traced here: 239 us
  waiting for transfers between devices  91.7 us (38%)
  Pallas kernels  84.3 us (35%)
  starting transfers between devices  35.1 us (15%)
  local copies, waits for them, and re-layouts  25.2 us (10%)
    ppermute x9, waiting for transfers between devices, over_y(): lax.ppermute(value, 'dp', [(y * NC + c, (y ^ k) * NC + c) for y in range(...  37.9 us
    ppermute x8, waiting for transfers between devices, over_x(): out.append(lax.ppermute(sends[k - 1], 'expert', pairs))  30.5 us
    pallas_call x8, Pallas kernels, pick_rows(): pl.pallas_call(functools.partial(pick_kernel, nx=nx, top=top, n_meta=len(...  25.6 us
    unnamed x98, local copies, waits for them, and re-layouts  25.1 us
    pallas_call x2, Pallas kernels, both_part(): pl.pallas_call(functools.partial(both_kernel, pieces=m, add=add), grid_sp...  18 us
    pallas_call x4, Pallas kernels, down_part(): pl.pallas_call(functools.partial(down_kernel, pieces=m, ins=ins, outs=out...  14.8 us
    pallas_call x4, Pallas kernels, back(): pl.pallas_call(functools.partial(back_kernel, parts=n), in_specs=whole(n...  13.6 us
    pallas_call x4, Pallas kernels, gate_up(): pl.pallas_call(functools.partial(gate_up_kernel, parts=len(parts), ny=ny)...  12.1 us
  transfers between devices with their start and end apart: 29, of which 18 were waited for; matrix products, arithmetic and copies ran while one was open for 0% of the time, Pallas kernels for 31%

profile of v3, /device:TPU:0, one launch (start us, length us, event | category | flops | bytes accessed | tf_op | source)
XLA Modules:
  0.0 239.4 jit_solution(11178324701945359271)
XLA Ops:
  6.5 4.7 %collective-permute-start.2 = (bf16[256,3712]{1,0:T(8,128)(2,1)S(1)}, bf16[256,3712]{1,0:T(8,128)(2,1)}, u32[]{:S(2)}, u32[]{:S(2)}) collective-permute-start(bf16[256,3712]{1,0:T(8,128)(2,1)S(1)} %pack.1.refs_0_.refs_1_), channel_id=1, source_target_pairs={{0,2},{1,3},{2,0},{3,1},{4,6},{5,7},{6,4},{7,5},{8,10},{9,11},{10,... | collective-permute-start | bytes 5701640 | tf_op jit(solution)/shard_map/ppermute | solution.py:360
  15.9 3.1 %pick.9 = (bf16[80,3584]{1,0:T(8,128)(2,1)S(1)}, bf16[80,3584]{1,0:T(8,128)(2,1)}) custom-call(s32[2,2]{1,0:T(2,128)S(1)} %pad_add_fusion.ids_ref, bf16[256,3712]{1,0:T(8,128)(2,1)S(1)} %pack.1.refs_0_.refs_1_, bf16[256,3712]{1,0:T(8,128)(2,1)S(1)} %pack.1.refs_0_.refs_1_), custom_call_target="tpu_custom_call" | custom-call | flops 3000000000 | bytes 1000 | tf_op jit(solution)/shard_map/pick/pallas_call | solution.py:123
  20.4 10.2 %collective-permute-done.refs_1_ = bf16[80,3584]{1,0:T(8,128)(2,1)S(1)} collective-permute-done((bf16[80,3584]{1,0:T(8,128)(2,1)}, bf16[80,3584]{1,0:T(8,128)(2,1)S(1)}, u32[]{:S(2)}, u32[]{:S(2)}) %collective-permute-start) | collective-permute-done | bytes 573472 | tf_op jit(solution)/shard_map/ppermute | solution.py:372
  41.2 3.1 %copy-done.28 = bf16[1,1024,3584]{2,1,0:T(8,128)(2,1)S(1)} copy-done((bf16[1,1024,3584]{2,1,0:T(8,128)(2,1)S(1)}, bf16[1,1024,3584]{2,1,0:T(8,128)(2,1)}, u32[]{:S(2)}) %copy-start.28) | copy-done | bytes 7340056
  44.3 3.7 %back.4 = (bf16[160,2048]{1,0:T(8,128)(2,1)S(1)}, bf16[160,1024]{1,0:T(8,128)(2,1)S(1)}, bf16[160,3584]{1,0:T(8,128)(2,1)S(1)}) custom-call(bf16[80,3584]{1,0:T(8,128)(2,1)S(1)} %copy-done.41, bf16[80,3584]{1,0:T(8,128)(2,1)} %collective-permute-done.4.refs_1_, bf16[1,1024,3584]{2,1,0:T(8,128)(2,1)S(1)} %copy-done.28, ...), custom_call_target="tpu_custom_call" | custom-call | flops 3000000000 | bytes 1000 | tf_op jit(solution)/shard_map/back/pallas_call | solution.py:205
  48.7 3.7 %collective-permute-done.2.refs_0_.refs_1_ = bf16[256,3712]{1,0:T(8,128)(2,1)} collective-permute-done((bf16[256,3712]{1,0:T(8,128)(2,1)S(1)}, bf16[256,3712]{1,0:T(8,128)(2,1)}, u32[]{:S(2)}, u32[]{:S(2)}) %collective-permute-start.2) | collective-permute-done | bytes 1900576 | tf_op jit(solution)/shard_map/ppermute | solution.py:360
  56.6 3.9 %pick.10 = (bf16[80,3584]{1,0:T(8,128)(2,1)S(1)}, bf16[80,3584]{1,0:T(8,128)(2,1)S(1)}) custom-call(s32[2,2]{1,0:T(2,128)S(1)} %pad_add_fusion.ids_ref, bf16[256,3712]{1,0:T(8,128)(2,1)} %collective-permute-done.2.refs_0_.refs_1_, bf16[256,3712]{1,0:T(8,128)(2,1)} %collective-permute-done.2.refs_0_.refs_1_), custom_call_target="tpu_custom_call" | custom-call | flops 3000000000 | bytes 1000 | tf_op jit(solution)/shard_map/pick/pallas_call | solution.py:123
  62.1 3.4 %pick.11 = (bf16[80,3584]{1,0:T(8,128)(2,1)S(1)}, bf16[80,3584]{1,0:T(8,128)(2,1)S(1)}) custom-call(s32[2,2]{1,0:T(2,128)S(1)} %pad_add_fusion.ids_ref, bf16[256,3712]{1,0:T(8,128)(2,1)} %collective-permute-done.2.refs_0_.refs_1_, bf16[256,3712]{1,0:T(8,128)(2,1)} %collective-permute-done.2.refs_0_.refs_1_), custom_call_target="tpu_custom_call" | custom-call | flops 3000000000 | bytes 1000 | tf_op jit(solution)/shard_map/pick/pallas_call | solution.py:123
  65.5 5.0 %collective-permute-done.1.refs_1_ = bf16[160,1792]{1,0:T(8,128)(2,1)S(1)} collective-permute-done((bf16[160,1792]{1,0:T(8,128)(2,1)S(1)}, bf16[160,1792]{1,0:T(8,128)(2,1)S(1)}, u32[]{:S(2)}, u32[]{:S(2)}) %collective-permute-start.1) | collective-permute-done | bytes 573472 | tf_op jit(solution)/shard_map/ppermute | solution.py:381
  72.0 4.6 %collective-permute-done.5.refs_1_ = bf16[80,3584]{1,0:T(8,128)(2,1)S(1)} collective-permute-done((bf16[80,3584]{1,0:T(8,128)(2,1)S(1)}, bf16[80,3584]{1,0:T(8,128)(2,1)S(1)}, u32[]{:S(2)}, u32[]{:S(2)}) %collective-permute-start.5) | collective-permute-done | bytes 573472 | tf_op jit(solution)/shard_map/ppermute | solution.py:372
  76.5 5.9 %collective-permute-done.10.refs_9_ = bf16[160,2048]{1,0:T(8,128)(2,1)S(1)} collective-permute-done((bf16[160,2048]{1,0:T(8,128)(2,1)S(1)}, bf16[160,2048]{1,0:T(8,128)(2,1)S(1)}, u32[]{:S(2)}, u32[]{:S(2)}) %collective-permute-start.10) | collective-permute-done | bytes 655392 | tf_op jit(solution)/shard_map/ppermute | solution.py:381
  82.5 3.7 %collective-permute-done.9.refs_1_ = bf16[80,3584]{1,0:T(8,128)(2,1)S(1)} collective-permute-done((bf16[80,3584]{1,0:T(8,128)(2,1)S(1)}, bf16[80,3584]{1,0:T(8,128)(2,1)S(1)}, u32[]{:S(2)}, u32[]{:S(2)}) %collective-permute-start.9) | collective-permute-done | bytes 573472 | tf_op jit(solution)/shard_map/ppermute | solution.py:372
  93.3 3.5 %collective-permute-done.7.refs_0_.refs_2_ = bf16[256,3712]{1,0:T(8,128)(2,1)S(1)} collective-permute-done((bf16[256,3712]{1,0:T(8,128)(2,1)}, bf16[256,3712]{1,0:T(8,128)(2,1)S(1)}, u32[]{:S(2)}, u32[]{:S(2)}) %collective-permute-start.7) | collective-permute-done | bytes 1900576 | tf_op jit(solution)/shard_map/ppermute | solution.py:363
  109.0 7.6 %collective-permute-done.11.refs_1_ = bf16[80,3584]{1,0:T(8,128)(2,1)S(1)} collective-permute-done((bf16[80,3584]{1,0:T(8,128)(2,1)S(1)}, bf16[80,3584]{1,0:T(8,128)(2,1)S(1)}, u32[]{:S(2)}, u32[]{:S(2)}) %collective-permute-start.11) | collective-permute-done | bytes 573472 | tf_op jit(solution)/shard_map/ppermute | solution.py:372
  116.5 3.3 %gate_up.6 = (f32[160,1024]{1,0:T(8,128)S(1)}, f32[160,1024]{1,0:T(8,128)S(1)}, bf16[160,1792]{1,0:T(8,128)(2,1)S(1)}, bf16[160,1792]{1,0:T(8,128)(2,1)}) custom-call(s32[1]{0:T(128)} %bitcast.1.y_ref, bf16[80,3584]{1,0:T(8,128)(2,1)S(1)} %get-tuple-element.99.refs_0_, bf16[80,3584]{1,0:T(8,128)(2,1)S(1)} %collective-permute-done.11.refs_1_, ...), custom_call_target="tpu_custom_call" | custom-call | flops 3000000000 | bytes 1000 | tf_op jit(solution)/shard_map/gate_up/pallas_call | solution.py:170
  119.8 4.0 %collective-permute-done.13.refs_1_.refs_3_ = bf16[128,3712]{1,0:T(8,128)(2,1)S(1)} collective-permute-done((bf16[128,3712]{1,0:T(8,128)(2,1)S(1)}, bf16[128,3712]{1,0:T(8,128)(2,1)S(1)}, u32[]{:S(2)}, u32[]{:S(2)}) %collective-permute-start.13) | collective-permute-done | bytes 950304 | tf_op jit(solution)/shard_map/ppermute | solution.py:366
  123.9 3.1 %pick.14 = (bf16[80,3584]{1,0:T(8,128)(2,1)S(1)}, bf16[80,3584]{1,0:T(8,128)(2,1)S(1)}) custom-call(s32[2,2]{1,0:T(2,128)S(1)} %pad_add_fusion.ids_ref, bf16[256,3712]{1,0:T(8,128)(2,1)} %collective-permute-done.3.refs_0_.refs_2_, bf16[128,3712]{1,0:T(8,128)(2,1)S(1)} %collective-permute-done.13.refs_1_.refs_3_, ...), custom_call_target="tpu_custom_call" | custom-call | flops 3000000000 | bytes 1000 | tf_op jit(solution)/shard_map/pick/pallas_call | solution.py:123
  130.1 3.5 %back.6 = (bf16[160,2048]{1,0:T(8,128)(2,1)}, bf16[160,1024]{1,0:T(8,128)(2,1)S(1)}, bf16[160,3584]{1,0:T(8,128)(2,1)S(1)}) custom-call(bf16[80,3584]{1,0:T(8,128)(2,1)S(1)} %get-tuple-element.103.refs_0_, bf16[80,3584]{1,0:T(8,128)(2,1)S(1)} %collective-permute-done.16.refs_1_, bf16[1,1024,3584]{2,1,0:T(8,128)(2,1)S(1)} %bitcast.14, ...), custom_call_target="tpu_custom_call" | custom-call | flops 3000000000 | bytes 1000 | tf_op jit(solution)/shard_map/back/pallas_call | solution.py:205
  134.1 6.4 %collective-permute-done.15.refs_3_ = bf16[128,3584]{1,0:T(8,128)(2,1)S(1)} collective-permute-done((bf16[128,3584]{1,0:T(8,128)(2,1)S(1)}, bf16[128,3584]{1,0:T(8,128)(2,1)S(1)}, u32[]{:S(2)}, u32[]{:S(2)}) %collective-permute-start.15) | collective-permute-done | bytes 917536 | tf_op jit(solution)/shard_map/ppermute | solution.py:366
  140.6 4.1 %pick.15 = (bf16[80,3584]{1,0:T(8,128)(2,1)S(1)}, bf16[80,3584]{1,0:T(8,128)(2,1)}) custom-call(s32[2,2]{1,0:T(2,128)S(1)} %pad_add_fusion.ids_ref, bf16[256,3712]{1,0:T(8,128)(2,1)} %collective-permute-done.3.refs_0_.refs_2_, bf16[128,3712]{1,0:T(8,128)(2,1)S(1)} %collective-permute-done.13.refs_1_.refs_3_, ...), custom_call_target="tpu_custom_call" | custom-call | flops 3000000000 | bytes 1000 | tf_op jit(solution)/shard_map/pick/pallas_call | solution.py:123
  146.2 3.3 %gate_up.7 = (f32[160,1024]{1,0:T(8,128)S(1)}, f32[160,1024]{1,0:T(8,128)S(1)}, bf16[160,1792]{1,0:T(8,128)(2,1)S(1)}, bf16[160,1792]{1,0:T(8,128)(2,1)}) custom-call(s32[1]{0:T(128)} %bitcast.1.y_ref, bf16[80,3584]{1,0:T(8,128)(2,1)S(1)} %get-tuple-element.110.refs_0_, bf16[80,3584]{1,0:T(8,128)(2,1)S(1)} %collective-permute-done.14.refs_1_, ...), custom_call_target="tpu_custom_call" | custom-call | flops 3000000000 | bytes 1000 | tf_op jit(solution)/shard_map/gate_up/pallas_call | solution.py:170
  153.6 3.5 %collective-permute-done.19.refs_1_ = bf16[80,3584]{1,0:T(8,128)(2,1)} collective-permute-done((bf16[80,3584]{1,0:T(8,128)(2,1)}, bf16[80,3584]{1,0:T(8,128)(2,1)}, u32[]{:S(2)}, u32[]{:S(2)}) %collective-permute-start.19) | collective-permute-done | bytes 573472 | tf_op jit(solution)/shard_map/ppermute | solution.py:372
  157.1 7.1 %collective-permute-done.18.refs_7_ = bf16[160,1792]{1,0:T(8,128)(2,1)} collective-permute-done((bf16[160,1792]{1,0:T(8,128)(2,1)}, bf16[160,1792]{1,0:T(8,128)(2,1)}, u32[]{:S(2)}, u32[]{:S(2)}) %collective-permute-start.18) | collective-permute-done | bytes 573472 | tf_op jit(solution)/shard_map/ppermute | solution.py:381
  170.6 3.7 %back.7 = (bf16[160,2048]{1,0:T(8,128)(2,1)S(1)}, bf16[160,1024]{1,0:T(8,128)(2,1)S(1)}, bf16[160,3584]{1,0:T(8,128)(2,1)S(1)}) custom-call(bf16[80,3584]{1,0:T(8,128)(2,1)S(1)} %copy-done.39, bf16[80,3584]{1,0:T(8,128)(2,1)} %collective-permute-done.19.refs_1_, bf16[1,1024,3584]{2,1,0:T(8,128)(2,1)S(1)} %copy-done.29, f32[160,1024]{1,0:T(8,128)S(1)} %copy-done.33, ...), custom_call_target="tpu_custom_call" | custom-call | flops 3000000000 | bytes 1000 | tf_op jit(solution)/shard_map/back/pallas_call | solution.py:205
  174.3 3.4 %down_part.5 = bf16[256,3584]{1,0:T(8,128)(2,1)S(1)} custom-call(s32[1]{0:T(128)S(6)} %add.53.s_ref, bf16[160,1024]{1,0:T(8,128)(2,1)S(1)} %copy-done.23, bf16[160,1024]{1,0:T(8,128)(2,1)S(1)} %copy-done.25, bf16[160,1024]{1,0:T(8,128)(2,1)S(1)} %copy-done.27, bf16[160,1024]{1,0:T(8,128)(2,1)S(1)} %get-tuple-element.128.refs_3_, ...), custom_call_target="tpu_custom_call" | custom-call | flops 3000000000 | bytes 1000 | tf_op jit(solution)/shard_map/down_part/pallas_call | solution.py:258
  177.7 3.4 %down_part.4 = bf16[256,3584]{1,0:T(8,128)(2,1)S(1)} custom-call(s32[1]{0:T(128)S(6)} %add.52.s_ref, bf16[160,1024]{1,0:T(8,128)(2,1)S(1)} %copy-done.23, bf16[160,1024]{1,0:T(8,128)(2,1)S(1)} %copy-done.25, bf16[160,1024]{1,0:T(8,128)(2,1)S(1)} %copy-done.27, bf16[160,1024]{1,0:T(8,128)(2,1)S(1)} %get-tuple-element.128.refs_3_, ...), custom_call_target="tpu_custom_call" | custom-call | flops 3000000000 | bytes 1000 | tf_op jit(solution)/shard_map/down_part/pallas_call | solution.py:258
  187.6 4.0 %down_part.6 = bf16[256,3584]{1,0:T(8,128)(2,1)S(1)} custom-call(s32[1]{0:T(128)S(6)} %add.51.s_ref, bf16[160,1024]{1,0:T(8,128)(2,1)S(1)} %copy-done.23, bf16[160,1024]{1,0:T(8,128)(2,1)S(1)} %copy-done.25, bf16[160,1024]{1,0:T(8,128)(2,1)S(1)} %copy-done.27, bf16[160,1024]{1,0:T(8,128)(2,1)S(1)} %get-tuple-element.128.refs_3_, ...), custom_call_target="tpu_custom_call" | custom-call | flops 3000000000 | bytes 1000 | tf_op jit(solution)/shard_map/down_part/pallas_call | solution.py:258
  193.2 6.1 %collective-permute-done.23.refs_15_ = bf16[160,2048]{1,0:T(8,128)(2,1)S(1)} collective-permute-done((bf16[160,2048]{1,0:T(8,128)(2,1)S(1)}, bf16[160,2048]{1,0:T(8,128)(2,1)S(1)}, u32[]{:S(2)}, u32[]{:S(2)}) %collective-permute-start.23) | collective-permute-done | bytes 655392 | tf_op jit(solution)/shard_map/ppermute | solution.py:381
  199.4 7.9 %both_part.2 = (bf16[896,512]{1,0:T(8,128)(2,1)S(1)}, bf16[896,512]{1,0:T(8,128)(2,1)S(1)}, bf16[896,512]{1,0:T(8,128)(2,1)S(1)}, bf16[896,512]{1,0:T(8,128)(2,1)S(1)}) custom-call(s32[1]{0:T(128)S(6)} %sub.14.c_ref, bf16[160,1792]{1,0:T(8,128)(2,1)S(1)} %copy-done.11, bf16[160,1792]{1,0:T(8,128)(2,1)S(1)} %copy-done.13, bf16[160,1792]{1,0:T(8,128)(2,1)S(1)} %copy-done.15, ...), custom_call_target="tpu_custom_call" | custom-call | flops 3000000000 | bytes 1000 | tf_op jit(solution)/shard_map/both_part/pallas_call | solution.py:317
  208.4 4.0 %down_part.7 = f32[256,3584]{1,0:T(8,128)S(1)} custom-call(s32[1]{0:T(128)S(6)} %add.54.s_ref, bf16[160,1024]{1,0:T(8,128)(2,1)S(1)} %copy-done.23, bf16[160,1024]{1,0:T(8,128)(2,1)S(1)} %copy-done.25, bf16[160,1024]{1,0:T(8,128)(2,1)S(1)} %copy-done.27, bf16[160,1024]{1,0:T(8,128)(2,1)S(1)} %get-tuple-element.128.refs_3_, ...), custom_call_target="tpu_custom_call" | custom-call | flops 3000000000 | bytes 1000 | tf_op jit(solution)/shard_map/down_part/pallas_call | solution.py:258
  213.8 10.1 %both_part.3 = (bf16[896,1024]{1,0:T(8,128)(2,1)}, bf16[896,1024]{1,0:T(8,128)(2,1)}) custom-call(s32[1]{0:T(128)} %bitcast.c_ref, bf16[160,1792]{1,0:T(8,128)(2,1)S(1)} %copy-done.11, bf16[160,1792]{1,0:T(8,128)(2,1)S(1)} %copy-done.13, bf16[160,1792]{1,0:T(8,128)(2,1)S(1)} %copy-done.15, bf16[160,1792]{1,0:T(8,128)(2,1)S(1)} %copy-done.17, ...), custom_call_target="tpu_custom_call" | custom-call | flops 3000000000 | bytes 1000 | tf_op jit(solution)/shard_map/both_part/pallas_call | solution.py:317
  223.9 13.8 %collective-permute-done.28 = bf16[256,3584]{1,0:T(8,128)(2,1)S(1)} collective-permute-done((bf16[256,3584]{1,0:T(8,128)(2,1)S(1)}, bf16[256,3584]{1,0:T(8,128)(2,1)S(1)}, u32[]{:S(2)}, u32[]{:S(2)}) %collective-permute-start.28) | collective-permute-done | bytes 1835040 | tf_op jit(solution)/shard_map/ppermute | solution.py:381
  (157 shorter events, 77.2 us)
Async XLA Ops:
  4.6 44.1 %collective-permute-start.3 = (bf16[256,3712]{1,0:T(8,128)(2,1)S(1)}, bf16[256,3712]{1,0:T(8,128)(2,1)}, u32[]{:S(2)}, u32[]{:S(2)}) collective-permute-start(bf16[256,3712]{1,0:T(8,128)(2,1)S(1)} %pack.1.refs_0_.refs_1_), channel_id=1, source_target_pairs={{2,4},{3,5},{4,2},{5,3},{10,12},{11,13},{12,10},{13,11},{18,20},{1... | collective-permute-start | bytes 5701640 | tf_op jit(solution)/shard_map/ppermute | solution.py:360
  6.5 45.9 %collective-permute-start.2 = (bf16[256,3712]{1,0:T(8,128)(2,1)S(1)}, bf16[256,3712]{1,0:T(8,128)(2,1)}, u32[]{:S(2)}, u32[]{:S(2)}) collective-permute-start(bf16[256,3712]{1,0:T(8,128)(2,1)S(1)} %pack.1.refs_0_.refs_1_), channel_id=1, source_target_pairs={{0,2},{1,3},{2,0},{3,1},{4,6},{5,7},{6,4},{7,5},{8,10},{9,11},{10,... | collective-permute-start | bytes 5701640 | tf_op jit(solution)/shard_map/ppermute | solution.py:360
  14.4 16.1 %collective-permute-start = (bf16[80,3584]{1,0:T(8,128)(2,1)}, bf16[80,3584]{1,0:T(8,128)(2,1)S(1)}, u32[]{:S(2)}, u32[]{:S(2)}) collective-permute-start(bf16[80,3584]{1,0:T(8,128)(2,1)} %get-tuple-element.74), channel_id=1, source_target_pairs={{0,1},{1,0},{2,3},{3,2},{4,5},{5,4},{6,7},{7,6},{8,9},{9,8},{10,11... | collective-permute-start | bytes 1720328 | tf_op jit(solution)/shard_map/ppermute | solution.py:372
  19.9 21.3 %collective-permute-start.4 = (bf16[80,3584]{1,0:T(8,128)(2,1)}, bf16[80,3584]{1,0:T(8,128)(2,1)}, u32[]{:S(2)}, u32[]{:S(2)}) collective-permute-start(bf16[80,3584]{1,0:T(8,128)(2,1)} %get-tuple-element.79), channel_id=1, source_target_pairs={{0,1},{1,0},{2,3},{3,2},{4,5},{5,4},{6,7},{7,6},{8,9},{9,8},{10,11... | collective-permute-start | bytes 1720328 | tf_op jit(solution)/shard_map/ppermute | solution.py:372
  52.4 44.4 %collective-permute-start.7 = (bf16[256,3712]{1,0:T(8,128)(2,1)}, bf16[256,3712]{1,0:T(8,128)(2,1)S(1)}, u32[]{:S(2)}, u32[]{:S(2)}) collective-permute-start(bf16[256,3712]{1,0:T(8,128)(2,1)} %collective-permute-done.3.refs_0_.refs_2_), channel_id=1, source_target_pairs={{2,0},{3,1},{4,6},{5,7},{10,8},{11,9},{12,14},{13,15},{18,16},{19,... | collective-permute-start | bytes 5701640 | tf_op jit(solution)/shard_map/ppermute | solution.py:363
  53.7 43.1 %collective-permute-start.8 = (bf16[256,3712]{1,0:T(8,128)(2,1)}, bf16[256,3712]{1,0:T(8,128)(2,1)S(1)}, u32[]{:S(2)}, u32[]{:S(2)}) collective-permute-start(bf16[256,3712]{1,0:T(8,128)(2,1)} %collective-permute-done.2.refs_0_.refs_1_), channel_id=1, source_target_pairs={{2,4},{3,5},{4,2},{5,3},{10,12},{11,13},{12,10},{13,11},{18,20},{1... | collective-permute-start | bytes 5701640 | tf_op jit(solution)/shard_map/ppermute | solution.py:363
  54.5 16.0 %collective-permute-start.1 = (bf16[160,1792]{1,0:T(8,128)(2,1)S(1)}, bf16[160,1792]{1,0:T(8,128)(2,1)S(1)}, u32[]{:S(2)}, u32[]{:S(2)}) collective-permute-start(bf16[160,1792]{1,0:T(8,128)(2,1)S(1)} %get-tuple-element.76), channel_id=1, source_target_pairs={{0,16},{8,24},{16,0},{24,8},{1,17},{9,25},{17,1},{25,9},{2,18},{10... | collective-permute-start | bytes 1720328 | tf_op jit(solution)/shard_map/ppermute | solution.py:381
  56.1 26.4 %collective-permute-start.10 = (bf16[160,2048]{1,0:T(8,128)(2,1)S(1)}, bf16[160,2048]{1,0:T(8,128)(2,1)S(1)}, u32[]{:S(2)}, u32[]{:S(2)}) collective-permute-start(bf16[160,2048]{1,0:T(8,128)(2,1)S(1)} %get-tuple-element.134.refs_8_), channel_id=1, source_target_pairs={{0,16},{8,24},{16,0},{24,8},{1,17},{9,25},{17,1},{25,9},{2,18},{10... | collective-permute-start | bytes 1966088 | tf_op jit(solution)/shard_map/ppermute | solution.py:381
  56.6 29.6 %slice-start = ((s8[7340032]{0:T(1024)(128)(4,1)}), s8[4194304]{0:T(1024)(128)(4,1)S(1)}, s32[]{:S(2)}) async-start(s8[7340032]{0:T(1024)(128)(4,1)} %bitcast.9), calls=%async_computation | async-start | bytes 8388608
  56.6 29.6 %slice-start.2 = ((s8[7340032]{0:T(1024)(128)(4,1)}), s8[4194304]{0:T(1024)(128)(4,1)S(1)}, s32[]{:S(2)}) async-start(s8[7340032]{0:T(1024)(128)(4,1)} %bitcast.11), calls=%async_computation.2 | async-start | bytes 8388608
  60.5 25.7 %slice-start.1 = ((s8[7340032]{0:T(1024)(128)(4,1)}), s8[3145728]{0:T(1024)(128)(4,1)S(1)}, s32[]{:S(2)}) async-start(s8[7340032]{0:T(1024)(128)(4,1)} %bitcast.9), calls=%async_computation.1 | async-start | bytes 6291456
  60.5 16.0 %collective-permute-start.5 = (bf16[80,3584]{1,0:T(8,128)(2,1)S(1)}, bf16[80,3584]{1,0:T(8,128)(2,1)S(1)}, u32[]{:S(2)}, u32[]{:S(2)}) collective-permute-start(bf16[80,3584]{1,0:T(8,128)(2,1)S(1)} %get-tuple-element.85), channel_id=1, source_target_pairs={{0,1},{1,0},{2,3},{3,2},{4,5},{5,4},{6,7},{7,6},{8,9},{9,8},{10,11... | collective-permute-start | bytes 1720328 | tf_op jit(solution)/shard_map/ppermute | solution.py:372
  70.5 15.7 %collective-permute-start.9 = (bf16[80,3584]{1,0:T(8,128)(2,1)S(1)}, bf16[80,3584]{1,0:T(8,128)(2,1)S(1)}, u32[]{:S(2)}, u32[]{:S(2)}) collective-permute-start(bf16[80,3584]{1,0:T(8,128)(2,1)S(1)} %get-tuple-element.92), channel_id=1, source_target_pairs={{0,1},{1,0},{2,3},{3,2},{4,5},{5,4},{6,7},{7,6},{8,9},{9,8},{10,11... | collective-permute-start | bytes 1720328 | tf_op jit(solution)/shard_map/ppermute | solution.py:372
  89.0 18.6 %collective-permute-start.6 = (bf16[160,1792]{1,0:T(8,128)(2,1)S(1)}, bf16[160,1792]{1,0:T(8,128)(2,1)S(1)}, u32[]{:S(2)}, u32[]{:S(2)}) collective-permute-start(bf16[160,1792]{1,0:T(8,128)(2,1)S(1)} %get-tuple-element.90), channel_id=1, source_target_pairs={{0,16},{8,24},{16,0},{24,8},{1,17},{9,25},{17,1},{25,9},{2,18},{10... | collective-permute-start | bytes 1720328 | tf_op jit(solution)/shard_map/ppermute | solution.py:381
  96.9 27.0 %collective-permute-start.13 = (bf16[128,3712]{1,0:T(8,128)(2,1)S(1)}, bf16[128,3712]{1,0:T(8,128)(2,1)S(1)}, u32[]{:S(2)}, u32[]{:S(2)}) collective-permute-start(bf16[128,3712]{1,0:T(8,128)(2,1)S(1)} %slice.8), channel_id=1, source_target_pairs={{2,0},{3,1},{4,6},{5,7},{10,8},{11,9},{12,14},{13,15},{18,16},{19,... | collective-permute-start | bytes 2850824 | tf_op jit(solution)/shard_map/ppermute | solution.py:366
  100.5 16.0 %collective-permute-start.11 = (bf16[80,3584]{1,0:T(8,128)(2,1)S(1)}, bf16[80,3584]{1,0:T(8,128)(2,1)S(1)}, u32[]{:S(2)}, u32[]{:S(2)}) collective-permute-start(bf16[80,3584]{1,0:T(8,128)(2,1)S(1)} %get-tuple-element.100), channel_id=1, source_target_pairs={{0,1},{1,0},{2,3},{3,2},{4,5},{5,4},{6,7},{7,6},{8,9},{9,8},{10,11... | collective-permute-start | bytes 1720328 | tf_op jit(solution)/shard_map/ppermute | solution.py:372
  102.1 28.0 %collective-permute-start.17 = (bf16[160,2048]{1,0:T(8,128)(2,1)S(1)}, bf16[160,2048]{1,0:T(8,128)(2,1)S(1)}, u32[]{:S(2)}, u32[]{:S(2)}) collective-permute-start(bf16[160,2048]{1,0:T(8,128)(2,1)S(1)} %get-tuple-element.96.refs_10_), channel_id=1, source_target_pairs={{0,16},{8,24},{16,0},{24,8},{1,17},{9,25},{17,1},{25,9},{2,18},{10... | collective-permute-start | bytes 1966088 | tf_op jit(solution)/shard_map/ppermute | solution.py:381
  103.7 36.9 %collective-permute-start.15 = (bf16[128,3584]{1,0:T(8,128)(2,1)S(1)}, bf16[128,3584]{1,0:T(8,128)(2,1)S(1)}, u32[]{:S(2)}, u32[]{:S(2)}) collective-permute-start(bf16[128,3584]{1,0:T(8,128)(2,1)S(1)} %slice.9), channel_id=1, source_target_pairs={{2,0},{3,1},{4,6},{5,7},{10,8},{11,9},{12,14},{13,15},{18,16},{19,... | collective-permute-start | bytes 2752520 | tf_op jit(solution)/shard_map/ppermute | solution.py:366
  108.4 21.7 %collective-permute-start.16 = (bf16[80,3584]{1,0:T(8,128)(2,1)S(1)}, bf16[80,3584]{1,0:T(8,128)(2,1)S(1)}, u32[]{:S(2)}, u32[]{:S(2)}) collective-permute-start(bf16[80,3584]{1,0:T(8,128)(2,1)S(1)} %get-tuple-element.112), channel_id=1, source_target_pairs={{0,1},{1,0},{2,3},{3,2},{4,5},{5,4},{6,7},{7,6},{8,9},{9,8},{10,11... | collective-permute-start | bytes 1720328 | tf_op jit(solution)/shard_map/ppermute | solution.py:372
  127.0 19.2 %collective-permute-start.14 = (bf16[80,3584]{1,0:T(8,128)(2,1)S(1)}, bf16[80,3584]{1,0:T(8,128)(2,1)S(1)}, u32[]{:S(2)}, u32[]{:S(2)}) collective-permute-start(bf16[80,3584]{1,0:T(8,128)(2,1)S(1)} %get-tuple-element.111), channel_id=1, source_target_pairs={{0,1},{1,0},{2,3},{3,2},{4,5},{5,4},{6,7},{7,6},{8,9},{9,8},{10,11... | collective-permute-start | bytes 1720328 | tf_op jit(solution)/shard_map/ppermute | solution.py:372
  128.6 25.0 %collective-permute-start.12 = (bf16[160,1792]{1,0:T(8,128)(2,1)}, bf16[160,1792]{1,0:T(8,128)(2,1)}, u32[]{:S(2)}, u32[]{:S(2)}) collective-permute-start(bf16[160,1792]{1,0:T(8,128)(2,1)} %get-tuple-element.106), channel_id=1, source_target_pairs={{0,16},{8,24},{16,0},{24,8},{1,17},{9,25},{17,1},{25,9},{2,18},{10... | collective-permute-start | bytes 1720328 | tf_op jit(solution)/shard_map/ppermute | solution.py:381
  133.6 23.5 %collective-permute-start.20 = (bf16[160,2048]{1,0:T(8,128)(2,1)}, bf16[160,2048]{1,0:T(8,128)(2,1)}, u32[]{:S(2)}, u32[]{:S(2)}) collective-permute-start(bf16[160,2048]{1,0:T(8,128)(2,1)} %get-tuple-element.115.refs_12_), channel_id=1, source_target_pairs={{0,16},{8,24},{16,0},{24,8},{1,17},{9,25},{17,1},{25,9},{2,18},{10... | collective-permute-start | bytes 1966088 | tf_op jit(solution)/shard_map/ppermute | solution.py:381
  144.7 12.4 %collective-permute-start.19 = (bf16[80,3584]{1,0:T(8,128)(2,1)}, bf16[80,3584]{1,0:T(8,128)(2,1)}, u32[]{:S(2)}, u32[]{:S(2)}) collective-permute-start(bf16[80,3584]{1,0:T(8,128)(2,1)} %get-tuple-element.124), channel_id=1, source_target_pairs={{0,1},{1,0},{2,3},{3,2},{4,5},{5,4},{6,7},{7,6},{8,9},{9,8},{10,11... | collective-permute-start | bytes 1720328 | tf_op jit(solution)/shard_map/ppermute | solution.py:372
  152.1 12.2 %collective-permute-start.18 = (bf16[160,1792]{1,0:T(8,128)(2,1)}, bf16[160,1792]{1,0:T(8,128)(2,1)}, u32[]{:S(2)}, u32[]{:S(2)}) collective-permute-start(bf16[160,1792]{1,0:T(8,128)(2,1)} %get-tuple-element.120), channel_id=1, source_target_pairs={{0,16},{8,24},{16,0},{24,8},{1,17},{9,25},{17,1},{25,9},{2,18},{10... | collective-permute-start | bytes 1720328 | tf_op jit(solution)/shard_map/ppermute | solution.py:381
  181.1 3.9 %collective-permute-start.21 = (bf16[256,3584]{1,0:T(8,128)(2,1)S(1)}, bf16[256,3584]{1,0:T(8,128)(2,1)S(1)}, u32[]{:S(2)}, u32[]{:S(2)}) collective-permute-start(bf16[256,3584]{1,0:T(8,128)(2,1)S(1)} %down_part.4), channel_id=1, source_target_pairs={{0,8},{8,0},{16,24},{24,16},{1,9},{9,1},{17,25},{25,17},{2,10},{10... | collective-permute-start | bytes 5505032 | tf_op jit(solution)/shard_map/ppermute | solution.py:378
  181.2 6.4 %collective-permute-start.22 = (bf16[256,3584]{1,0:T(8,128)(2,1)S(1)}, bf16[256,3584]{1,0:T(8,128)(2,1)S(1)}, u32[]{:S(2)}, u32[]{:S(2)}) collective-permute-start(bf16[256,3584]{1,0:T(8,128)(2,1)S(1)} %down_part.5), channel_id=1, source_target_pairs={{0,8},{8,0},{16,24},{24,16},{1,9},{9,1},{17,25},{25,17},{2,10},{10... | collective-permute-start | bytes 5505032 | tf_op jit(solution)/shard_map/ppermute | solution.py:378
  181.7 17.6 %collective-permute-start.23 = (bf16[160,2048]{1,0:T(8,128)(2,1)S(1)}, bf16[160,2048]{1,0:T(8,128)(2,1)S(1)}, u32[]{:S(2)}, u32[]{:S(2)}) collective-permute-start(bf16[160,2048]{1,0:T(8,128)(2,1)S(1)} %get-tuple-element.135.refs_14_), channel_id=1, source_target_pairs={{0,16},{8,24},{16,0},{24,8},{1,17},{9,25},{17,1},{25,9},{2,18},{10... | collective-permute-start | bytes 1966088 | tf_op jit(solution)/shard_map/ppermute | solution.py:381
  191.6 46.1 %collective-permute-start.28 = (bf16[256,3584]{1,0:T(8,128)(2,1)S(1)}, bf16[256,3584]{1,0:T(8,128)(2,1)S(1)}, u32[]{:S(2)}, u32[]{:S(2)}) collective-permute-start(bf16[256,3584]{1,0:T(8,128)(2,1)S(1)} %down_part.6), channel_id=1, source_target_pairs={{0,16},{8,24},{16,0},{24,8},{1,17},{9,25},{17,1},{25,9},{2,18},{10... | collective-permute-start | bytes 5505032 | tf_op jit(solution)/shard_map/ppermute | solution.py:381
  207.3 5.1 %collective-permute-start.24 = (bf16[896,512]{1,0:T(8,128)(2,1)S(1)}, bf16[896,512]{1,0:T(8,128)(2,1)S(1)}, u32[]{:S(2)}, u32[]{:S(2)}) collective-permute-start(bf16[896,512]{1,0:T(8,128)(2,1)S(1)} %get-tuple-element.136), channel_id=1, source_target_pairs={{0,8},{8,0},{16,24},{24,16},{1,9},{9,1},{17,25},{25,17},{2,10},{10... | collective-permute-start | bytes 2752520 | tf_op jit(solution)/shard_map/ppermute | solution.py:378
  207.4 5.1 %collective-permute-start.25 = (bf16[896,512]{1,0:T(8,128)(2,1)S(1)}, bf16[896,512]{1,0:T(8,128)(2,1)S(1)}, u32[]{:S(2)}, u32[]{:S(2)}) collective-permute-start(bf16[896,512]{1,0:T(8,128)(2,1)S(1)} %get-tuple-element.137), channel_id=1, source_target_pairs={{0,8},{8,0},{16,24},{24,16},{1,9},{9,1},{17,25},{25,17},{2,10},{10... | collective-permute-start | bytes 2752520 | tf_op jit(solution)/shard_map/ppermute | solution.py:378
  207.9 4.6 %collective-permute-start.26 = (bf16[896,512]{1,0:T(8,128)(2,1)S(1)}, bf16[896,512]{1,0:T(8,128)(2,1)S(1)}, u32[]{:S(2)}, u32[]{:S(2)}) collective-permute-start(bf16[896,512]{1,0:T(8,128)(2,1)S(1)} %get-tuple-element.138), channel_id=1, source_target_pairs={{0,8},{8,0},{16,24},{24,16},{1,9},{9,1},{17,25},{25,17},{2,10},{10... | collective-permute-start | bytes 2752520 | tf_op jit(solution)/shard_map/ppermute | solution.py:378
  207.9 5.8 %collective-permute-start.27 = (bf16[896,512]{1,0:T(8,128)(2,1)S(1)}, bf16[896,512]{1,0:T(8,128)(2,1)S(1)}, u32[]{:S(2)}, u32[]{:S(2)}) collective-permute-start(bf16[896,512]{1,0:T(8,128)(2,1)S(1)} %get-tuple-element.139), channel_id=1, source_target_pairs={{0,8},{8,0},{16,24},{24,16},{1,9},{9,1},{17,25},{25,17},{2,10},{10... | collective-permute-start | bytes 2752520 | tf_op jit(solution)/shard_map/ppermute | solution.py:378
  (46 other events, 346.1 us)

commit v4 on v3

--- a/solution.py
+++ b/solution.py
@@ -215,6 +215,43 @@
         cost_estimate=COST,
         name="back",
     )(*parts, w_down, gate, up)
+
+
+def sends_kernel(s_ref, *refs, pieces):
+    lefts, cots, refs = refs[: 2 * pieces], refs[2 * pieces : 3 * pieces], refs[3 * pieces :]
+    outs, (left, right) = refs[:2], refs[2:]
+    rows = cots[0].shape[0]
+    for k in range(pieces):
+        right[k * rows : (k + 1) * rows, :] = cots[k][...]
+    for i in range(2):
+        for k in range(pieces):
+            left[k * rows : (k + 1) * rows, :] = lefts[i * pieces + k][...]
+        outs[i][...] = contract_rows(left[...], right[...]).astype(BF16)
+
+
+def down_sends(indices, hidden, cot, n):
+    rows, width = cot[0].shape
+    m = len(cot)
+    tile = width // 4
+    return pl.pallas_call(
+        functools.partial(sends_kernel, pieces=m),
+        grid_spec=pltpu.PrefetchScalarGridSpec(
+            num_scalar_prefetch=1,
+            grid=(4,),
+            in_specs=[
+                pl.BlockSpec((rows, n), lambda j, s_ref, i=i: (0, s_ref[i]))
+                for i in range(2)
+                for _ in range(m)
+            ]
+            + [pl.BlockSpec((rows, tile), lambda j, s_ref: (0, j))] * m,
+            out_specs=[pl.BlockSpec((n, tile), lambda j, s_ref: (0, j))] * 2,
+            scratch_shapes=[pltpu.VMEM((m * rows, n), BF16), pltpu.VMEM((m * rows, tile), BF16)],
+        ),
+        out_shape=[jax.ShapeDtypeStruct((n, width), BF16)] * 2,
+        compiler_params=params(12),
+        cost_estimate=COST,
+        name="down_sends",
+    )(indices, *hidden, *hidden, *cot)
 
 
 def down_kernel(s_ref, *refs, pieces, ins, outs):
@@ -455,16 +492,22 @@
         c3, t3 = pick([c_mid, xc_end], (), [c_mid, cc_end])
         s3 = after(s3, c3)
         g3, u3, xs3 = forward([x3, *s3])
-        t3 = after(t3, xs2, d2, xs3)
+        t3 = after(t3, xs2, d2)
         f3, d3 = backward([c3, *t3], g3, u3)
 
         n = ff // n_dp
+        hidden = after(hidden, xs3)
 
         def to_core(yy):
             return over_core(down_part(yy * NC + (1 - c_arr), hidden, cot_rows, n)[0])
 
-        sent = [to_core(y_arr ^ k) for k in range(1, ny)]
-        own_recv = to_core(y_arr)
+        if ny == 2:
+            other = jnp.concatenate([(y_arr ^ k) * NC + (1 - c_arr) for k in (1, 0)])
+            first, second = down_sends(other, hidden, cot_rows, n)
+            sent, own_recv = [over_core(first)], over_core(second)
+        else:
+            sent = [to_core(y_arr ^ k) for k in range(1, ny)]
+            own_recv = to_core(y_arr)
         landed, totals = [], []
         for k in range(1, ny):
             recv = sent[k - 1]

time: 240 us -> 232 us (0.967)
  waiting for transfers between devices: 91.7 us -> 84.3 us
    ppermute x9, waiting for transfers between devices: 37.9 us -> 30.6 us  [over_y(): lax.ppermute(value, 'dp', [(y * NC + c, (y ^ k) * NC + c) for y in range(...]
    pallas_call x4 -> x2, Pallas kernels: 14.8 us -> 8.05 us  [down_part(): pl.pallas_call(functools.partial(down_kernel, pieces=m, ins=ins, outs=out...]
    pallas_call x0 -> x1, Pallas kernels: none -> 5.58 us  [down_sends(): pl.pallas_call(functools.partial(sends_kernel, pieces=m), grid_spec=pltpu...]
  transfers between devices with their start and end apart: 29 -> 29, of which waited for: 18 -> 17; matrix products, arithmetic and copies ran while one was open for 0% -> 0% of each run, Pallas kernels for 31% -> 34%
where the time goes in v4:
time: 232 us; the launch traced here: 231 us
  waiting for transfers between devices  84.3 us (36%)
  Pallas kernels  83.5 us (36%)
  starting transfers between devices  34.9 us (15%)
  local copies, waits for them, and re-layouts  25.3 us (11%)
    ppermute x9, waiting for transfers between devices, over_y(): lax.ppermute(value, 'dp', [(y * NC + c, (y ^ k) * NC + c) for y in range(...  30.6 us
    ppermute x8, waiting for transfers between devices, over_x(): out.append(lax.ppermute(sends[k - 1], 'expert', pairs))  30.4 us
    pallas_call x8, Pallas kernels, pick_rows(): pl.pallas_call(functools.partial(pick_kernel, nx=nx, top=top, n_meta=len(...  25.7 us
    unnamed x98, local copies, waits for them, and re-layouts  25.1 us
    pallas_call x2, Pallas kernels, both_part(): pl.pallas_call(functools.partial(both_kernel, pieces=m, add=add), grid_sp...  18.3 us
    pallas_call x4, Pallas kernels, back(): pl.pallas_call(functools.partial(back_kernel, parts=n), in_specs=whole(n...  13.6 us
    pallas_call x4, Pallas kernels, gate_up(): pl.pallas_call(functools.partial(gate_up_kernel, parts=len(parts), ny=ny)...  12.1 us
    ppermute x9, starting transfers between devices, over_y(): lax.ppermute(value, 'dp', [(y * NC + c, (y ^ k) * NC + c) for y in range(...  11.8 us
  transfers between devices with their start and end apart: 29, of which 17 were waited for; matrix products, arithmetic and copies ran while one was open for 0% of the time, Pallas kernels for 34%

profile of v4, /device:TPU:0, one launch (start us, length us, event | category | flops | bytes accessed | tf_op | source)
XLA Modules:
  0.0 231.1 jit_solution(9232546528484926357)
XLA Ops:
  6.5 4.7 %collective-permute-start.2 = (bf16[256,3712]{1,0:T(8,128)(2,1)S(1)}, bf16[256,3712]{1,0:T(8,128)(2,1)}, u32[]{:S(2)}, u32[]{:S(2)}) collective-permute-start(bf16[256,3712]{1,0:T(8,128)(2,1)S(1)} %pack.1.refs_0_.refs_1_), channel_id=1, source_target_pairs={{0,2},{1,3},{2,0},{3,1},{4,6},{5,7},{6,4},{7,5},{8,10},{9,11},{10,... | collective-permute-start | bytes 5701640 | tf_op jit(solution)/shard_map/ppermute | solution.py:397
  15.9 3.1 %pick.9 = (bf16[80,3584]{1,0:T(8,128)(2,1)S(1)}, bf16[80,3584]{1,0:T(8,128)(2,1)}) custom-call(s32[2,2]{1,0:T(2,128)S(1)} %pad_add_fusion.ids_ref, bf16[256,3712]{1,0:T(8,128)(2,1)S(1)} %pack.1.refs_0_.refs_1_, bf16[256,3712]{1,0:T(8,128)(2,1)S(1)} %pack.1.refs_0_.refs_1_), custom_call_target="tpu_custom_call" | custom-call | flops 3000000000 | bytes 1000 | tf_op jit(solution)/shard_map/pick/pallas_call | solution.py:123
  20.4 10.2 %collective-permute-done.refs_1_ = bf16[80,3584]{1,0:T(8,128)(2,1)S(1)} collective-permute-done((bf16[80,3584]{1,0:T(8,128)(2,1)}, bf16[80,3584]{1,0:T(8,128)(2,1)S(1)}, u32[]{:S(2)}, u32[]{:S(2)}) %collective-permute-start) | collective-permute-done | bytes 573472 | tf_op jit(solution)/shard_map/ppermute | solution.py:409
  30.6 3.1 %copy-done = bf16[1,3584,1024]{2,1,0:T(8,128)(2,1)S(1)} copy-done((bf16[1,3584,1024]{2,1,0:T(8,128)(2,1)S(1)}, bf16[1,3584,1024]{2,1,0:T(8,128)(2,1)}, u32[]{:S(2)}) %copy-start) | copy-done | bytes 7340056
  41.2 3.1 %copy-done.28 = bf16[1,1024,3584]{2,1,0:T(8,128)(2,1)S(1)} copy-done((bf16[1,1024,3584]{2,1,0:T(8,128)(2,1)S(1)}, bf16[1,1024,3584]{2,1,0:T(8,128)(2,1)}, u32[]{:S(2)}) %copy-start.28) | copy-done | bytes 7340056
  44.3 3.7 %back.4 = (bf16[160,2048]{1,0:T(8,128)(2,1)S(1)}, bf16[160,1024]{1,0:T(8,128)(2,1)S(1)}, bf16[160,3584]{1,0:T(8,128)(2,1)S(1)}) custom-call(bf16[80,3584]{1,0:T(8,128)(2,1)S(1)} %copy-done.41, bf16[80,3584]{1,0:T(8,128)(2,1)} %collective-permute-done.4.refs_1_, bf16[1,1024,3584]{2,1,0:T(8,128)(2,1)S(1)} %copy-done.28, ...), custom_call_target="tpu_custom_call" | custom-call | flops 3000000000 | bytes 1000 | tf_op jit(solution)/shard_map/back/pallas_call | solution.py:205
  48.7 3.7 %collective-permute-done.2.refs_0_.refs_1_ = bf16[256,3712]{1,0:T(8,128)(2,1)} collective-permute-done((bf16[256,3712]{1,0:T(8,128)(2,1)S(1)}, bf16[256,3712]{1,0:T(8,128)(2,1)}, u32[]{:S(2)}, u32[]{:S(2)}) %collective-permute-start.2) | collective-permute-done | bytes 1900576 | tf_op jit(solution)/shard_map/ppermute | solution.py:397
  56.6 3.9 %pick.10 = (bf16[80,3584]{1,0:T(8,128)(2,1)S(1)}, bf16[80,3584]{1,0:T(8,128)(2,1)S(1)}) custom-call(s32[2,2]{1,0:T(2,128)S(1)} %pad_add_fusion.ids_ref, bf16[256,3712]{1,0:T(8,128)(2,1)} %collective-permute-done.2.refs_0_.refs_1_, bf16[256,3712]{1,0:T(8,128)(2,1)} %collective-permute-done.2.refs_0_.refs_1_), custom_call_target="tpu_custom_call" | custom-call | flops 3000000000 | bytes 1000 | tf_op jit(solution)/shard_map/pick/pallas_call | solution.py:123
  62.1 3.4 %pick.11 = (bf16[80,3584]{1,0:T(8,128)(2,1)S(1)}, bf16[80,3584]{1,0:T(8,128)(2,1)S(1)}) custom-call(s32[2,2]{1,0:T(2,128)S(1)} %pad_add_fusion.ids_ref, bf16[256,3712]{1,0:T(8,128)(2,1)} %collective-permute-done.2.refs_0_.refs_1_, bf16[256,3712]{1,0:T(8,128)(2,1)} %collective-permute-done.2.refs_0_.refs_1_), custom_call_target="tpu_custom_call" | custom-call | flops 3000000000 | bytes 1000 | tf_op jit(solution)/shard_map/pick/pallas_call | solution.py:123
  65.5 5.0 %collective-permute-done.1.refs_1_ = bf16[160,1792]{1,0:T(8,128)(2,1)S(1)} collective-permute-done((bf16[160,1792]{1,0:T(8,128)(2,1)S(1)}, bf16[160,1792]{1,0:T(8,128)(2,1)S(1)}, u32[]{:S(2)}, u32[]{:S(2)}) %collective-permute-start.1) | collective-permute-done | bytes 573472 | tf_op jit(solution)/shard_map/ppermute | solution.py:418
  72.0 4.6 %collective-permute-done.5.refs_1_ = bf16[80,3584]{1,0:T(8,128)(2,1)S(1)} collective-permute-done((bf16[80,3584]{1,0:T(8,128)(2,1)S(1)}, bf16[80,3584]{1,0:T(8,128)(2,1)S(1)}, u32[]{:S(2)}, u32[]{:S(2)}) %collective-permute-start.5) | collective-permute-done | bytes 573472 | tf_op jit(solution)/shard_map/ppermute | solution.py:409
  76.5 5.9 %collective-permute-done.10.refs_9_ = bf16[160,2048]{1,0:T(8,128)(2,1)S(1)} collective-permute-done((bf16[160,2048]{1,0:T(8,128)(2,1)S(1)}, bf16[160,2048]{1,0:T(8,128)(2,1)S(1)}, u32[]{:S(2)}, u32[]{:S(2)}) %collective-permute-start.10) | collective-permute-done | bytes 655392 | tf_op jit(solution)/shard_map/ppermute | solution.py:418
  82.5 3.7 %collective-permute-done.9.refs_1_ = bf16[80,3584]{1,0:T(8,128)(2,1)S(1)} collective-permute-done((bf16[80,3584]{1,0:T(8,128)(2,1)S(1)}, bf16[80,3584]{1,0:T(8,128)(2,1)S(1)}, u32[]{:S(2)}, u32[]{:S(2)}) %collective-permute-start.9) | collective-permute-done | bytes 573472 | tf_op jit(solution)/shard_map/ppermute | solution.py:409
  93.3 3.5 %collective-permute-done.7.refs_0_.refs_2_ = bf16[256,3712]{1,0:T(8,128)(2,1)S(1)} collective-permute-done((bf16[256,3712]{1,0:T(8,128)(2,1)}, bf16[256,3712]{1,0:T(8,128)(2,1)S(1)}, u32[]{:S(2)}, u32[]{:S(2)}) %collective-permute-start.7) | collective-permute-done | bytes 1900576 | tf_op jit(solution)/shard_map/ppermute | solution.py:400
  109.0 7.5 %collective-permute-done.11.refs_1_ = bf16[80,3584]{1,0:T(8,128)(2,1)S(1)} collective-permute-done((bf16[80,3584]{1,0:T(8,128)(2,1)S(1)}, bf16[80,3584]{1,0:T(8,128)(2,1)S(1)}, u32[]{:S(2)}, u32[]{:S(2)}) %collective-permute-start.11) | collective-permute-done | bytes 573472 | tf_op jit(solution)/shard_map/ppermute | solution.py:409
  116.5 3.3 %gate_up.6 = (f32[160,1024]{1,0:T(8,128)S(1)}, f32[160,1024]{1,0:T(8,128)S(1)}, bf16[160,1792]{1,0:T(8,128)(2,1)S(1)}, bf16[160,1792]{1,0:T(8,128)(2,1)}) custom-call(s32[1]{0:T(128)} %bitcast.1.y_ref, bf16[80,3584]{1,0:T(8,128)(2,1)S(1)} %get-tuple-element.105.refs_0_, bf16[80,3584]{1,0:T(8,128)(2,1)S(1)} %collective-permute-done.11.refs_1_, ...), custom_call_target="tpu_custom_call" | custom-call | flops 3000000000 | bytes 1000 | tf_op jit(solution)/shard_map/gate_up/pallas_call | solution.py:170
  119.8 4.0 %collective-permute-done.13.refs_1_.refs_3_ = bf16[128,3712]{1,0:T(8,128)(2,1)S(1)} collective-permute-done((bf16[128,3712]{1,0:T(8,128)(2,1)S(1)}, bf16[128,3712]{1,0:T(8,128)(2,1)S(1)}, u32[]{:S(2)}, u32[]{:S(2)}) %collective-permute-start.13) | collective-permute-done | bytes 950304 | tf_op jit(solution)/shard_map/ppermute | solution.py:403
  123.9 3.1 %pick.14 = (bf16[80,3584]{1,0:T(8,128)(2,1)S(1)}, bf16[80,3584]{1,0:T(8,128)(2,1)S(1)}) custom-call(s32[2,2]{1,0:T(2,128)S(1)} %pad_add_fusion.ids_ref, bf16[256,3712]{1,0:T(8,128)(2,1)} %collective-permute-done.3.refs_0_.refs_2_, bf16[128,3712]{1,0:T(8,128)(2,1)S(1)} %collective-permute-done.13.refs_1_.refs_3_, ...), custom_call_target="tpu_custom_call" | custom-call | flops 3000000000 | bytes 1000 | tf_op jit(solution)/shard_map/pick/pallas_call | solution.py:123
  130.1 3.5 %back.6 = (bf16[160,2048]{1,0:T(8,128)(2,1)}, bf16[160,1024]{1,0:T(8,128)(2,1)S(1)}, bf16[160,3584]{1,0:T(8,128)(2,1)S(1)}) custom-call(bf16[80,3584]{1,0:T(8,128)(2,1)S(1)} %get-tuple-element.109.refs_0_, bf16[80,3584]{1,0:T(8,128)(2,1)S(1)} %collective-permute-done.16.refs_1_, bf16[1,1024,3584]{2,1,0:T(8,128)(2,1)S(1)} %bitcast.14, ...), custom_call_target="tpu_custom_call" | custom-call | flops 3000000000 | bytes 1000 | tf_op jit(solution)/shard_map/back/pallas_call | solution.py:205
  134.1 6.4 %collective-permute-done.15.refs_3_ = bf16[128,3584]{1,0:T(8,128)(2,1)S(1)} collective-permute-done((bf16[128,3584]{1,0:T(8,128)(2,1)S(1)}, bf16[128,3584]{1,0:T(8,128)(2,1)S(1)}, u32[]{:S(2)}, u32[]{:S(2)}) %collective-permute-start.15) | collective-permute-done | bytes 917536 | tf_op jit(solution)/shard_map/ppermute | solution.py:403
  140.6 4.1 %pick.15 = (bf16[80,3584]{1,0:T(8,128)(2,1)S(1)}, bf16[80,3584]{1,0:T(8,128)(2,1)}) custom-call(s32[2,2]{1,0:T(2,128)S(1)} %pad_add_fusion.ids_ref, bf16[256,3712]{1,0:T(8,128)(2,1)} %collective-permute-done.3.refs_0_.refs_2_, bf16[128,3712]{1,0:T(8,128)(2,1)S(1)} %collective-permute-done.13.refs_1_.refs_3_, ...), custom_call_target="tpu_custom_call" | custom-call | flops 3000000000 | bytes 1000 | tf_op jit(solution)/shard_map/pick/pallas_call | solution.py:123
  146.2 3.3 %gate_up.7 = (f32[160,1024]{1,0:T(8,128)S(1)}, f32[160,1024]{1,0:T(8,128)S(1)}, bf16[160,1792]{1,0:T(8,128)(2,1)S(1)}, bf16[160,1792]{1,0:T(8,128)(2,1)}) custom-call(s32[1]{0:T(128)} %bitcast.1.y_ref, bf16[80,3584]{1,0:T(8,128)(2,1)S(1)} %get-tuple-element.116.refs_0_, bf16[80,3584]{1,0:T(8,128)(2,1)S(1)} %collective-permute-done.14.refs_1_, ...), custom_call_target="tpu_custom_call" | custom-call | flops 3000000000 | bytes 1000 | tf_op jit(solution)/shard_map/gate_up/pallas_call | solution.py:170
  153.6 3.5 %collective-permute-done.19.refs_1_ = bf16[80,3584]{1,0:T(8,128)(2,1)} collective-permute-done((bf16[80,3584]{1,0:T(8,128)(2,1)}, bf16[80,3584]{1,0:T(8,128)(2,1)}, u32[]{:S(2)}, u32[]{:S(2)}) %collective-permute-start.19) | collective-permute-done | bytes 573472 | tf_op jit(solution)/shard_map/ppermute | solution.py:409
  157.1 3.1 %copy-done.29 = bf16[1,1024,3584]{2,1,0:T(8,128)(2,1)S(1)} copy-done((bf16[1,1024,3584]{2,1,0:T(8,128)(2,1)S(1)}, bf16[1,1024,3584]{2,1,0:T(8,128)(2,1)}, u32[]{:S(2)}) %copy-start.29) | copy-done | bytes 7340056
  163.4 3.7 %back.7 = (bf16[160,2048]{1,0:T(8,128)(2,1)S(1)}, bf16[160,1024]{1,0:T(8,128)(2,1)S(1)}, bf16[160,3584]{1,0:T(8,128)(2,1)S(1)}) custom-call(bf16[80,3584]{1,0:T(8,128)(2,1)S(1)} %copy-done.39, bf16[80,3584]{1,0:T(8,128)(2,1)} %collective-permute-done.19.refs_1_, bf16[1,1024,3584]{2,1,0:T(8,128)(2,1)S(1)} %copy-done.29, f32[160,1024]{1,0:T(8,128)S(1)} %copy-done.33, ...), custom_call_target="tpu_custom_call" | custom-call | flops 3000000000 | bytes 1000 | tf_op jit(solution)/shard_map/back/pallas_call | solution.py:205
  167.2 5.6 %down_sends.1 = (bf16[256,3584]{1,0:T(8,128)(2,1)S(1)}, bf16[256,3584]{1,0:T(8,128)(2,1)S(1)}) custom-call(s32[2]{0:T(128)S(1)} %pad_add_fusion.1.s_ref, bf16[160,1024]{1,0:T(8,128)(2,1)S(1)} %copy-done.23, bf16[160,1024]{1,0:T(8,128)(2,1)S(1)} %copy-done.25, bf16[160,1024]{1,0:T(8,128)(2,1)S(1)} %copy-done.27, ...), custom_call_target="tpu_custom_call" | custom-call | flops 3000000000 | bytes 1000 | tf_op jit(solution)/shard_map/down_sends/pallas_call | solution.py:236
  179.3 4.0 %down_part.2 = bf16[256,3584]{1,0:T(8,128)(2,1)S(1)} custom-call(s32[1]{0:T(128)S(6)} %add.51.s_ref, bf16[160,1024]{1,0:T(8,128)(2,1)S(1)} %copy-done.23, bf16[160,1024]{1,0:T(8,128)(2,1)S(1)} %copy-done.25, bf16[160,1024]{1,0:T(8,128)(2,1)S(1)} %copy-done.27, bf16[160,1024]{1,0:T(8,128)(2,1)S(1)} %get-tuple-element.138.refs_3_.refs_7_, ...), custom_call_target="tpu_custom_call" | custom-call | flops 3000000000 | bytes 1000 | tf_op jit(solution)/shard_map/down_part/pallas_call | solution.py:295
  184.9 6.1 %collective-permute-done.23.refs_15_ = bf16[160,2048]{1,0:T(8,128)(2,1)S(1)} collective-permute-done((bf16[160,2048]{1,0:T(8,128)(2,1)S(1)}, bf16[160,2048]{1,0:T(8,128)(2,1)S(1)}, u32[]{:S(2)}, u32[]{:S(2)}) %collective-permute-start.23) | collective-permute-done | bytes 655392 | tf_op jit(solution)/shard_map/ppermute | solution.py:418
  191.1 8.1 %both_part.2 = (bf16[896,512]{1,0:T(8,128)(2,1)S(1)}, bf16[896,512]{1,0:T(8,128)(2,1)S(1)}, bf16[896,512]{1,0:T(8,128)(2,1)S(1)}, bf16[896,512]{1,0:T(8,128)(2,1)S(1)}) custom-call(s32[1]{0:T(128)S(6)} %sub.14.c_ref, bf16[160,1792]{1,0:T(8,128)(2,1)S(1)} %copy-done.11, bf16[160,1792]{1,0:T(8,128)(2,1)S(1)} %copy-done.13, bf16[160,1792]{1,0:T(8,128)(2,1)S(1)} %copy-done.15, ...), custom_call_target="tpu_custom_call" | custom-call | flops 3000000000 | bytes 1000 | tf_op jit(solution)/shard_map/both_part/pallas_call | solution.py:354
  200.3 4.0 %down_part.3 = f32[256,3584]{1,0:T(8,128)S(1)} custom-call(s32[1]{0:T(128)S(6)} %add.54.s_ref, bf16[160,1024]{1,0:T(8,128)(2,1)S(1)} %copy-done.23, bf16[160,1024]{1,0:T(8,128)(2,1)S(1)} %copy-done.25, bf16[160,1024]{1,0:T(8,128)(2,1)S(1)} %copy-done.27, bf16[160,1024]{1,0:T(8,128)(2,1)S(1)} %get-tuple-element.138.refs_3_.refs_7_, ...), custom_call_target="tpu_custom_call" | custom-call | flops 3000000000 | bytes 1000 | tf_op jit(solution)/shard_map/down_part/pallas_call | solution.py:295
  205.7 10.1 %both_part.3 = (bf16[896,1024]{1,0:T(8,128)(2,1)}, bf16[896,1024]{1,0:T(8,128)(2,1)}) custom-call(s32[1]{0:T(128)} %bitcast.c_ref, bf16[160,1792]{1,0:T(8,128)(2,1)S(1)} %copy-done.11, bf16[160,1792]{1,0:T(8,128)(2,1)S(1)} %copy-done.13, bf16[160,1792]{1,0:T(8,128)(2,1)S(1)} %copy-done.15, bf16[160,1792]{1,0:T(8,128)(2,1)S(1)} %copy-done.17, ...), custom_call_target="tpu_custom_call" | custom-call | flops 3000000000 | bytes 1000 | tf_op jit(solution)/shard_map/both_part/pallas_call | solution.py:354
  215.8 13.6 %collective-permute-done.28 = bf16[256,3584]{1,0:T(8,128)(2,1)S(1)} collective-permute-done((bf16[256,3584]{1,0:T(8,128)(2,1)S(1)}, bf16[256,3584]{1,0:T(8,128)(2,1)S(1)}, u32[]{:S(2)}, u32[]{:S(2)}) %collective-permute-start.28) | collective-permute-done | bytes 1835040 | tf_op jit(solution)/shard_map/ppermute | solution.py:418
  (157 shorter events, 71.1 us)
Async XLA Ops:
  4.6 44.1 %collective-permute-start.3 = (bf16[256,3712]{1,0:T(8,128)(2,1)S(1)}, bf16[256,3712]{1,0:T(8,128)(2,1)}, u32[]{:S(2)}, u32[]{:S(2)}) collective-permute-start(bf16[256,3712]{1,0:T(8,128)(2,1)S(1)} %pack.1.refs_0_.refs_1_), channel_id=1, source_target_pairs={{2,4},{3,5},{4,2},{5,3},{10,12},{11,13},{12,10},{13,11},{18,20},{1... | collective-permute-start | bytes 5701640 | tf_op jit(solution)/shard_map/ppermute | solution.py:397
  6.5 45.9 %collective-permute-start.2 = (bf16[256,3712]{1,0:T(8,128)(2,1)S(1)}, bf16[256,3712]{1,0:T(8,128)(2,1)}, u32[]{:S(2)}, u32[]{:S(2)}) collective-permute-start(bf16[256,3712]{1,0:T(8,128)(2,1)S(1)} %pack.1.refs_0_.refs_1_), channel_id=1, source_target_pairs={{0,2},{1,3},{2,0},{3,1},{4,6},{5,7},{6,4},{7,5},{8,10},{9,11},{10,... | collective-permute-start | bytes 5701640 | tf_op jit(solution)/shard_map/ppermute | solution.py:397
  14.4 16.1 %collective-permute-start = (bf16[80,3584]{1,0:T(8,128)(2,1)}, bf16[80,3584]{1,0:T(8,128)(2,1)S(1)}, u32[]{:S(2)}, u32[]{:S(2)}) collective-permute-start(bf16[80,3584]{1,0:T(8,128)(2,1)} %get-tuple-element.80), channel_id=1, source_target_pairs={{0,1},{1,0},{2,3},{3,2},{4,5},{5,4},{6,7},{7,6},{8,9},{9,8},{10,11... | collective-permute-start | bytes 1720328 | tf_op jit(solution)/shard_map/ppermute | solution.py:409
  19.9 21.3 %collective-permute-start.4 = (bf16[80,3584]{1,0:T(8,128)(2,1)}, bf16[80,3584]{1,0:T(8,128)(2,1)}, u32[]{:S(2)}, u32[]{:S(2)}) collective-permute-start(bf16[80,3584]{1,0:T(8,128)(2,1)} %get-tuple-element.85), channel_id=1, source_target_pairs={{0,1},{1,0},{2,3},{3,2},{4,5},{5,4},{6,7},{7,6},{8,9},{9,8},{10,11... | collective-permute-start | bytes 1720328 | tf_op jit(solution)/shard_map/ppermute | solution.py:409
  52.4 44.4 %collective-permute-start.7 = (bf16[256,3712]{1,0:T(8,128)(2,1)}, bf16[256,3712]{1,0:T(8,128)(2,1)S(1)}, u32[]{:S(2)}, u32[]{:S(2)}) collective-permute-start(bf16[256,3712]{1,0:T(8,128)(2,1)} %collective-permute-done.3.refs_0_.refs_2_), channel_id=1, source_target_pairs={{2,0},{3,1},{4,6},{5,7},{10,8},{11,9},{12,14},{13,15},{18,16},{19,... | collective-permute-start | bytes 5701640 | tf_op jit(solution)/shard_map/ppermute | solution.py:400
  53.7 43.1 %collective-permute-start.8 = (bf16[256,3712]{1,0:T(8,128)(2,1)}, bf16[256,3712]{1,0:T(8,128)(2,1)S(1)}, u32[]{:S(2)}, u32[]{:S(2)}) collective-permute-start(bf16[256,3712]{1,0:T(8,128)(2,1)} %collective-permute-done.2.refs_0_.refs_1_), channel_id=1, source_target_pairs={{2,4},{3,5},{4,2},{5,3},{10,12},{11,13},{12,10},{13,11},{18,20},{1... | collective-permute-start | bytes 5701640 | tf_op jit(solution)/shard_map/ppermute | solution.py:400
  54.5 16.0 %collective-permute-start.1 = (bf16[160,1792]{1,0:T(8,128)(2,1)S(1)}, bf16[160,1792]{1,0:T(8,128)(2,1)S(1)}, u32[]{:S(2)}, u32[]{:S(2)}) collective-permute-start(bf16[160,1792]{1,0:T(8,128)(2,1)S(1)} %get-tuple-element.82), channel_id=1, source_target_pairs={{0,16},{8,24},{16,0},{24,8},{1,17},{9,25},{17,1},{25,9},{2,18},{10... | collective-permute-start | bytes 1720328 | tf_op jit(solution)/shard_map/ppermute | solution.py:418
  56.1 26.4 %collective-permute-start.10 = (bf16[160,2048]{1,0:T(8,128)(2,1)S(1)}, bf16[160,2048]{1,0:T(8,128)(2,1)S(1)}, u32[]{:S(2)}, u32[]{:S(2)}) collective-permute-start(bf16[160,2048]{1,0:T(8,128)(2,1)S(1)} %get-tuple-element.146.refs_8_), channel_id=1, source_target_pairs={{0,16},{8,24},{16,0},{24,8},{1,17},{9,25},{17,1},{25,9},{2,18},{10... | collective-permute-start | bytes 1966088 | tf_op jit(solution)/shard_map/ppermute | solution.py:418
  56.6 29.6 %slice-start = ((s8[7340032]{0:T(1024)(128)(4,1)}), s8[4194304]{0:T(1024)(128)(4,1)S(1)}, s32[]{:S(2)}) async-start(s8[7340032]{0:T(1024)(128)(4,1)} %bitcast.9), calls=%async_computation | async-start | bytes 8388608
  56.6 29.6 %slice-start.2 = ((s8[7340032]{0:T(1024)(128)(4,1)}), s8[4194304]{0:T(1024)(128)(4,1)S(1)}, s32[]{:S(2)}) async-start(s8[7340032]{0:T(1024)(128)(4,1)} %bitcast.11), calls=%async_computation.2 | async-start | bytes 8388608
  60.5 25.7 %slice-start.1 = ((s8[7340032]{0:T(1024)(128)(4,1)}), s8[3145728]{0:T(1024)(128)(4,1)S(1)}, s32[]{:S(2)}) async-start(s8[7340032]{0:T(1024)(128)(4,1)} %bitcast.9), calls=%async_computation.1 | async-start | bytes 6291456
  60.5 16.0 %collective-permute-start.5 = (bf16[80,3584]{1,0:T(8,128)(2,1)S(1)}, bf16[80,3584]{1,0:T(8,128)(2,1)S(1)}, u32[]{:S(2)}, u32[]{:S(2)}) collective-permute-start(bf16[80,3584]{1,0:T(8,128)(2,1)S(1)} %get-tuple-element.91), channel_id=1, source_target_pairs={{0,1},{1,0},{2,3},{3,2},{4,5},{5,4},{6,7},{7,6},{8,9},{9,8},{10,11... | collective-permute-start | bytes 1720328 | tf_op jit(solution)/shard_map/ppermute | solution.py:409
  70.5 15.7 %collective-permute-start.9 = (bf16[80,3584]{1,0:T(8,128)(2,1)S(1)}, bf16[80,3584]{1,0:T(8,128)(2,1)S(1)}, u32[]{:S(2)}, u32[]{:S(2)}) collective-permute-start(bf16[80,3584]{1,0:T(8,128)(2,1)S(1)} %get-tuple-element.98), channel_id=1, source_target_pairs={{0,1},{1,0},{2,3},{3,2},{4,5},{5,4},{6,7},{7,6},{8,9},{9,8},{10,11... | collective-permute-start | bytes 1720328 | tf_op jit(solution)/shard_map/ppermute | solution.py:409
  89.0 18.6 %collective-permute-start.6 = (bf16[160,1792]{1,0:T(8,128)(2,1)S(1)}, bf16[160,1792]{1,0:T(8,128)(2,1)S(1)}, u32[]{:S(2)}, u32[]{:S(2)}) collective-permute-start(bf16[160,1792]{1,0:T(8,128)(2,1)S(1)} %get-tuple-element.96), channel_id=1, source_target_pairs={{0,16},{8,24},{16,0},{24,8},{1,17},{9,25},{17,1},{25,9},{2,18},{10... | collective-permute-start | bytes 1720328 | tf_op jit(solution)/shard_map/ppermute | solution.py:418
  96.9 27.0 %collective-permute-start.13 = (bf16[128,3712]{1,0:T(8,128)(2,1)S(1)}, bf16[128,3712]{1,0:T(8,128)(2,1)S(1)}, u32[]{:S(2)}, u32[]{:S(2)}) collective-permute-start(bf16[128,3712]{1,0:T(8,128)(2,1)S(1)} %slice.8), channel_id=1, source_target_pairs={{2,0},{3,1},{4,6},{5,7},{10,8},{11,9},{12,14},{13,15},{18,16},{19,... | collective-permute-start | bytes 2850824 | tf_op jit(solution)/shard_map/ppermute | solution.py:403
  100.5 16.0 %collective-permute-start.11 = (bf16[80,3584]{1,0:T(8,128)(2,1)S(1)}, bf16[80,3584]{1,0:T(8,128)(2,1)S(1)}, u32[]{:S(2)}, u32[]{:S(2)}) collective-permute-start(bf16[80,3584]{1,0:T(8,128)(2,1)S(1)} %get-tuple-element.106), channel_id=1, source_target_pairs={{0,1},{1,0},{2,3},{3,2},{4,5},{5,4},{6,7},{7,6},{8,9},{9,8},{10,11... | collective-permute-start | bytes 1720328 | tf_op jit(solution)/shard_map/ppermute | solution.py:409
  102.1 28.0 %collective-permute-start.17 = (bf16[160,2048]{1,0:T(8,128)(2,1)S(1)}, bf16[160,2048]{1,0:T(8,128)(2,1)S(1)}, u32[]{:S(2)}, u32[]{:S(2)}) collective-permute-start(bf16[160,2048]{1,0:T(8,128)(2,1)S(1)} %get-tuple-element.102.refs_10_), channel_id=1, source_target_pairs={{0,16},{8,24},{16,0},{24,8},{1,17},{9,25},{17,1},{25,9},{2,18},{10... | collective-permute-start | bytes 1966088 | tf_op jit(solution)/shard_map/ppermute | solution.py:418
  103.7 36.9 %collective-permute-start.15 = (bf16[128,3584]{1,0:T(8,128)(2,1)S(1)}, bf16[128,3584]{1,0:T(8,128)(2,1)S(1)}, u32[]{:S(2)}, u32[]{:S(2)}) collective-permute-start(bf16[128,3584]{1,0:T(8,128)(2,1)S(1)} %slice.9), channel_id=1, source_target_pairs={{2,0},{3,1},{4,6},{5,7},{10,8},{11,9},{12,14},{13,15},{18,16},{19,... | collective-permute-start | bytes 2752520 | tf_op jit(solution)/shard_map/ppermute | solution.py:403
  108.4 21.7 %collective-permute-start.16 = (bf16[80,3584]{1,0:T(8,128)(2,1)S(1)}, bf16[80,3584]{1,0:T(8,128)(2,1)S(1)}, u32[]{:S(2)}, u32[]{:S(2)}) collective-permute-start(bf16[80,3584]{1,0:T(8,128)(2,1)S(1)} %get-tuple-element.118), channel_id=1, source_target_pairs={{0,1},{1,0},{2,3},{3,2},{4,5},{5,4},{6,7},{7,6},{8,9},{9,8},{10,11... | collective-permute-start | bytes 1720328 | tf_op jit(solution)/shard_map/ppermute | solution.py:409
  127.0 19.2 %collective-permute-start.14 = (bf16[80,3584]{1,0:T(8,128)(2,1)S(1)}, bf16[80,3584]{1,0:T(8,128)(2,1)S(1)}, u32[]{:S(2)}, u32[]{:S(2)}) collective-permute-start(bf16[80,3584]{1,0:T(8,128)(2,1)S(1)} %get-tuple-element.117), channel_id=1, source_target_pairs={{0,1},{1,0},{2,3},{3,2},{4,5},{5,4},{6,7},{7,6},{8,9},{9,8},{10,11... | collective-permute-start | bytes 1720328 | tf_op jit(solution)/shard_map/ppermute | solution.py:409
  128.6 25.1 %collective-permute-start.12 = (bf16[160,1792]{1,0:T(8,128)(2,1)}, bf16[160,1792]{1,0:T(8,128)(2,1)}, u32[]{:S(2)}, u32[]{:S(2)}) collective-permute-start(bf16[160,1792]{1,0:T(8,128)(2,1)} %get-tuple-element.112), channel_id=1, source_target_pairs={{0,16},{8,24},{16,0},{24,8},{1,17},{9,25},{17,1},{25,9},{2,18},{10... | collective-permute-start | bytes 1720328 | tf_op jit(solution)/shard_map/ppermute | solution.py:418
  133.6 23.5 %collective-permute-start.20 = (bf16[160,2048]{1,0:T(8,128)(2,1)}, bf16[160,2048]{1,0:T(8,128)(2,1)}, u32[]{:S(2)}, u32[]{:S(2)}) collective-permute-start(bf16[160,2048]{1,0:T(8,128)(2,1)} %get-tuple-element.121.refs_12_), channel_id=1, source_target_pairs={{0,16},{8,24},{16,0},{24,8},{1,17},{9,25},{17,1},{25,9},{2,18},{10... | collective-permute-start | bytes 1966088 | tf_op jit(solution)/shard_map/ppermute | solution.py:418
  144.7 12.4 %collective-permute-start.19 = (bf16[80,3584]{1,0:T(8,128)(2,1)}, bf16[80,3584]{1,0:T(8,128)(2,1)}, u32[]{:S(2)}, u32[]{:S(2)}) collective-permute-start(bf16[80,3584]{1,0:T(8,128)(2,1)} %get-tuple-element.130), channel_id=1, source_target_pairs={{0,1},{1,0},{2,3},{3,2},{4,5},{5,4},{6,7},{7,6},{8,9},{9,8},{10,11... | collective-permute-start | bytes 1720328 | tf_op jit(solution)/shard_map/ppermute | solution.py:409
  152.1 15.2 %collective-permute-start.18 = (bf16[160,1792]{1,0:T(8,128)(2,1)}, bf16[160,1792]{1,0:T(8,128)(2,1)}, u32[]{:S(2)}, u32[]{:S(2)}) collective-permute-start(bf16[160,1792]{1,0:T(8,128)(2,1)} %get-tuple-element.126), channel_id=1, source_target_pairs={{0,16},{8,24},{16,0},{24,8},{1,17},{9,25},{17,1},{25,9},{2,18},{10... | collective-permute-start | bytes 1720328 | tf_op jit(solution)/shard_map/ppermute | solution.py:418
  172.8 3.9 %collective-permute-start.21 = (bf16[256,3584]{1,0:T(8,128)(2,1)S(1)}, bf16[256,3584]{1,0:T(8,128)(2,1)S(1)}, u32[]{:S(2)}, u32[]{:S(2)}) collective-permute-start(bf16[256,3584]{1,0:T(8,128)(2,1)S(1)} %get-tuple-element.143), channel_id=1, source_target_pairs={{0,8},{8,0},{16,24},{24,16},{1,9},{9,1},{17,25},{25,17},{2,10},{10... | collective-permute-start | bytes 5505032 | tf_op jit(solution)/shard_map/ppermute | solution.py:415
  172.9 6.4 %collective-permute-start.22 = (bf16[256,3584]{1,0:T(8,128)(2,1)S(1)}, bf16[256,3584]{1,0:T(8,128)(2,1)S(1)}, u32[]{:S(2)}, u32[]{:S(2)}) collective-permute-start(bf16[256,3584]{1,0:T(8,128)(2,1)S(1)} %get-tuple-element.144), channel_id=1, source_target_pairs={{0,8},{8,0},{16,24},{24,16},{1,9},{9,1},{17,25},{25,17},{2,10},{10... | collective-permute-start | bytes 5505032 | tf_op jit(solution)/shard_map/ppermute | solution.py:415
  173.4 17.6 %collective-permute-start.23 = (bf16[160,2048]{1,0:T(8,128)(2,1)S(1)}, bf16[160,2048]{1,0:T(8,128)(2,1)S(1)}, u32[]{:S(2)}, u32[]{:S(2)}) collective-permute-start(bf16[160,2048]{1,0:T(8,128)(2,1)S(1)} %get-tuple-element.147.refs_14_), channel_id=1, source_target_pairs={{0,16},{8,24},{16,0},{24,8},{1,17},{9,25},{17,1},{25,9},{2,18},{10... | collective-permute-start | bytes 1966088 | tf_op jit(solution)/shard_map/ppermute | solution.py:418
  183.3 46.1 %collective-permute-start.28 = (bf16[256,3584]{1,0:T(8,128)(2,1)S(1)}, bf16[256,3584]{1,0:T(8,128)(2,1)S(1)}, u32[]{:S(2)}, u32[]{:S(2)}) collective-permute-start(bf16[256,3584]{1,0:T(8,128)(2,1)S(1)} %down_part.2), channel_id=1, source_target_pairs={{0,16},{8,24},{16,0},{24,8},{1,17},{9,25},{17,1},{25,9},{2,18},{10... | collective-permute-start | bytes 5505032 | tf_op jit(solution)/shard_map/ppermute | solution.py:418
  199.2 5.1 %collective-permute-start.24 = (bf16[896,512]{1,0:T(8,128)(2,1)S(1)}, bf16[896,512]{1,0:T(8,128)(2,1)S(1)}, u32[]{:S(2)}, u32[]{:S(2)}) collective-permute-start(bf16[896,512]{1,0:T(8,128)(2,1)S(1)} %get-tuple-element.148), channel_id=1, source_target_pairs={{0,8},{8,0},{16,24},{24,16},{1,9},{9,1},{17,25},{25,17},{2,10},{10... | collective-permute-start | bytes 2752520 | tf_op jit(solution)/shard_map/ppermute | solution.py:415
  199.3 5.1 %collective-permute-start.25 = (bf16[896,512]{1,0:T(8,128)(2,1)S(1)}, bf16[896,512]{1,0:T(8,128)(2,1)S(1)}, u32[]{:S(2)}, u32[]{:S(2)}) collective-permute-start(bf16[896,512]{1,0:T(8,128)(2,1)S(1)} %get-tuple-element.149), channel_id=1, source_target_pairs={{0,8},{8,0},{16,24},{24,16},{1,9},{9,1},{17,25},{25,17},{2,10},{10... | collective-permute-start | bytes 2752520 | tf_op jit(solution)/shard_map/ppermute | solution.py:415
  199.8 4.6 %collective-permute-start.26 = (bf16[896,512]{1,0:T(8,128)(2,1)S(1)}, bf16[896,512]{1,0:T(8,128)(2,1)S(1)}, u32[]{:S(2)}, u32[]{:S(2)}) collective-permute-start(bf16[896,512]{1,0:T(8,128)(2,1)S(1)} %get-tuple-element.150), channel_id=1, source_target_pairs={{0,8},{8,0},{16,24},{24,16},{1,9},{9,1},{17,25},{25,17},{2,10},{10... | collective-permute-start | bytes 2752520 | tf_op jit(solution)/shard_map/ppermute | solution.py:415
  199.9 5.8 %collective-permute-start.27 = (bf16[896,512]{1,0:T(8,128)(2,1)S(1)}, bf16[896,512]{1,0:T(8,128)(2,1)S(1)}, u32[]{:S(2)}, u32[]{:S(2)}) collective-permute-start(bf16[896,512]{1,0:T(8,128)(2,1)S(1)} %get-tuple-element.151), channel_id=1, source_target_pairs={{0,8},{8,0},{16,24},{24,16},{1,9},{9,1},{17,25},{25,17},{2,10},{10... | collective-permute-start | bytes 2752520 | tf_op jit(solution)/shard_map/ppermute | solution.py:415
  (46 other events, 346.0 us)

commit v5 on v4

--- a/solution.py
+++ b/solution.py
@@ -10,7 +10,7 @@
 NZ = 4
 NC = 2
 F32, BF16 = jnp.float32, jnp.bfloat16
-COST = pl.CostEstimate(flops=3000000000, bytes_accessed=1000, transcendentals=0)
+COST = pl.CostEstimate(flops=2000000000, bytes_accessed=1000, transcendentals=0)
 
 
 LANES = 128

time: 232 us -> 230 us (level)
  local copies, waits for them, and re-layouts: 25.3 us -> 19.7 us
  Pallas kernels: 83.5 us -> 87 us
    unnamed x98 -> x96, local copies, waits for them, and re-layouts: 25.1 us -> 19.5 us
    ppermute x2, waiting for transfers between devices: 10.5 us -> 6.34 us  [hop3(): return lax.ppermute(b_mid, 'expert', outward)]
    ppermute x9, waiting for transfers between devices: 30.6 us -> 33.1 us  [over_y(): lax.ppermute(value, 'dp', [(y * NC + c, (y ^ k) * NC + c) for y in range(...]
  transfers between devices with their start and end apart: 29 -> 29, of which waited for: 17 -> 17; matrix products, arithmetic and copies ran while one was open for 0% -> 0% of each run, Pallas kernels for 34% -> 35%
where the time goes in v5:
time: 230 us; the launch traced here: 229 us
  Pallas kernels  87 us (38%)
  waiting for transfers between devices  83.1 us (36%)
  starting transfers between devices  36.2 us (16%)
  local copies, waits for them, and re-layouts  19.7 us (9%)
    ppermute x9, waiting for transfers between devices, over_y(): lax.ppermute(value, 'dp', [(y * NC + c, (y ^ k) * NC + c) for y in range(...  33.1 us
    ppermute x8, waiting for transfers between devices, over_x(): out.append(lax.ppermute(sends[k - 1], 'expert', pairs))  30.2 us
    pallas_call x8, Pallas kernels, pick_rows(): pl.pallas_call(functools.partial(pick_kernel, nx=nx, top=top, n_meta=len(...  26.5 us
    unnamed x96, local copies, waits for them, and re-layouts  19.5 us
    pallas_call x2, Pallas kernels, both_part(): pl.pallas_call(functools.partial(both_kernel, pieces=m, add=add), grid_sp...  18 us
    pallas_call x4, Pallas kernels, back(): pl.pallas_call(functools.partial(back_kernel, parts=n), in_specs=whole(n...  13.9 us
    pallas_call x4, Pallas kernels, gate_up(): pl.pallas_call(functools.partial(gate_up_kernel, parts=len(parts), ny=ny)...  13.4 us
    ppermute x9, starting transfers between devices, over_y(): lax.ppermute(value, 'dp', [(y * NC + c, (y ^ k) * NC + c) for y in range(...  12.9 us
  transfers between devices with their start and end apart: 29, of which 17 were waited for; matrix products, arithmetic and copies ran while one was open for 0% of the time, Pallas kernels for 35%

profile of v5, /device:TPU:0, one launch (start us, length us, event | category | flops | bytes accessed | tf_op | source)
XLA Modules:
  0.0 229.0 jit_solution(3942660460887260596)
XLA Ops:
  7.8 4.6 %collective-permute-start.2 = (bf16[256,3712]{1,0:T(8,128)(2,1)}, bf16[256,3712]{1,0:T(8,128)(2,1)}, u32[]{:S(2)}, u32[]{:S(2)}) collective-permute-start(bf16[256,3712]{1,0:T(8,128)(2,1)} %pack.1.refs_0_.refs_1_), channel_id=1, source_target_pairs={{0,2},{1,3},{2,0},{3,1},{4,6},{5,7},{6,4},{7,5},{8,10},{9,11},{10,... | collective-permute-start | bytes 5701640 | tf_op jit(solution)/shard_map/ppermute | solution.py:397
  12.6 4.0 %pick.8 = (bf16[80,3584]{1,0:T(8,128)(2,1)S(1)}, bf16[80,3584]{1,0:T(8,128)(2,1)}) custom-call(s32[2,2]{1,0:T(2,128)S(1)} %pad_add_fusion.ids_ref, bf16[256,3712]{1,0:T(8,128)(2,1)} %pack.1.refs_0_.refs_1_, bf16[256,3712]{1,0:T(8,128)(2,1)} %pack.1.refs_0_.refs_1_), custom_call_target="tpu_custom_call" | custom-call | flops 2000000000 | bytes 1000 | tf_op jit(solution)/shard_map/pick/pallas_call | solution.py:123
  19.0 4.3 %pick.9 = (bf16[80,3584]{1,0:T(8,128)(2,1)S(1)}, bf16[80,3584]{1,0:T(8,128)(2,1)}) custom-call(s32[2,2]{1,0:T(2,128)S(1)} %pad_add_fusion.ids_ref, bf16[256,3712]{1,0:T(8,128)(2,1)} %pack.1.refs_0_.refs_1_, bf16[256,3712]{1,0:T(8,128)(2,1)} %pack.1.refs_0_.refs_1_), custom_call_target="tpu_custom_call" | custom-call | flops 2000000000 | bytes 1000 | tf_op jit(solution)/shard_map/pick/pallas_call | solution.py:123
  24.6 9.1 %collective-permute-done.refs_1_ = bf16[80,3584]{1,0:T(8,128)(2,1)} collective-permute-done((bf16[80,3584]{1,0:T(8,128)(2,1)}, bf16[80,3584]{1,0:T(8,128)(2,1)}, u32[]{:S(2)}, u32[]{:S(2)}) %collective-permute-start) | collective-permute-done | bytes 573472 | tf_op jit(solution)/shard_map/ppermute | solution.py:409
  33.7 3.1 %copy-done = bf16[1,3584,1024]{2,1,0:T(8,128)(2,1)S(1)} copy-done((bf16[1,3584,1024]{2,1,0:T(8,128)(2,1)S(1)}, bf16[1,3584,1024]{2,1,0:T(8,128)(2,1)}, u32[]{:S(2)}) %copy-start) | copy-done | bytes 7340056
  36.8 3.1 %copy-done.1 = bf16[1,3584,1024]{2,1,0:T(8,128)(2,1)S(1)} copy-done((bf16[1,3584,1024]{2,1,0:T(8,128)(2,1)S(1)}, bf16[1,3584,1024]{2,1,0:T(8,128)(2,1)}, u32[]{:S(2)}) %copy-start.1) | copy-done | bytes 7340056
  40.9 4.0 %gate_up.4 = (f32[160,1024]{1,0:T(8,128)S(1)}, f32[160,1024]{1,0:T(8,128)S(1)}, bf16[160,1792]{1,0:T(8,128)(2,1)S(1)}, bf16[160,1792]{1,0:T(8,128)(2,1)S(1)}) custom-call(s32[1]{0:T(128)} %bitcast.1.y_ref, bf16[80,3584]{1,0:T(8,128)(2,1)S(1)} %copy-done.36, bf16[80,3584]{1,0:T(8,128)(2,1)} %collective-permute-done.refs_1_, ...), custom_call_target="tpu_custom_call" | custom-call | flops 2000000000 | bytes 1000 | tf_op jit(solution)/shard_map/gate_up/pallas_call | solution.py:170
  45.1 3.9 %back.4 = (bf16[160,2048]{1,0:T(8,128)(2,1)S(1)}, bf16[160,1024]{1,0:T(8,128)(2,1)S(1)}, bf16[160,3584]{1,0:T(8,128)(2,1)S(1)}) custom-call(bf16[80,3584]{1,0:T(8,128)(2,1)S(1)} %copy-done.34, bf16[80,3584]{1,0:T(8,128)(2,1)} %collective-permute-done.4.refs_1_, bf16[1,1024,3584]{2,1,0:T(8,128)(2,1)S(1)} %bitcast.14, ...), custom_call_target="tpu_custom_call" | custom-call | flops 2000000000 | bytes 1000 | tf_op jit(solution)/shard_map/back/pallas_call | solution.py:205
  50.0 3.9 %collective-permute-done.2.refs_0_.refs_1_ = bf16[256,3712]{1,0:T(8,128)(2,1)} collective-permute-done((bf16[256,3712]{1,0:T(8,128)(2,1)}, bf16[256,3712]{1,0:T(8,128)(2,1)}, u32[]{:S(2)}, u32[]{:S(2)}) %collective-permute-start.2) | collective-permute-done | bytes 1900576 | tf_op jit(solution)/shard_map/ppermute | solution.py:397
  62.7 3.1 %pick.11 = (bf16[80,3584]{1,0:T(8,128)(2,1)S(1)}, bf16[80,3584]{1,0:T(8,128)(2,1)S(1)}) custom-call(s32[2,2]{1,0:T(2,128)S(1)} %pad_add_fusion.ids_ref, bf16[256,3712]{1,0:T(8,128)(2,1)} %collective-permute-done.2.refs_0_.refs_1_, bf16[256,3712]{1,0:T(8,128)(2,1)} %collective-permute-done.2.refs_0_.refs_1_), custom_call_target="tpu_custom_call" | custom-call | flops 2000000000 | bytes 1000 | tf_op jit(solution)/shard_map/pick/pallas_call | solution.py:123
  65.8 6.1 %collective-permute-done.1.refs_1_ = bf16[160,1792]{1,0:T(8,128)(2,1)S(1)} collective-permute-done((bf16[160,1792]{1,0:T(8,128)(2,1)S(1)}, bf16[160,1792]{1,0:T(8,128)(2,1)S(1)}, u32[]{:S(2)}, u32[]{:S(2)}) %collective-permute-start.1) | collective-permute-done | bytes 573472 | tf_op jit(solution)/shard_map/ppermute | solution.py:418
  73.5 3.7 %collective-permute-done.5.refs_1_ = bf16[80,3584]{1,0:T(8,128)(2,1)S(1)} collective-permute-done((bf16[80,3584]{1,0:T(8,128)(2,1)S(1)}, bf16[80,3584]{1,0:T(8,128)(2,1)S(1)}, u32[]{:S(2)}, u32[]{:S(2)}) %collective-permute-start.5) | collective-permute-done | bytes 573472 | tf_op jit(solution)/shard_map/ppermute | solution.py:409
  77.1 6.8 %collective-permute-done.10.refs_9_ = bf16[160,2048]{1,0:T(8,128)(2,1)S(1)} collective-permute-done((bf16[160,2048]{1,0:T(8,128)(2,1)S(1)}, bf16[160,2048]{1,0:T(8,128)(2,1)S(1)}, u32[]{:S(2)}, u32[]{:S(2)}) %collective-permute-start.10) | collective-permute-done | bytes 655392 | tf_op jit(solution)/shard_map/ppermute | solution.py:418
  84.0 3.1 %collective-permute-done.9.refs_1_ = bf16[80,3584]{1,0:T(8,128)(2,1)S(1)} collective-permute-done((bf16[80,3584]{1,0:T(8,128)(2,1)S(1)}, bf16[80,3584]{1,0:T(8,128)(2,1)S(1)}, u32[]{:S(2)}, u32[]{:S(2)}) %collective-permute-start.9) | collective-permute-done | bytes 573472 | tf_op jit(solution)/shard_map/ppermute | solution.py:409
  95.5 3.9 %collective-permute-done.7.refs_0_.refs_2_ = bf16[256,3712]{1,0:T(8,128)(2,1)S(1)} collective-permute-done((bf16[256,3712]{1,0:T(8,128)(2,1)}, bf16[256,3712]{1,0:T(8,128)(2,1)S(1)}, u32[]{:S(2)}, u32[]{:S(2)}) %collective-permute-start.7) | collective-permute-done | bytes 1900576 | tf_op jit(solution)/shard_map/ppermute | solution.py:400
  110.2 7.6 %collective-permute-done.11.refs_1_ = bf16[80,3584]{1,0:T(8,128)(2,1)S(1)} collective-permute-done((bf16[80,3584]{1,0:T(8,128)(2,1)S(1)}, bf16[80,3584]{1,0:T(8,128)(2,1)S(1)}, u32[]{:S(2)}, u32[]{:S(2)}) %collective-permute-start.11) | collective-permute-done | bytes 573472 | tf_op jit(solution)/shard_map/ppermute | solution.py:409
  117.8 3.4 %gate_up.6 = (f32[160,1024]{1,0:T(8,128)S(1)}, f32[160,1024]{1,0:T(8,128)S(1)}, bf16[160,1792]{1,0:T(8,128)(2,1)S(1)}, bf16[160,1792]{1,0:T(8,128)(2,1)}) custom-call(s32[1]{0:T(128)} %bitcast.1.y_ref, bf16[80,3584]{1,0:T(8,128)(2,1)S(1)} %get-tuple-element.105.refs_0_, bf16[80,3584]{1,0:T(8,128)(2,1)S(1)} %collective-permute-done.11.refs_1_, ...), custom_call_target="tpu_custom_call" | custom-call | flops 2000000000 | bytes 1000 | tf_op jit(solution)/shard_map/gate_up/pallas_call | solution.py:170
  123.0 3.1 %pick.14 = (bf16[80,3584]{1,0:T(8,128)(2,1)S(1)}, bf16[80,3584]{1,0:T(8,128)(2,1)S(1)}) custom-call(s32[2,2]{1,0:T(2,128)S(1)} %pad_add_fusion.ids_ref, bf16[256,3712]{1,0:T(8,128)(2,1)} %collective-permute-done.3.refs_0_.refs_2_, bf16[128,3712]{1,0:T(8,128)(2,1)S(1)} %collective-permute-done.13.refs_1_.refs_3_, ...), custom_call_target="tpu_custom_call" | custom-call | flops 2000000000 | bytes 1000 | tf_op jit(solution)/shard_map/pick/pallas_call | solution.py:123
  130.1 3.6 %back.6 = (bf16[160,2048]{1,0:T(8,128)(2,1)}, bf16[160,1024]{1,0:T(8,128)(2,1)S(1)}, bf16[160,3584]{1,0:T(8,128)(2,1)S(1)}) custom-call(bf16[80,3584]{1,0:T(8,128)(2,1)S(1)} %get-tuple-element.109.refs_0_, bf16[80,3584]{1,0:T(8,128)(2,1)S(1)} %collective-permute-done.16.refs_1_, bf16[1,1024,3584]{2,1,0:T(8,128)(2,1)S(1)} %bitcast.14, ...), custom_call_target="tpu_custom_call" | custom-call | flops 2000000000 | bytes 1000 | tf_op jit(solution)/shard_map/back/pallas_call | solution.py:205
  135.2 4.5 %collective-permute-done.15.refs_3_ = bf16[128,3584]{1,0:T(8,128)(2,1)S(1)} collective-permute-done((bf16[128,3584]{1,0:T(8,128)(2,1)S(1)}, bf16[128,3584]{1,0:T(8,128)(2,1)S(1)}, u32[]{:S(2)}, u32[]{:S(2)}) %collective-permute-start.15) | collective-permute-done | bytes 917536 | tf_op jit(solution)/shard_map/ppermute | solution.py:403
  139.6 4.2 %pick.15 = (bf16[80,3584]{1,0:T(8,128)(2,1)S(1)}, bf16[80,3584]{1,0:T(8,128)(2,1)}) custom-call(s32[2,2]{1,0:T(2,128)S(1)} %pad_add_fusion.ids_ref, bf16[256,3712]{1,0:T(8,128)(2,1)} %collective-permute-done.3.refs_0_.refs_2_, bf16[128,3712]{1,0:T(8,128)(2,1)S(1)} %collective-permute-done.13.refs_1_.refs_3_, ...), custom_call_target="tpu_custom_call" | custom-call | flops 2000000000 | bytes 1000 | tf_op jit(solution)/shard_map/pick/pallas_call | solution.py:123
  146.1 3.3 %gate_up.7 = (f32[160,1024]{1,0:T(8,128)S(1)}, f32[160,1024]{1,0:T(8,128)S(1)}, bf16[160,1792]{1,0:T(8,128)(2,1)S(1)}, bf16[160,1792]{1,0:T(8,128)(2,1)}) custom-call(s32[1]{0:T(128)} %bitcast.1.y_ref, bf16[80,3584]{1,0:T(8,128)(2,1)S(1)} %get-tuple-element.116.refs_0_, bf16[80,3584]{1,0:T(8,128)(2,1)S(1)} %collective-permute-done.14.refs_1_, ...), custom_call_target="tpu_custom_call" | custom-call | flops 2000000000 | bytes 1000 | tf_op jit(solution)/shard_map/gate_up/pallas_call | solution.py:170
  151.0 6.0 %collective-permute-done.19.refs_1_ = bf16[80,3584]{1,0:T(8,128)(2,1)} collective-permute-done((bf16[80,3584]{1,0:T(8,128)(2,1)}, bf16[80,3584]{1,0:T(8,128)(2,1)}, u32[]{:S(2)}, u32[]{:S(2)}) %collective-permute-start.19) | collective-permute-done | bytes 573472 | tf_op jit(solution)/shard_map/ppermute | solution.py:409
  157.0 3.1 %copy-done.2 = bf16[1,1024,3584]{2,1,0:T(8,128)(2,1)S(1)} copy-done((bf16[1,1024,3584]{2,1,0:T(8,128)(2,1)S(1)}, bf16[1,1024,3584]{2,1,0:T(8,128)(2,1)}, u32[]{:S(2)}) %copy-start.2) | copy-done | bytes 7340056
  161.2 3.8 %back.7 = (bf16[160,2048]{1,0:T(8,128)(2,1)S(1)}, bf16[160,1024]{1,0:T(8,128)(2,1)S(1)}, bf16[160,3584]{1,0:T(8,128)(2,1)S(1)}) custom-call(bf16[80,3584]{1,0:T(8,128)(2,1)S(1)} %copy-done.32, bf16[80,3584]{1,0:T(8,128)(2,1)} %collective-permute-done.19.refs_1_, bf16[1,1024,3584]{2,1,0:T(8,128)(2,1)S(1)} %copy-done.2, ...), custom_call_target="tpu_custom_call" | custom-call | flops 2000000000 | bytes 1000 | tf_op jit(solution)/shard_map/back/pallas_call | solution.py:205
  165.0 5.6 %down_sends.1 = (bf16[256,3584]{1,0:T(8,128)(2,1)S(1)}, bf16[256,3584]{1,0:T(8,128)(2,1)S(1)}) custom-call(s32[2]{0:T(128)S(1)} %pad_add_fusion.1.s_ref, bf16[160,1024]{1,0:T(8,128)(2,1)S(1)} %get-tuple-element.135.refs_0_.refs_4_, bf16[160,1024]{1,0:T(8,128)(2,1)S(1)} %copy-done.28, bf16[160,1024]{1,0:T(8,128)(2,1)S(1)} %copy-done.30, ...), custom_call_target="tpu_custom_call" | custom-call | flops 2000000000 | bytes 1000 | tf_op jit(solution)/shard_map/down_sends/pallas_call | solution.py:236
  177.1 4.0 %down_part.2 = bf16[256,3584]{1,0:T(8,128)(2,1)S(1)} custom-call(s32[1]{0:T(128)S(6)} %add.51.s_ref, bf16[160,1024]{1,0:T(8,128)(2,1)S(1)} %get-tuple-element.135.refs_0_.refs_4_, bf16[160,1024]{1,0:T(8,128)(2,1)S(1)} %copy-done.28, bf16[160,1024]{1,0:T(8,128)(2,1)S(1)} %copy-done.30, bf16[160,1024]{1,0:T(8,128)(2,1)S(1)} %get-tuple-element.138.refs_3_.refs_7_, ...), custom_call_target="tpu_custom_call" | custom-call | flops 2000000000 | bytes 1000 | tf_op jit(solution)/shard_map/down_part/pallas_call | solution.py:295
  182.7 6.2 %collective-permute-done.23.refs_15_ = bf16[160,2048]{1,0:T(8,128)(2,1)S(1)} collective-permute-done((bf16[160,2048]{1,0:T(8,128)(2,1)S(1)}, bf16[160,2048]{1,0:T(8,128)(2,1)S(1)}, u32[]{:S(2)}, u32[]{:S(2)}) %collective-permute-start.23) | collective-permute-done | bytes 655392 | tf_op jit(solution)/shard_map/ppermute | solution.py:418
  189.0 8.0 %both_part.2 = (bf16[896,512]{1,0:T(8,128)(2,1)S(1)}, bf16[896,512]{1,0:T(8,128)(2,1)S(1)}, bf16[896,512]{1,0:T(8,128)(2,1)S(1)}, bf16[896,512]{1,0:T(8,128)(2,1)S(1)}) custom-call(s32[1]{0:T(128)S(6)} %sub.14.c_ref, bf16[160,1792]{1,0:T(8,128)(2,1)S(1)} %copy-done.18, bf16[160,1792]{1,0:T(8,128)(2,1)S(1)} %copy-done.20, bf16[160,1792]{1,0:T(8,128)(2,1)S(1)} %copy-done.22, ...), custom_call_target="tpu_custom_call" | custom-call | flops 2000000000 | bytes 1000 | tf_op jit(solution)/shard_map/both_part/pallas_call | solution.py:354
  198.1 4.0 %down_part.3 = f32[256,3584]{1,0:T(8,128)S(1)} custom-call(s32[1]{0:T(128)S(6)} %add.54.s_ref, bf16[160,1024]{1,0:T(8,128)(2,1)S(1)} %get-tuple-element.135.refs_0_.refs_4_, bf16[160,1024]{1,0:T(8,128)(2,1)S(1)} %copy-done.28, bf16[160,1024]{1,0:T(8,128)(2,1)S(1)} %copy-done.30, bf16[160,1024]{1,0:T(8,128)(2,1)S(1)} %get-tuple-element.138.refs_3_.refs_7_, ...), custom_call_target="tpu_custom_call" | custom-call | flops 2000000000 | bytes 1000 | tf_op jit(solution)/shard_map/down_part/pallas_call | solution.py:295
  203.5 10.0 %both_part.3 = (bf16[896,1024]{1,0:T(8,128)(2,1)}, bf16[896,1024]{1,0:T(8,128)(2,1)}) custom-call(s32[1]{0:T(128)} %bitcast.c_ref, bf16[160,1792]{1,0:T(8,128)(2,1)S(1)} %copy-done.18, bf16[160,1792]{1,0:T(8,128)(2,1)S(1)} %copy-done.20, bf16[160,1792]{1,0:T(8,128)(2,1)S(1)} %copy-done.22, bf16[160,1792]{1,0:T(8,128)(2,1)S(1)} %copy-done.24, ...), custom_call_target="tpu_custom_call" | custom-call | flops 2000000000 | bytes 1000 | tf_op jit(solution)/shard_map/both_part/pallas_call | solution.py:354
  213.5 13.9 %collective-permute-done.28 = bf16[256,3584]{1,0:T(8,128)(2,1)S(1)} collective-permute-done((bf16[256,3584]{1,0:T(8,128)(2,1)S(1)}, bf16[256,3584]{1,0:T(8,128)(2,1)S(1)}, u32[]{:S(2)}, u32[]{:S(2)}) %collective-permute-start.28) | collective-permute-done | bytes 1835040 | tf_op jit(solution)/shard_map/ppermute | solution.py:418
  (155 shorter events, 66.8 us)
Async XLA Ops:
  5.9 44.1 %collective-permute-start.3 = (bf16[256,3712]{1,0:T(8,128)(2,1)}, bf16[256,3712]{1,0:T(8,128)(2,1)}, u32[]{:S(2)}, u32[]{:S(2)}) collective-permute-start(bf16[256,3712]{1,0:T(8,128)(2,1)} %pack.1.refs_0_.refs_1_), channel_id=1, source_target_pairs={{2,4},{3,5},{4,2},{5,3},{10,12},{11,13},{12,10},{13,11},{18,20},{1... | collective-permute-start | bytes 5701640 | tf_op jit(solution)/shard_map/ppermute | solution.py:397
  7.8 46.1 %collective-permute-start.2 = (bf16[256,3712]{1,0:T(8,128)(2,1)}, bf16[256,3712]{1,0:T(8,128)(2,1)}, u32[]{:S(2)}, u32[]{:S(2)}) collective-permute-start(bf16[256,3712]{1,0:T(8,128)(2,1)} %pack.1.refs_0_.refs_1_), channel_id=1, source_target_pairs={{0,2},{1,3},{2,0},{3,1},{4,6},{5,7},{6,4},{7,5},{8,10},{9,11},{10,... | collective-permute-start | bytes 5701640 | tf_op jit(solution)/shard_map/ppermute | solution.py:397
  17.5 16.2 %collective-permute-start = (bf16[80,3584]{1,0:T(8,128)(2,1)}, bf16[80,3584]{1,0:T(8,128)(2,1)}, u32[]{:S(2)}, u32[]{:S(2)}) collective-permute-start(bf16[80,3584]{1,0:T(8,128)(2,1)} %get-tuple-element.80), channel_id=1, source_target_pairs={{0,1},{1,0},{2,3},{3,2},{4,5},{5,4},{6,7},{7,6},{8,9},{9,8},{10,11... | collective-permute-start | bytes 1720328 | tf_op jit(solution)/shard_map/ppermute | solution.py:409
  24.1 20.9 %collective-permute-start.4 = (bf16[80,3584]{1,0:T(8,128)(2,1)}, bf16[80,3584]{1,0:T(8,128)(2,1)}, u32[]{:S(2)}, u32[]{:S(2)}) collective-permute-start(bf16[80,3584]{1,0:T(8,128)(2,1)} %get-tuple-element.85), channel_id=1, source_target_pairs={{0,1},{1,0},{2,3},{3,2},{4,5},{5,4},{6,7},{7,6},{8,9},{9,8},{10,11... | collective-permute-start | bytes 1720328 | tf_op jit(solution)/shard_map/ppermute | solution.py:409
  45.0 42.0 %slice-start = ((s8[7340032]{0:T(1024)(128)(4,1)}), s8[4194304]{0:T(1024)(128)(4,1)S(1)}, s32[]{:S(2)}) async-start(s8[7340032]{0:T(1024)(128)(4,1)} %bitcast.9), calls=%async_computation | async-start | bytes 8388608
  45.0 42.0 %slice-start.2 = ((s8[7340032]{0:T(1024)(128)(4,1)}), s8[4194304]{0:T(1024)(128)(4,1)S(1)}, s32[]{:S(2)}) async-start(s8[7340032]{0:T(1024)(128)(4,1)} %bitcast.11), calls=%async_computation.2 | async-start | bytes 8388608
  53.9 37.6 %collective-permute-start.8 = (bf16[256,3712]{1,0:T(8,128)(2,1)}, bf16[256,3712]{1,0:T(8,128)(2,1)S(1)}, u32[]{:S(2)}, u32[]{:S(2)}) collective-permute-start(bf16[256,3712]{1,0:T(8,128)(2,1)} %collective-permute-done.2.refs_0_.refs_1_), channel_id=1, source_target_pairs={{2,4},{3,5},{4,2},{5,3},{10,12},{11,13},{12,10},{13,11},{18,20},{1... | collective-permute-start | bytes 5701640 | tf_op jit(solution)/shard_map/ppermute | solution.py:400
  54.7 44.8 %collective-permute-start.7 = (bf16[256,3712]{1,0:T(8,128)(2,1)}, bf16[256,3712]{1,0:T(8,128)(2,1)S(1)}, u32[]{:S(2)}, u32[]{:S(2)}) collective-permute-start(bf16[256,3712]{1,0:T(8,128)(2,1)} %collective-permute-done.3.refs_0_.refs_2_), channel_id=1, source_target_pairs={{2,0},{3,1},{4,6},{5,7},{10,8},{11,9},{12,14},{13,15},{18,16},{19,... | collective-permute-start | bytes 5701640 | tf_op jit(solution)/shard_map/ppermute | solution.py:400
  56.0 31.1 %slice-start.1 = ((s8[7340032]{0:T(1024)(128)(4,1)}), s8[3145728]{0:T(1024)(128)(4,1)S(1)}, s32[]{:S(2)}) async-start(s8[7340032]{0:T(1024)(128)(4,1)} %bitcast.9), calls=%async_computation.1 | async-start | bytes 6291456
  56.0 16.0 %collective-permute-start.1 = (bf16[160,1792]{1,0:T(8,128)(2,1)S(1)}, bf16[160,1792]{1,0:T(8,128)(2,1)S(1)}, u32[]{:S(2)}, u32[]{:S(2)}) collective-permute-start(bf16[160,1792]{1,0:T(8,128)(2,1)S(1)} %get-tuple-element.82), channel_id=1, source_target_pairs={{0,16},{8,24},{16,0},{24,8},{1,17},{9,25},{17,1},{25,9},{2,18},{10... | collective-permute-start | bytes 1720328 | tf_op jit(solution)/shard_map/ppermute | solution.py:418
  57.6 26.4 %collective-permute-start.10 = (bf16[160,2048]{1,0:T(8,128)(2,1)S(1)}, bf16[160,2048]{1,0:T(8,128)(2,1)S(1)}, u32[]{:S(2)}, u32[]{:S(2)}) collective-permute-start(bf16[160,2048]{1,0:T(8,128)(2,1)S(1)} %get-tuple-element.146.refs_8_), channel_id=1, source_target_pairs={{0,16},{8,24},{16,0},{24,8},{1,17},{9,25},{17,1},{25,9},{2,18},{10... | collective-permute-start | bytes 1966088 | tf_op jit(solution)/shard_map/ppermute | solution.py:418
  61.1 16.0 %collective-permute-start.5 = (bf16[80,3584]{1,0:T(8,128)(2,1)S(1)}, bf16[80,3584]{1,0:T(8,128)(2,1)S(1)}, u32[]{:S(2)}, u32[]{:S(2)}) collective-permute-start(bf16[80,3584]{1,0:T(8,128)(2,1)S(1)} %get-tuple-element.91), channel_id=1, source_target_pairs={{0,1},{1,0},{2,3},{3,2},{4,5},{5,4},{6,7},{7,6},{8,9},{9,8},{10,11... | collective-permute-start | bytes 1720328 | tf_op jit(solution)/shard_map/ppermute | solution.py:409
  72.0 15.1 %collective-permute-start.9 = (bf16[80,3584]{1,0:T(8,128)(2,1)S(1)}, bf16[80,3584]{1,0:T(8,128)(2,1)S(1)}, u32[]{:S(2)}, u32[]{:S(2)}) collective-permute-start(bf16[80,3584]{1,0:T(8,128)(2,1)S(1)} %get-tuple-element.98), channel_id=1, source_target_pairs={{0,1},{1,0},{2,3},{3,2},{4,5},{5,4},{6,7},{7,6},{8,9},{9,8},{10,11... | collective-permute-start | bytes 1720328 | tf_op jit(solution)/shard_map/ppermute | solution.py:409
  89.9 19.0 %collective-permute-start.6 = (bf16[160,1792]{1,0:T(8,128)(2,1)S(1)}, bf16[160,1792]{1,0:T(8,128)(2,1)S(1)}, u32[]{:S(2)}, u32[]{:S(2)}) collective-permute-start(bf16[160,1792]{1,0:T(8,128)(2,1)S(1)} %get-tuple-element.96), channel_id=1, source_target_pairs={{0,16},{8,24},{16,0},{24,8},{1,17},{9,25},{17,1},{25,9},{2,18},{10... | collective-permute-start | bytes 1720328 | tf_op jit(solution)/shard_map/ppermute | solution.py:418
  91.6 31.4 %collective-permute-start.13 = (bf16[128,3712]{1,0:T(8,128)(2,1)S(1)}, bf16[128,3712]{1,0:T(8,128)(2,1)S(1)}, u32[]{:S(2)}, u32[]{:S(2)}) collective-permute-start(bf16[128,3712]{1,0:T(8,128)(2,1)S(1)} %slice.8), channel_id=1, source_target_pairs={{2,0},{3,1},{4,6},{5,7},{10,8},{11,9},{12,14},{13,15},{18,16},{19,... | collective-permute-start | bytes 2850824 | tf_op jit(solution)/shard_map/ppermute | solution.py:403
  101.8 16.0 %collective-permute-start.11 = (bf16[80,3584]{1,0:T(8,128)(2,1)S(1)}, bf16[80,3584]{1,0:T(8,128)(2,1)S(1)}, u32[]{:S(2)}, u32[]{:S(2)}) collective-permute-start(bf16[80,3584]{1,0:T(8,128)(2,1)S(1)} %get-tuple-element.106), channel_id=1, source_target_pairs={{0,1},{1,0},{2,3},{3,2},{4,5},{5,4},{6,7},{7,6},{8,9},{9,8},{10,11... | collective-permute-start | bytes 1720328 | tf_op jit(solution)/shard_map/ppermute | solution.py:409
  103.4 25.9 %collective-permute-start.17 = (bf16[160,2048]{1,0:T(8,128)(2,1)S(1)}, bf16[160,2048]{1,0:T(8,128)(2,1)S(1)}, u32[]{:S(2)}, u32[]{:S(2)}) collective-permute-start(bf16[160,2048]{1,0:T(8,128)(2,1)S(1)} %get-tuple-element.102.refs_10_), channel_id=1, source_target_pairs={{0,16},{8,24},{16,0},{24,8},{1,17},{9,25},{17,1},{25,9},{2,18},{10... | collective-permute-start | bytes 1966088 | tf_op jit(solution)/shard_map/ppermute | solution.py:418
  104.9 34.7 %collective-permute-start.15 = (bf16[128,3584]{1,0:T(8,128)(2,1)S(1)}, bf16[128,3584]{1,0:T(8,128)(2,1)S(1)}, u32[]{:S(2)}, u32[]{:S(2)}) collective-permute-start(bf16[128,3584]{1,0:T(8,128)(2,1)S(1)} %slice.9), channel_id=1, source_target_pairs={{2,0},{3,1},{4,6},{5,7},{10,8},{11,9},{12,14},{13,15},{18,16},{19,... | collective-permute-start | bytes 2752520 | tf_op jit(solution)/shard_map/ppermute | solution.py:403
  109.7 20.4 %collective-permute-start.16 = (bf16[80,3584]{1,0:T(8,128)(2,1)S(1)}, bf16[80,3584]{1,0:T(8,128)(2,1)S(1)}, u32[]{:S(2)}, u32[]{:S(2)}) collective-permute-start(bf16[80,3584]{1,0:T(8,128)(2,1)S(1)} %get-tuple-element.118), channel_id=1, source_target_pairs={{0,1},{1,0},{2,3},{3,2},{4,5},{5,4},{6,7},{7,6},{8,9},{9,8},{10,11... | collective-permute-start | bytes 1720328 | tf_op jit(solution)/shard_map/ppermute | solution.py:409
  126.1 20.0 %collective-permute-start.14 = (bf16[80,3584]{1,0:T(8,128)(2,1)S(1)}, bf16[80,3584]{1,0:T(8,128)(2,1)S(1)}, u32[]{:S(2)}, u32[]{:S(2)}) collective-permute-start(bf16[80,3584]{1,0:T(8,128)(2,1)S(1)} %get-tuple-element.117), channel_id=1, source_target_pairs={{0,1},{1,0},{2,3},{3,2},{4,5},{5,4},{6,7},{7,6},{8,9},{9,8},{10,11... | collective-permute-start | bytes 1720328 | tf_op jit(solution)/shard_map/ppermute | solution.py:409
  127.7 23.3 %collective-permute-start.12 = (bf16[160,1792]{1,0:T(8,128)(2,1)}, bf16[160,1792]{1,0:T(8,128)(2,1)}, u32[]{:S(2)}, u32[]{:S(2)}) collective-permute-start(bf16[160,1792]{1,0:T(8,128)(2,1)} %get-tuple-element.112), channel_id=1, source_target_pairs={{0,16},{8,24},{16,0},{24,8},{1,17},{9,25},{17,1},{25,9},{2,18},{10... | collective-permute-start | bytes 1720328 | tf_op jit(solution)/shard_map/ppermute | solution.py:418
  133.6 23.4 %collective-permute-start.20 = (bf16[160,2048]{1,0:T(8,128)(2,1)}, bf16[160,2048]{1,0:T(8,128)(2,1)S(1)}, u32[]{:S(2)}, u32[]{:S(2)}) collective-permute-start(bf16[160,2048]{1,0:T(8,128)(2,1)} %get-tuple-element.121.refs_12_), channel_id=1, source_target_pairs={{0,16},{8,24},{16,0},{24,8},{1,17},{9,25},{17,1},{25,9},{2,18},{10... | collective-permute-start | bytes 1966088 | tf_op jit(solution)/shard_map/ppermute | solution.py:418
  144.6 12.4 %collective-permute-start.19 = (bf16[80,3584]{1,0:T(8,128)(2,1)}, bf16[80,3584]{1,0:T(8,128)(2,1)}, u32[]{:S(2)}, u32[]{:S(2)}) collective-permute-start(bf16[80,3584]{1,0:T(8,128)(2,1)} %get-tuple-element.130), channel_id=1, source_target_pairs={{0,1},{1,0},{2,3},{3,2},{4,5},{5,4},{6,7},{7,6},{8,9},{9,8},{10,11... | collective-permute-start | bytes 1720328 | tf_op jit(solution)/shard_map/ppermute | solution.py:409
  149.4 15.6 %collective-permute-start.18 = (bf16[160,1792]{1,0:T(8,128)(2,1)}, bf16[160,1792]{1,0:T(8,128)(2,1)S(1)}, u32[]{:S(2)}, u32[]{:S(2)}) collective-permute-start(bf16[160,1792]{1,0:T(8,128)(2,1)} %get-tuple-element.126), channel_id=1, source_target_pairs={{0,16},{8,24},{16,0},{24,8},{1,17},{9,25},{17,1},{25,9},{2,18},{10... | collective-permute-start | bytes 1720328 | tf_op jit(solution)/shard_map/ppermute | solution.py:418
  170.6 3.9 %collective-permute-start.21 = (bf16[256,3584]{1,0:T(8,128)(2,1)S(1)}, bf16[256,3584]{1,0:T(8,128)(2,1)S(1)}, u32[]{:S(2)}, u32[]{:S(2)}) collective-permute-start(bf16[256,3584]{1,0:T(8,128)(2,1)S(1)} %get-tuple-element.143), channel_id=1, source_target_pairs={{0,8},{8,0},{16,24},{24,16},{1,9},{9,1},{17,25},{25,17},{2,10},{10... | collective-permute-start | bytes 5505032 | tf_op jit(solution)/shard_map/ppermute | solution.py:415
  170.7 6.4 %collective-permute-start.22 = (bf16[256,3584]{1,0:T(8,128)(2,1)S(1)}, bf16[256,3584]{1,0:T(8,128)(2,1)S(1)}, u32[]{:S(2)}, u32[]{:S(2)}) collective-permute-start(bf16[256,3584]{1,0:T(8,128)(2,1)S(1)} %get-tuple-element.144), channel_id=1, source_target_pairs={{0,8},{8,0},{16,24},{24,16},{1,9},{9,1},{17,25},{25,17},{2,10},{10... | collective-permute-start | bytes 5505032 | tf_op jit(solution)/shard_map/ppermute | solution.py:415
  171.3 17.7 %collective-permute-start.23 = (bf16[160,2048]{1,0:T(8,128)(2,1)S(1)}, bf16[160,2048]{1,0:T(8,128)(2,1)S(1)}, u32[]{:S(2)}, u32[]{:S(2)}) collective-permute-start(bf16[160,2048]{1,0:T(8,128)(2,1)S(1)} %get-tuple-element.147.refs_14_), channel_id=1, source_target_pairs={{0,16},{8,24},{16,0},{24,8},{1,17},{9,25},{17,1},{25,9},{2,18},{10... | collective-permute-start | bytes 1966088 | tf_op jit(solution)/shard_map/ppermute | solution.py:418
  181.1 46.2 %collective-permute-start.28 = (bf16[256,3584]{1,0:T(8,128)(2,1)S(1)}, bf16[256,3584]{1,0:T(8,128)(2,1)S(1)}, u32[]{:S(2)}, u32[]{:S(2)}) collective-permute-start(bf16[256,3584]{1,0:T(8,128)(2,1)S(1)} %down_part.2), channel_id=1, source_target_pairs={{0,16},{8,24},{16,0},{24,8},{1,17},{9,25},{17,1},{25,9},{2,18},{10... | collective-permute-start | bytes 5505032 | tf_op jit(solution)/shard_map/ppermute | solution.py:418
  197.0 5.1 %collective-permute-start.24 = (bf16[896,512]{1,0:T(8,128)(2,1)S(1)}, bf16[896,512]{1,0:T(8,128)(2,1)S(1)}, u32[]{:S(2)}, u32[]{:S(2)}) collective-permute-start(bf16[896,512]{1,0:T(8,128)(2,1)S(1)} %get-tuple-element.148), channel_id=1, source_target_pairs={{0,8},{8,0},{16,24},{24,16},{1,9},{9,1},{17,25},{25,17},{2,10},{10... | collective-permute-start | bytes 2752520 | tf_op jit(solution)/shard_map/ppermute | solution.py:415
  197.1 5.1 %collective-permute-start.25 = (bf16[896,512]{1,0:T(8,128)(2,1)S(1)}, bf16[896,512]{1,0:T(8,128)(2,1)S(1)}, u32[]{:S(2)}, u32[]{:S(2)}) collective-permute-start(bf16[896,512]{1,0:T(8,128)(2,1)S(1)} %get-tuple-element.149), channel_id=1, source_target_pairs={{0,8},{8,0},{16,24},{24,16},{1,9},{9,1},{17,25},{25,17},{2,10},{10... | collective-permute-start | bytes 2752520 | tf_op jit(solution)/shard_map/ppermute | solution.py:415
  197.6 4.6 %collective-permute-start.26 = (bf16[896,512]{1,0:T(8,128)(2,1)S(1)}, bf16[896,512]{1,0:T(8,128)(2,1)S(1)}, u32[]{:S(2)}, u32[]{:S(2)}) collective-permute-start(bf16[896,512]{1,0:T(8,128)(2,1)S(1)} %get-tuple-element.150), channel_id=1, source_target_pairs={{0,8},{8,0},{16,24},{24,16},{1,9},{9,1},{17,25},{25,17},{2,10},{10... | collective-permute-start | bytes 2752520 | tf_op jit(solution)/shard_map/ppermute | solution.py:415
  197.7 5.8 %collective-permute-start.27 = (bf16[896,512]{1,0:T(8,128)(2,1)S(1)}, bf16[896,512]{1,0:T(8,128)(2,1)S(1)}, u32[]{:S(2)}, u32[]{:S(2)}) collective-permute-start(bf16[896,512]{1,0:T(8,128)(2,1)S(1)} %get-tuple-element.151), channel_id=1, source_target_pairs={{0,8},{8,0},{16,24},{24,16},{1,9},{9,1},{17,25},{25,17},{2,10},{10... | collective-permute-start | bytes 2752520 | tf_op jit(solution)/shard_map/ppermute | solution.py:415
  (45 other events, 366.4 us)
